TPU v7x, 512 devices: a whole 4x8x8 slice. The times are simulated.
512 devices in a mesh: row: 16 (over x_hi, z), col: 32 (over y, x_lo, core).
Axes of the slice: x: 4 (x_hi: 2, x_lo: 2; x = x_hi * 2 + x_lo), y: 8, z: 8, core: 2. Of those that a mesh axis runs over, the one named last changes fastest.
Arguments:
- h_blocks: bfloat16 [16, 32, 8, 128, 128], P('row', 'col'), as said below
- h_index: int32 [16, 32, 2, 8], P('row', 'col'), may hold values from 0 to 3, as said below
- z_blocks: bfloat16 [16, 32, 8, 128, 128], P('row', 'col'), as said below
- z_index: int32 [16, 32, 2, 8], P('row', 'col'), may hold values from 0 to 3, as said below
- keep_index: int32 [16, 32, 2, 8], P('row', 'col'), may hold values from 0 to 3, as said below
Outputs:
- filtered: float32 [16, 32, 4, 128, 128], P('row', 'col')
Inputs may be any that keep to these rules, and one draw needn't show every extreme that they name: `h_blocks`: grid positions whose lists name the same H tile hold equal blocks. `z_blocks`: grid positions whose lists name the same Z tile hold equal blocks. `h_index`: each list holds 8 distinct block positions; grid positions that name the same H tile hold equal lists. `z_index`: each list holds 8 distinct block positions; grid positions that name the same Z tile hold equal lists. `keep_index`: each list holds 8 distinct block positions; the 2 grid positions with equal i and c hold equal lists.
All inputs are finite; a program needn't handle non-finite values.
Results may differ from a plain program's by a relative error of at most 0.0003.
Values may be sent and summed in bfloat16 or wider, within the bound.
No kernel may reach another device: no remote copies, remote signals or barrier semaphores. Data moves between devices by JAX's collectives and lax.ppermute only.
A program may use at most 64 MiB of HBM per device.

v0:
```python
import jax
import jax.numpy as jnp
from jax import lax
from jax.sharding import PartitionSpec as P

TILE = 4


def from_behind(block, axis, distance):
    devices = range(lax.axis_size(axis))
    route = [((i - distance) % len(devices), i) for i in devices]
    return lax.ppermute(block, axis, route)


def from_partner(shard, axis, stride):
    return lax.ppermute(shard, axis, [(i, i ^ 1 << stride) for i in range(lax.axis_size(axis))])


def densify(blocks, places):
    count = blocks.shape[0]
    width = blocks.shape[1]
    slots = places[0] * TILE + places[1]
    selector = (jnp.arange(TILE * TILE, dtype=jnp.int32)[:, None] == slots[None, :]).astype(
        blocks.dtype
    )
    flat = jnp.dot(
        selector, blocks.reshape(count, width * width), preferred_element_type=jnp.float32
    )
    flat = flat.astype(blocks.dtype)
    return (
        flat.reshape(TILE, TILE, width, width)
        .transpose(0, 2, 1, 3)
        .reshape(TILE * width, TILE * width)
    )


def pick_blocks(dense, kept_pos):
    width = dense.shape[0] // TILE
    tiles = (
        dense.reshape(TILE, width, TILE, width)
        .transpose(0, 2, 1, 3)
        .reshape(TILE * TILE, width * width)
    )
    slots = kept_pos[0] * TILE + kept_pos[1]
    selector = (slots[:, None] == jnp.arange(TILE * TILE, dtype=jnp.int32)[None, :]).astype(
        jnp.float32
    )
    picked = jnp.dot(
        selector, tiles, precision=lax.Precision.HIGHEST, preferred_element_type=jnp.float32
    )
    return picked.reshape(kept_pos.shape[1], width, width)


def accumulate(running, h_list, h_pos, z_list, z_pos):
    h_dense = densify(h_list, h_pos)
    z_dense = densify(z_list, z_pos)
    return running + jnp.dot(h_dense, z_dense, preferred_element_type=jnp.float32)


def per_device(h_blocks, h_index, z_blocks, z_index, keep_index):
    grid_size = lax.axis_size("row")
    layers = lax.axis_size("col") // grid_size
    step_count = grid_size // layers
    kept_pos = keep_index[0, 0]
    width = h_blocks.shape[3]
    running = jnp.zeros((TILE * width, TILE * width), jnp.float32)
    h_list = h_blocks[0, 0]
    h_pos = h_index[0, 0]
    z_list = z_blocks[0, 0]
    z_pos = z_index[0, 0]
    for turn_index in range(step_count):
        running = accumulate(running, h_list, h_pos, z_list, z_pos)
        if turn_index + 1 < step_count:
            h_list, h_pos = from_behind((h_list, h_pos), "col", -layers)
            z_list, z_pos = from_behind((z_list, z_pos), "row", -1)
    picked = pick_blocks(running, kept_pos)
    half_count = picked.shape[0] // layers
    layer_bit = lax.axis_index("col") % layers
    partner = from_partner(picked, "col", 0)
    combined = picked + partner
    own_part = lax.dynamic_slice_in_dim(combined, layer_bit * half_count, half_count, 0)
    return own_part[None, None]


def solution(mesh):
    return jax.shard_map(
        per_device,
        mesh=mesh,
        in_specs=(
            P("row", "col", None, None, None),
            P("row", "col", None, None),
            P("row", "col", None, None, None),
            P("row", "col", None, None),
            P("row", "col", None, None),
        ),
        out_specs=P("row", "col", None, None, None),
        check_vma=False,
    )
```

profile of v0, /device:TPU:1, one launch (start us, length us, event | category | flops | bytes accessed | tf_op | source)
XLA Modules:
  0.0 196.7 jit_solution(9165205961640019885)
XLA Ops:
  0.0 14.1 %collective-permute-start.3 = (bf16[8,128,128]{2,1,0:T(8,128)(2,1)}, bf16[8,128,128]{2,1,0:T(8,128)(2,1)S(1)}, u32[]{:S(2)}, u32[]{:S(2)}) collective-permute-start(bf16[8,128,128]{2,1,0:T(8,128)(2,1)} %bitcast.318), channel_id=1, source_target_pairs={{32,0},{64,32},{96,64},{128,96},{160,128},{192,160},{224,192},{256... | collective-permute-start | bytes 786440 | tf_op jit(solution)/shard_map/ppermute | solution.py:12
  16.3 5.1 %collective-permute-start.1 = (bf16[8,128,128]{2,1,0:T(8,128)(2,1)}, bf16[8,128,128]{2,1,0:T(8,128)(2,1)S(1)}, u32[]{:S(2)}, u32[]{:S(2)}) collective-permute-start(bf16[8,128,128]{2,1,0:T(8,128)(2,1)} %bitcast.320), channel_id=1, source_target_pairs={{2,0},{3,1},{4,2},{5,3},{6,4},{7,5},{8,6},{9,7},{10,8},{11,9},{12,... | collective-permute-start | bytes 786440 | tf_op jit(solution)/shard_map/ppermute | solution.py:12
  21.4 3.1 %collective-permute-start = (s32[2,8]{1,0:T(2,128)S(1)}, s32[2,8]{1,0:T(2,128)S(1)}, u32[]{:S(2)}, u32[]{:S(2)}) collective-permute-start(s32[2,8]{1,0:T(2,128)S(1)} %bitcast.337), channel_id=1, source_target_pairs={{2,0},{3,1},{4,2},{5,3},{6,4},{7,5},{8,6},{9,7},{10,8},{11,9},{12,... | collective-permute-start | bytes 200 | tf_op jit(solution)/shard_map/ppermute | solution.py:12
  30.6 3.0 %collective-permute-start.4 = (s32[2,8]{1,0:T(2,128)S(1)}, s32[2,8]{1,0:T(2,128)S(1)}, u32[]{:S(2)}, u32[]{:S(2)}) collective-permute-start(s32[2,8]{1,0:T(2,128)S(1)} %collective-permute-done), channel_id=1, source_target_pairs={{2,0},{3,1},{4,2},{5,3},{6,4},{7,5},{8,6},{9,7},{10,8},{11,9},{12,... | collective-permute-start | bytes 200 | tf_op jit(solution)/shard_map/ppermute | solution.py:12
  33.6 4.9 %collective-permute-start.10 = (s32[2,8]{1,0:T(2,128)S(1)}, s32[2,8]{1,0:T(2,128)S(1)}, u32[]{:S(2)}, u32[]{:S(2)}) collective-permute-start(s32[2,8]{1,0:T(2,128)S(1)} %collective-permute-done.6), channel_id=1, source_target_pairs={{32,0},{64,32},{96,64},{128,96},{160,128},{192,160},{224,192},{256... | collective-permute-start | bytes 200 | tf_op jit(solution)/shard_map/ppermute | solution.py:12
  38.5 3.0 %collective-permute-start.8 = (s32[2,8]{1,0:T(2,128)S(1)}, s32[2,8]{1,0:T(2,128)S(1)}, u32[]{:S(2)}, u32[]{:S(2)}) collective-permute-start(s32[2,8]{1,0:T(2,128)S(1)} %collective-permute-done.4), channel_id=1, source_target_pairs={{2,0},{3,1},{4,2},{5,3},{6,4},{7,5},{8,6},{9,7},{10,8},{11,9},{12,... | collective-permute-start | bytes 200 | tf_op jit(solution)/shard_map/ppermute | solution.py:12
  41.5 4.9 %collective-permute-start.14 = (s32[2,8]{1,0:T(2,128)S(1)}, s32[2,8]{1,0:T(2,128)S(1)}, u32[]{:S(2)}, u32[]{:S(2)}) collective-permute-start(s32[2,8]{1,0:T(2,128)S(1)} %collective-permute-done.10), channel_id=1, source_target_pairs={{32,0},{64,32},{96,64},{128,96},{160,128},{192,160},{224,192},{256... | collective-permute-start | bytes 200 | tf_op jit(solution)/shard_map/ppermute | solution.py:12
  46.4 3.0 %collective-permute-start.12 = (s32[2,8]{1,0:T(2,128)S(1)}, s32[2,8]{1,0:T(2,128)S(1)}, u32[]{:S(2)}, u32[]{:S(2)}) collective-permute-start(s32[2,8]{1,0:T(2,128)S(1)} %collective-permute-done.8), channel_id=1, source_target_pairs={{2,0},{3,1},{4,2},{5,3},{6,4},{7,5},{8,6},{9,7},{10,8},{11,9},{12,... | collective-permute-start | bytes 200 | tf_op jit(solution)/shard_map/ppermute | solution.py:12
  49.4 4.9 %collective-permute-start.18 = (s32[2,8]{1,0:T(2,128)S(1)}, s32[2,8]{1,0:T(2,128)S(1)}, u32[]{:S(2)}, u32[]{:S(2)}) collective-permute-start(s32[2,8]{1,0:T(2,128)S(1)} %collective-permute-done.14), channel_id=1, source_target_pairs={{32,0},{64,32},{96,64},{128,96},{160,128},{192,160},{224,192},{256... | collective-permute-start | bytes 200 | tf_op jit(solution)/shard_map/ppermute | solution.py:12
  54.3 3.0 %collective-permute-start.16 = (s32[2,8]{1,0:T(2,128)S(1)}, s32[2,8]{1,0:T(2,128)S(1)}, u32[]{:S(2)}, u32[]{:S(2)}) collective-permute-start(s32[2,8]{1,0:T(2,128)S(1)} %collective-permute-done.12), channel_id=1, source_target_pairs={{2,0},{3,1},{4,2},{5,3},{6,4},{7,5},{8,6},{9,7},{10,8},{11,9},{12,... | collective-permute-start | bytes 200 | tf_op jit(solution)/shard_map/ppermute | solution.py:12
  57.4 4.9 %collective-permute-start.22 = (s32[2,8]{1,0:T(2,128)S(1)}, s32[2,8]{1,0:T(2,128)S(1)}, u32[]{:S(2)}, u32[]{:S(2)}) collective-permute-start(s32[2,8]{1,0:T(2,128)S(1)} %collective-permute-done.18), channel_id=1, source_target_pairs={{32,0},{64,32},{96,64},{128,96},{160,128},{192,160},{224,192},{256... | collective-permute-start | bytes 200 | tf_op jit(solution)/shard_map/ppermute | solution.py:12
  62.2 3.0 %collective-permute-start.20 = (s32[2,8]{1,0:T(2,128)S(1)}, s32[2,8]{1,0:T(2,128)S(1)}, u32[]{:S(2)}, u32[]{:S(2)}) collective-permute-start(s32[2,8]{1,0:T(2,128)S(1)} %collective-permute-done.16), channel_id=1, source_target_pairs={{2,0},{3,1},{4,2},{5,3},{6,4},{7,5},{8,6},{9,7},{10,8},{11,9},{12,... | collective-permute-start | bytes 200 | tf_op jit(solution)/shard_map/ppermute | solution.py:12
  65.3 4.9 %collective-permute-start.26 = (s32[2,8]{1,0:T(2,128)S(1)}, s32[2,8]{1,0:T(2,128)S(1)}, u32[]{:S(2)}, u32[]{:S(2)}) collective-permute-start(s32[2,8]{1,0:T(2,128)S(1)} %collective-permute-done.22), channel_id=1, source_target_pairs={{32,0},{64,32},{96,64},{128,96},{160,128},{192,160},{224,192},{256... | collective-permute-start | bytes 200 | tf_op jit(solution)/shard_map/ppermute | solution.py:12
  76.1 3.6 %collective-permute-start.7 = (bf16[8,128,128]{2,1,0:T(8,128)(2,1)S(1)}, bf16[8,128,128]{2,1,0:T(8,128)(2,1)S(1)}, u32[]{:S(2)}, u32[]{:S(2)}) collective-permute-start(bf16[8,128,128]{2,1,0:T(8,128)(2,1)S(1)} %collective-permute-done.3), channel_id=1, source_target_pairs={{32,0},{64,32},{96,64},{128,96},{160,128},{192,160},{224,192},{256... | collective-permute-start | bytes 786440 | tf_op jit(solution)/shard_map/ppermute | solution.py:12
  79.7 3.4 %collective-permute-start.5 = (bf16[8,128,128]{2,1,0:T(8,128)(2,1)S(1)}, bf16[8,128,128]{2,1,0:T(8,128)(2,1)S(1)}, u32[]{:S(2)}, u32[]{:S(2)}) collective-permute-start(bf16[8,128,128]{2,1,0:T(8,128)(2,1)S(1)} %collective-permute-done.1), channel_id=1, source_target_pairs={{2,0},{3,1},{4,2},{5,3},{6,4},{7,5},{8,6},{9,7},{10,8},{11,9},{12,... | collective-permute-start | bytes 786440 | tf_op jit(solution)/shard_map/ppermute | solution.py:12
  87.6 6.4 %collective-permute-start.11 = (bf16[8,128,128]{2,1,0:T(8,128)(2,1)S(1)}, bf16[8,128,128]{2,1,0:T(8,128)(2,1)S(1)}, u32[]{:S(2)}, u32[]{:S(2)}) collective-permute-start(bf16[8,128,128]{2,1,0:T(8,128)(2,1)S(1)} %collective-permute-done.7), channel_id=1, source_target_pairs={{32,0},{64,32},{96,64},{128,96},{160,128},{192,160},{224,192},{256... | collective-permute-start | bytes 786440 | tf_op jit(solution)/shard_map/ppermute | solution.py:12
  102.0 6.7 %collective-permute-start.15 = (bf16[8,128,128]{2,1,0:T(8,128)(2,1)S(1)}, bf16[8,128,128]{2,1,0:T(8,128)(2,1)S(1)}, u32[]{:S(2)}, u32[]{:S(2)}) collective-permute-start(bf16[8,128,128]{2,1,0:T(8,128)(2,1)S(1)} %collective-permute-done.11), channel_id=1, source_target_pairs={{32,0},{64,32},{96,64},{128,96},{160,128},{192,160},{224,192},{256... | collective-permute-start | bytes 786440 | tf_op jit(solution)/shard_map/ppermute | solution.py:12
  117.0 7.4 %collective-permute-start.19 = (bf16[8,128,128]{2,1,0:T(8,128)(2,1)S(1)}, bf16[8,128,128]{2,1,0:T(8,128)(2,1)S(1)}, u32[]{:S(2)}, u32[]{:S(2)}) collective-permute-start(bf16[8,128,128]{2,1,0:T(8,128)(2,1)S(1)} %collective-permute-done.15), channel_id=1, source_target_pairs={{32,0},{64,32},{96,64},{128,96},{160,128},{192,160},{224,192},{256... | collective-permute-start | bytes 786440 | tf_op jit(solution)/shard_map/ppermute | solution.py:12
  127.3 5.1 %collective-permute-done.19 = bf16[8,128,128]{2,1,0:T(8,128)(2,1)S(1)} collective-permute-done((bf16[8,128,128]{2,1,0:T(8,128)(2,1)S(1)}, bf16[8,128,128]{2,1,0:T(8,128)(2,1)S(1)}, u32[]{:S(2)}, u32[]{:S(2)}) %collective-permute-start.19) | collective-permute-done | bytes 262176 | tf_op jit(solution)/shard_map/ppermute | solution.py:12
  134.9 8.1 %collective-permute-start.23 = (bf16[8,128,128]{2,1,0:T(8,128)(2,1)S(1)}, bf16[8,128,128]{2,1,0:T(8,128)(2,1)S(1)}, u32[]{:S(2)}, u32[]{:S(2)}) collective-permute-start(bf16[8,128,128]{2,1,0:T(8,128)(2,1)S(1)} %collective-permute-done.19), channel_id=1, source_target_pairs={{32,0},{64,32},{96,64},{128,96},{160,128},{192,160},{224,192},{256... | collective-permute-start | bytes 786440 | tf_op jit(solution)/shard_map/ppermute | solution.py:12
  145.3 5.6 %collective-permute-done.23 = bf16[8,128,128]{2,1,0:T(8,128)(2,1)S(1)} collective-permute-done((bf16[8,128,128]{2,1,0:T(8,128)(2,1)S(1)}, bf16[8,128,128]{2,1,0:T(8,128)(2,1)S(1)}, u32[]{:S(2)}, u32[]{:S(2)}) %collective-permute-start.23) | collective-permute-done | bytes 262176 | tf_op jit(solution)/shard_map/ppermute | solution.py:12
  153.4 8.1 %collective-permute-start.27 = (bf16[8,128,128]{2,1,0:T(8,128)(2,1)S(1)}, bf16[8,128,128]{2,1,0:T(8,128)(2,1)S(1)}, u32[]{:S(2)}, u32[]{:S(2)}) collective-permute-start(bf16[8,128,128]{2,1,0:T(8,128)(2,1)S(1)} %collective-permute-done.23), channel_id=1, source_target_pairs={{32,0},{64,32},{96,64},{128,96},{160,128},{192,160},{224,192},{256... | collective-permute-start | bytes 786440 | tf_op jit(solution)/shard_map/ppermute | solution.py:12
  163.9 3.2 %collective-permute-done.27 = bf16[8,128,128]{2,1,0:T(8,128)(2,1)S(1)} collective-permute-done((bf16[8,128,128]{2,1,0:T(8,128)(2,1)S(1)}, bf16[8,128,128]{2,1,0:T(8,128)(2,1)S(1)}, u32[]{:S(2)}, u32[]{:S(2)}) %collective-permute-start.27) | collective-permute-done | bytes 262176 | tf_op jit(solution)/shard_map/ppermute | solution.py:12
  172.5 21.8 %collective-permute-start.28 = (f32[8,128,128]{2,0,1:T(8,128)S(1)}, f32[8,128,128]{2,0,1:T(8,128)S(1)}, u32[]{:S(2)}, u32[]{:S(2)}) collective-permute-start(f32[8,128,128]{2,0,1:T(8,128)S(1)} %fusion.16), channel_id=1, source_target_pairs={{0,1},{1,0},{2,3},{3,2},{4,5},{5,4},{6,7},{7,6},{8,9},{9,8},{10,11... | collective-permute-start | bytes 1572872 | tf_op jit(solution)/shard_map/ppermute | solution.py:16
  (120 shorter events, 54.7 us)
Async XLA Ops:
  0.0 74.5 %collective-permute-start.3 = (bf16[8,128,128]{2,1,0:T(8,128)(2,1)}, bf16[8,128,128]{2,1,0:T(8,128)(2,1)S(1)}, u32[]{:S(2)}, u32[]{:S(2)}) collective-permute-start(bf16[8,128,128]{2,1,0:T(8,128)(2,1)} %bitcast.318), channel_id=1, source_target_pairs={{32,0},{64,32},{96,64},{128,96},{160,128},{192,160},{224,192},{256... | collective-permute-start | bytes 786440 | tf_op jit(solution)/shard_map/ppermute | solution.py:12
  14.1 14.2 %collective-permute-start.2 = (s32[2,8]{1,0:T(2,128)S(1)}, s32[2,8]{1,0:T(2,128)S(1)}, u32[]{:S(2)}, u32[]{:S(2)}) collective-permute-start(s32[2,8]{1,0:T(2,128)S(1)} %bitcast.336), channel_id=1, source_target_pairs={{32,0},{64,32},{96,64},{128,96},{160,128},{192,160},{224,192},{256... | collective-permute-start | bytes 200 | tf_op jit(solution)/shard_map/ppermute | solution.py:12
  16.3 59.0 %collective-permute-start.1 = (bf16[8,128,128]{2,1,0:T(8,128)(2,1)}, bf16[8,128,128]{2,1,0:T(8,128)(2,1)S(1)}, u32[]{:S(2)}, u32[]{:S(2)}) collective-permute-start(bf16[8,128,128]{2,1,0:T(8,128)(2,1)} %bitcast.320), channel_id=1, source_target_pairs={{2,0},{3,1},{4,2},{5,3},{6,4},{7,5},{8,6},{9,7},{10,8},{11,9},{12,... | collective-permute-start | bytes 786440 | tf_op jit(solution)/shard_map/ppermute | solution.py:12
  21.4 9.1 %collective-permute-start = (s32[2,8]{1,0:T(2,128)S(1)}, s32[2,8]{1,0:T(2,128)S(1)}, u32[]{:S(2)}, u32[]{:S(2)}) collective-permute-start(s32[2,8]{1,0:T(2,128)S(1)} %bitcast.337), channel_id=1, source_target_pairs={{2,0},{3,1},{4,2},{5,3},{6,4},{7,5},{8,6},{9,7},{10,8},{11,9},{12,... | collective-permute-start | bytes 200 | tf_op jit(solution)/shard_map/ppermute | solution.py:12
  30.6 7.9 %collective-permute-start.4 = (s32[2,8]{1,0:T(2,128)S(1)}, s32[2,8]{1,0:T(2,128)S(1)}, u32[]{:S(2)}, u32[]{:S(2)}) collective-permute-start(s32[2,8]{1,0:T(2,128)S(1)} %collective-permute-done), channel_id=1, source_target_pairs={{2,0},{3,1},{4,2},{5,3},{6,4},{7,5},{8,6},{9,7},{10,8},{11,9},{12,... | collective-permute-start | bytes 200 | tf_op jit(solution)/shard_map/ppermute | solution.py:12
  33.6 7.9 %collective-permute-start.10 = (s32[2,8]{1,0:T(2,128)S(1)}, s32[2,8]{1,0:T(2,128)S(1)}, u32[]{:S(2)}, u32[]{:S(2)}) collective-permute-start(s32[2,8]{1,0:T(2,128)S(1)} %collective-permute-done.6), channel_id=1, source_target_pairs={{32,0},{64,32},{96,64},{128,96},{160,128},{192,160},{224,192},{256... | collective-permute-start | bytes 200 | tf_op jit(solution)/shard_map/ppermute | solution.py:12
  38.5 7.9 %collective-permute-start.8 = (s32[2,8]{1,0:T(2,128)S(1)}, s32[2,8]{1,0:T(2,128)S(1)}, u32[]{:S(2)}, u32[]{:S(2)}) collective-permute-start(s32[2,8]{1,0:T(2,128)S(1)} %collective-permute-done.4), channel_id=1, source_target_pairs={{2,0},{3,1},{4,2},{5,3},{6,4},{7,5},{8,6},{9,7},{10,8},{11,9},{12,... | collective-permute-start | bytes 200 | tf_op jit(solution)/shard_map/ppermute | solution.py:12
  41.5 7.9 %collective-permute-start.14 = (s32[2,8]{1,0:T(2,128)S(1)}, s32[2,8]{1,0:T(2,128)S(1)}, u32[]{:S(2)}, u32[]{:S(2)}) collective-permute-start(s32[2,8]{1,0:T(2,128)S(1)} %collective-permute-done.10), channel_id=1, source_target_pairs={{32,0},{64,32},{96,64},{128,96},{160,128},{192,160},{224,192},{256... | collective-permute-start | bytes 200 | tf_op jit(solution)/shard_map/ppermute | solution.py:12
  46.4 7.9 %collective-permute-start.12 = (s32[2,8]{1,0:T(2,128)S(1)}, s32[2,8]{1,0:T(2,128)S(1)}, u32[]{:S(2)}, u32[]{:S(2)}) collective-permute-start(s32[2,8]{1,0:T(2,128)S(1)} %collective-permute-done.8), channel_id=1, source_target_pairs={{2,0},{3,1},{4,2},{5,3},{6,4},{7,5},{8,6},{9,7},{10,8},{11,9},{12,... | collective-permute-start | bytes 200 | tf_op jit(solution)/shard_map/ppermute | solution.py:12
  49.4 7.9 %collective-permute-start.18 = (s32[2,8]{1,0:T(2,128)S(1)}, s32[2,8]{1,0:T(2,128)S(1)}, u32[]{:S(2)}, u32[]{:S(2)}) collective-permute-start(s32[2,8]{1,0:T(2,128)S(1)} %collective-permute-done.14), channel_id=1, source_target_pairs={{32,0},{64,32},{96,64},{128,96},{160,128},{192,160},{224,192},{256... | collective-permute-start | bytes 200 | tf_op jit(solution)/shard_map/ppermute | solution.py:12
  54.3 7.9 %collective-permute-start.16 = (s32[2,8]{1,0:T(2,128)S(1)}, s32[2,8]{1,0:T(2,128)S(1)}, u32[]{:S(2)}, u32[]{:S(2)}) collective-permute-start(s32[2,8]{1,0:T(2,128)S(1)} %collective-permute-done.12), channel_id=1, source_target_pairs={{2,0},{3,1},{4,2},{5,3},{6,4},{7,5},{8,6},{9,7},{10,8},{11,9},{12,... | collective-permute-start | bytes 200 | tf_op jit(solution)/shard_map/ppermute | solution.py:12
  57.4 7.9 %collective-permute-start.22 = (s32[2,8]{1,0:T(2,128)S(1)}, s32[2,8]{1,0:T(2,128)S(1)}, u32[]{:S(2)}, u32[]{:S(2)}) collective-permute-start(s32[2,8]{1,0:T(2,128)S(1)} %collective-permute-done.18), channel_id=1, source_target_pairs={{32,0},{64,32},{96,64},{128,96},{160,128},{192,160},{224,192},{256... | collective-permute-start | bytes 200 | tf_op jit(solution)/shard_map/ppermute | solution.py:12
  62.2 7.9 %collective-permute-start.20 = (s32[2,8]{1,0:T(2,128)S(1)}, s32[2,8]{1,0:T(2,128)S(1)}, u32[]{:S(2)}, u32[]{:S(2)}) collective-permute-start(s32[2,8]{1,0:T(2,128)S(1)} %collective-permute-done.16), channel_id=1, source_target_pairs={{2,0},{3,1},{4,2},{5,3},{6,4},{7,5},{8,6},{9,7},{10,8},{11,9},{12,... | collective-permute-start | bytes 200 | tf_op jit(solution)/shard_map/ppermute | solution.py:12
  65.3 7.9 %collective-permute-start.26 = (s32[2,8]{1,0:T(2,128)S(1)}, s32[2,8]{1,0:T(2,128)S(1)}, u32[]{:S(2)}, u32[]{:S(2)}) collective-permute-start(s32[2,8]{1,0:T(2,128)S(1)} %collective-permute-done.22), channel_id=1, source_target_pairs={{32,0},{64,32},{96,64},{128,96},{160,128},{192,160},{224,192},{256... | collective-permute-start | bytes 200 | tf_op jit(solution)/shard_map/ppermute | solution.py:12
  76.1 7.5 %collective-permute-start.7 = (bf16[8,128,128]{2,1,0:T(8,128)(2,1)S(1)}, bf16[8,128,128]{2,1,0:T(8,128)(2,1)S(1)}, u32[]{:S(2)}, u32[]{:S(2)}) collective-permute-start(bf16[8,128,128]{2,1,0:T(8,128)(2,1)S(1)} %collective-permute-done.3), channel_id=1, source_target_pairs={{32,0},{64,32},{96,64},{128,96},{160,128},{192,160},{224,192},{256... | collective-permute-start | bytes 786440 | tf_op jit(solution)/shard_map/ppermute | solution.py:12
  87.6 10.2 %collective-permute-start.11 = (bf16[8,128,128]{2,1,0:T(8,128)(2,1)S(1)}, bf16[8,128,128]{2,1,0:T(8,128)(2,1)S(1)}, u32[]{:S(2)}, u32[]{:S(2)}) collective-permute-start(bf16[8,128,128]{2,1,0:T(8,128)(2,1)S(1)} %collective-permute-done.7), channel_id=1, source_target_pairs={{32,0},{64,32},{96,64},{128,96},{160,128},{192,160},{224,192},{256... | collective-permute-start | bytes 786440 | tf_op jit(solution)/shard_map/ppermute | solution.py:12
  102.0 12.0 %collective-permute-start.15 = (bf16[8,128,128]{2,1,0:T(8,128)(2,1)S(1)}, bf16[8,128,128]{2,1,0:T(8,128)(2,1)S(1)}, u32[]{:S(2)}, u32[]{:S(2)}) collective-permute-start(bf16[8,128,128]{2,1,0:T(8,128)(2,1)S(1)} %collective-permute-done.11), channel_id=1, source_target_pairs={{32,0},{64,32},{96,64},{128,96},{160,128},{192,160},{224,192},{256... | collective-permute-start | bytes 786440 | tf_op jit(solution)/shard_map/ppermute | solution.py:12
  117.0 15.4 %collective-permute-start.19 = (bf16[8,128,128]{2,1,0:T(8,128)(2,1)S(1)}, bf16[8,128,128]{2,1,0:T(8,128)(2,1)S(1)}, u32[]{:S(2)}, u32[]{:S(2)}) collective-permute-start(bf16[8,128,128]{2,1,0:T(8,128)(2,1)S(1)} %collective-permute-done.15), channel_id=1, source_target_pairs={{32,0},{64,32},{96,64},{128,96},{160,128},{192,160},{224,192},{256... | collective-permute-start | bytes 786440 | tf_op jit(solution)/shard_map/ppermute | solution.py:12
  124.4 9.7 %collective-permute-start.17 = (bf16[8,128,128]{2,1,0:T(8,128)(2,1)S(1)}, bf16[8,128,128]{2,1,0:T(8,128)(2,1)S(1)}, u32[]{:S(2)}, u32[]{:S(2)}) collective-permute-start(bf16[8,128,128]{2,1,0:T(8,128)(2,1)S(1)} %collective-permute-done.13), channel_id=1, source_target_pairs={{2,0},{3,1},{4,2},{5,3},{6,4},{7,5},{8,6},{9,7},{10,8},{11,9},{12,... | collective-permute-start | bytes 786440 | tf_op jit(solution)/shard_map/ppermute | solution.py:12
  134.9 16.1 %collective-permute-start.23 = (bf16[8,128,128]{2,1,0:T(8,128)(2,1)S(1)}, bf16[8,128,128]{2,1,0:T(8,128)(2,1)S(1)}, u32[]{:S(2)}, u32[]{:S(2)}) collective-permute-start(bf16[8,128,128]{2,1,0:T(8,128)(2,1)S(1)} %collective-permute-done.19), channel_id=1, source_target_pairs={{32,0},{64,32},{96,64},{128,96},{160,128},{192,160},{224,192},{256... | collective-permute-start | bytes 786440 | tf_op jit(solution)/shard_map/ppermute | solution.py:12
  142.9 9.6 %collective-permute-start.21 = (bf16[8,128,128]{2,1,0:T(8,128)(2,1)S(1)}, bf16[8,128,128]{2,1,0:T(8,128)(2,1)S(1)}, u32[]{:S(2)}, u32[]{:S(2)}) collective-permute-start(bf16[8,128,128]{2,1,0:T(8,128)(2,1)S(1)} %collective-permute-done.17), channel_id=1, source_target_pairs={{2,0},{3,1},{4,2},{5,3},{6,4},{7,5},{8,6},{9,7},{10,8},{11,9},{12,... | collective-permute-start | bytes 786440 | tf_op jit(solution)/shard_map/ppermute | solution.py:12
  153.4 13.7 %collective-permute-start.27 = (bf16[8,128,128]{2,1,0:T(8,128)(2,1)S(1)}, bf16[8,128,128]{2,1,0:T(8,128)(2,1)S(1)}, u32[]{:S(2)}, u32[]{:S(2)}) collective-permute-start(bf16[8,128,128]{2,1,0:T(8,128)(2,1)S(1)} %collective-permute-done.23), channel_id=1, source_target_pairs={{32,0},{64,32},{96,64},{128,96},{160,128},{192,160},{224,192},{256... | collective-permute-start | bytes 786440 | tf_op jit(solution)/shard_map/ppermute | solution.py:12
  161.5 8.2 %collective-permute-start.25 = (bf16[8,128,128]{2,1,0:T(8,128)(2,1)S(1)}, bf16[8,128,128]{2,1,0:T(8,128)(2,1)S(1)}, u32[]{:S(2)}, u32[]{:S(2)}) collective-permute-start(bf16[8,128,128]{2,1,0:T(8,128)(2,1)S(1)} %collective-permute-done.21), channel_id=1, source_target_pairs={{2,0},{3,1},{4,2},{5,3},{6,4},{7,5},{8,6},{9,7},{10,8},{11,9},{12,... | collective-permute-start | bytes 786440 | tf_op jit(solution)/shard_map/ppermute | solution.py:12
  172.5 23.4 %collective-permute-start.28 = (f32[8,128,128]{2,0,1:T(8,128)S(1)}, f32[8,128,128]{2,0,1:T(8,128)S(1)}, u32[]{:S(2)}, u32[]{:S(2)}) collective-permute-start(f32[8,128,128]{2,0,1:T(8,128)S(1)} %fusion.16), channel_id=1, source_target_pairs={{0,1},{1,0},{2,3},{3,2},{4,5},{5,4},{6,7},{7,6},{8,9},{9,8},{10,11... | collective-permute-start | bytes 1572872 | tf_op jit(solution)/shard_map/ppermute | solution.py:16
  (9 other events, 52.1 us)
where the time goes:
time: 198 us; the launch traced here: 197 us
  starting transfers between devices  145 us (73%)
  waiting for transfers between devices  30.8 us (16%)
  matrix products  10.1 us (5%)
  local copies, waits for them, and re-layouts  9.96 us (5%)
    ppermute x28, starting transfers between devices, from_behind(): return lax.ppermute(block, axis, route)  123 us
    ppermute x28, waiting for transfers between devices, from_behind(): return lax.ppermute(block, axis, route)  29.3 us
    ppermute x1, starting transfers between devices, from_partner(): lax.ppermute(shard, axis, [(i, i ^ 1 << stride) for i in range(lax.axis_s...  21.8 us
    reshape x16, local copies, waits for them, and re-layouts, densify(): flat.reshape(TILE, TILE, width, width).transpose(0, 2, 1, 3)  6.55 us
    dot_general x16, matrix products, densify(): jnp.dot(selector, blocks.reshape(count, width * width), preferred_element...  5.52 us
  transfers between devices with their start and end apart: 29, of which 13 were waited for; matrix products, arithmetic and copies ran while one was open for 6% of the time, Pallas kernels for 0%

commit v1 on v0

v1 whole, which is shorter than its diff:
```python
import functools

import jax
import jax.numpy as jnp
from jax import lax
from jax.experimental import pallas as pl
from jax.experimental.pallas import tpu as pltpu
from jax.sharding import PartitionSpec as P

TILE = 4
NNZ = 8
WIDTH = 128
GRID = 16
HALF = 8
SPAN = TILE * WIDTH
ROWS = NNZ * WIDTH + 16
BOTH = ("row", "col")


def even_pair(n):
    return n ^ 1


def odd_pair(n):
    return ((n - 1) ^ 1) + 1


def flat_id(i, c, role):
    layer = role ^ int((i + c) % GRID >= HALF)
    return i * 2 * GRID + c * 2 + layer


def route(step):
    pairs = []
    for i in range(GRID):
        for c in range(GRID):
            for role in range(2):
                z, y, x = step(i % HALF, c // 2, c % 2, role)
                pairs.append((flat_id(i, c, role), flat_id(i // HALF * HALF + z % HALF, (y % HALF) * 2 + x, role)))
    return pairs


def pair_of(kind, n, role):
    return even_pair(n) if kind == role else odd_pair(n)


def exchange_z(x, kind):
    return lax.ppermute(x, BOTH, route(lambda z, y, xl, r: (pair_of(kind, z, r), y, xl)))


def exchange_y(x, kind):
    return lax.ppermute(x, BOTH, route(lambda z, y, xl, r: (z, pair_of(kind, y, r), xl)))


def exchange_x(x):
    return lax.ppermute(x, BOTH, route(lambda z, y, xl, r: (z, y, xl ^ 1)))


def with_slots(blocks, places):
    slots = (places[0] * TILE + places[1]).astype(blocks.dtype)
    tail = jnp.pad(slots[None, :], ((0, ROWS - NNZ * WIDTH - 1), (0, WIDTH - NNZ)))
    return jnp.concatenate([blocks.reshape(NNZ * WIDTH, WIDTH), tail], axis=0)


def product_kernel(
    keep, hp, h1, h2, h3, zp, z1, z2, z3, z4, own, other, hd, zd, acc, idx_v, idx_s, sem
):
    i = lax.axis_index("row")
    j = lax.axis_index("col")
    c = j >> 1
    layer = j & 1
    z = i & 7
    y = c >> 1
    xl = c & 1
    role = layer ^ (((i + c) & 15) >> 3)

    def near(n, kind):
        even = n ^ 1
        odd = ((n - 1) ^ 1) + 1
        return jnp.where(role == kind, even, odd) & 7

    def h_at(yy, xx):
        return (z + 2 * yy + xx) & 7

    def z_at(zz):
        return (zz + c) & 7

    ya = near(y, 0)
    yb = near(y, 1)
    yab = near(yb, 0)
    p = near(z, 0)
    w = near(z, 1)
    pw = near(w, 0)
    wp = near(p, 1)
    pwp = near(wp, 0)
    wpw = near(pw, 1)
    pwpw = near(wpw, 0)
    tiles = [
        (hp, 0, h_at(y, xl)),
        (h1, 0, h_at(y, xl ^ 1)),
        (h2, 0, h_at(ya, xl)),
        (h2, 1, h_at(ya, xl ^ 1)),
        (h3, 0, h_at(yb, xl)),
        (h3, 1, h_at(yb, xl ^ 1)),
        (h3, 2, h_at(yab, xl)),
        (h3, 3, h_at(yab, xl ^ 1)),
        (zp, 0, z_at(z)),
        (z1, 0, z_at(p)),
        (z2, 0, z_at(w)),
        (z2, 1, z_at(pw)),
        (z3, 0, z_at(wp)),
        (z3, 1, z_at(pwp)),
        (z4, 0, z_at(wpw)),
        (z4, 1, z_at(pwpw)),
    ]
    for n, (buf, part, _) in enumerate(tiles):
        base = part * ROWS + NNZ * WIDTH
        idx_v[n : n + 1, :] = buf[base : base + 16, :].astype(jnp.float32).astype(jnp.int32)[0:1]
    copy = pltpu.make_async_copy(idx_v, idx_s, sem)
    copy.start()

    @pl.loop(0, HALF)
    def _(u):
        at = pl.multiple_of(u * SPAN, SPAN)
        hd[:, pl.ds(at, SPAN)] = jnp.zeros((SPAN, SPAN), hd.dtype)
        zd[pl.ds(at, SPAN), :] = jnp.zeros((SPAN, SPAN), zd.dtype)

    copy.wait()
    for n, (buf, part, u) in enumerate(tiles):
        for k in range(NNZ):
            slot = idx_s[n, k]
            block = buf[part * ROWS + k * WIDTH : part * ROWS + (k + 1) * WIDTH, :]
            r = (slot >> 2) * WIDTH
            q = (slot & 3) * WIDTH
            if n < HALF:
                hd[pl.ds(pl.multiple_of(r, WIDTH), WIDTH), pl.ds(pl.multiple_of(u * SPAN + q, WIDTH), WIDTH)] = block
            else:
                zd[pl.ds(pl.multiple_of(u * SPAN + r, WIDTH), WIDTH), pl.ds(pl.multiple_of(q, WIDTH), WIDTH)] = block
    for m in range(0, SPAN, 256):
        acc[m : m + 256, :] = jnp.dot(hd[m : m + 256, :], zd[...], preferred_element_type=jnp.float32)
    for q in range(TILE):
        for dst, first in ((own, layer * TILE), (other, (1 - layer) * TILE)):
            r = pl.multiple_of(keep[0, first + q] * WIDTH, WIDTH)
            s = pl.multiple_of(keep[1, first + q] * WIDTH, WIDTH)
            dst[q] = acc[pl.ds(r, WIDTH), pl.ds(s, WIDTH)]


def product(keep, *tiles):
    vmem = pl.BlockSpec(memory_space=pltpu.VMEM)
    half = jax.ShapeDtypeStruct((TILE, WIDTH, WIDTH), jnp.float32)
    return pl.pallas_call(
        product_kernel,
        out_shape=(half, half),
        in_specs=[pl.BlockSpec(memory_space=pltpu.SMEM)] + [vmem] * len(tiles),
        out_specs=(vmem, vmem),
        scratch_shapes=[
            pltpu.VMEM((SPAN, HALF * SPAN), jnp.bfloat16),
            pltpu.VMEM((HALF * SPAN, SPAN), jnp.bfloat16),
            pltpu.VMEM((SPAN, SPAN), jnp.float32),
            pltpu.VMEM((GRID, WIDTH), jnp.int32),
            pltpu.SMEM((GRID, WIDTH), jnp.int32),
            pltpu.SemaphoreType.DMA,
        ],
        compiler_params=pltpu.CompilerParams(vmem_limit_bytes=32 * 1024 * 1024),
        cost_estimate=pl.CostEstimate(
            flops=2 * SPAN * SPAN * SPAN * HALF, bytes_accessed=5 * 1024 * 1024, transcendentals=0
        ),
        name="product",
    )(keep, *tiles)


def per_device(h_blocks, h_index, z_blocks, z_index, keep_index):
    zp = with_slots(z_blocks[0, 0], z_index[0, 0])
    z1 = exchange_z(zp, 0)
    hp = with_slots(h_blocks[0, 0], h_index[0, 0])
    h1 = exchange_x(hp)
    z2 = exchange_z(jnp.concatenate([zp, z1], axis=0), 1)
    h2 = exchange_y(jnp.concatenate([hp, h1], axis=0), 0)
    z3 = exchange_z(z2, 0)
    h3 = exchange_y(jnp.concatenate([hp, h1, h2], axis=0), 1)
    z4 = exchange_z(z3, 1)
    own, other = product(keep_index[0, 0], hp, h1, h2, h3, zp, z1, z2, z3, z4)
    partner = lax.ppermute(other, "col", [(j, j ^ 1) for j in range(2 * GRID)])
    return (own + partner)[None, None]


def solution(mesh):
    return jax.shard_map(
        per_device,
        mesh=mesh,
        in_specs=(
            P("row", "col", None, None, None),
            P("row", "col", None, None),
            P("row", "col", None, None, None),
            P("row", "col", None, None),
            P("row", "col", None, None),
        ),
        out_specs=P("row", "col", None, None, None),
        check_vma=False,
    )
```

time: 198 us -> 68.2 us (0.34)
  starting transfers between devices: 145 us -> 35.7 us
  matrix products: 10.1 us -> 0 us
  local copies, waits for them, and re-layouts: 9.96 us -> 0.03 us
  waiting for transfers between devices: 30.8 us -> 22.9 us
  Pallas kernels: 0 us -> 4.65 us
  other arithmetic: 0.18 us -> 4.38 us
    ppermute x29 -> x8, starting transfers between devices: 145 us -> 35.7 us  [the longest x4 19.4 us: exchange_z(): lax.ppermute(x, BOTH, route(lambda z, y, xl, r: (pair_of(kind, z, r), y,...]
    dot_general x25 -> x0, matrix products: 10.1 us -> none  [the longest x16 5.52 us: densify(): jnp.dot(selector, blocks.reshape(count, width * width), preferred_element...]
    ppermute x29 -> x8, waiting for transfers between devices: 30.8 us -> 22.9 us  [the longest x4 16.5 us: exchange_z(): lax.ppermute(x, BOTH, route(lambda z, y, xl, r: (pair_of(kind, z, r), y,...]
    reshape x18 -> x0, local copies, waits for them, and re-layouts: 7.03 us -> none  [the longest x16 6.55 us: densify(): flat.reshape(TILE, TILE, width, width).transpose(0, 2, 1, 3)]
    pallas_call x0 -> x1, Pallas kernels: none -> 4.65 us  [product(): pl.pallas_call(product_kernel, out_shape=(half, half), in_specs=[pl.Block...]
    unnamed x24 -> x6, local copies, waits for them, and re-layouts: 2.21 us -> 0.01 us
    concatenate x0 -> x5, other arithmetic: none -> 2.12 us  [the longest x2 1.98 us: with_slots(): return jnp.concatenate([blocks.reshape(NNZ * WIDTH, WIDTH), tail], axis=0)]
  transfers between devices with their start and end apart: 29 -> 8, of which waited for: 13 -> 5; matrix products, arithmetic and copies ran while one was open for 6% -> 3% of each run, Pallas kernels for 0% -> 0%
where the time goes in v1:
time: 68.2 us; the launch traced here: 67.8 us
  starting transfers between devices  35.7 us (52%)
  waiting for transfers between devices  22.9 us (34%)
  Pallas kernels  4.65 us (7%)
  other arithmetic  4.38 us (6%)
    ppermute x4, starting transfers between devices, exchange_z(): lax.ppermute(x, BOTH, route(lambda z, y, xl, r: (pair_of(kind, z, r), y,...  19.4 us
    ppermute x4, waiting for transfers between devices, exchange_z(): lax.ppermute(x, BOTH, route(lambda z, y, xl, r: (pair_of(kind, z, r), y,...  16.5 us
    ppermute x2, starting transfers between devices, exchange_y(): lax.ppermute(x, BOTH, route(lambda z, y, xl, r: (z, pair_of(kind, y, r),...  6.74 us
    ppermute x1, starting transfers between devices, per_device(): partner = lax.ppermute(other, 'col', [(j, j ^ 1) for j in range(2 * GRID)])  5.58 us
    ppermute x2, waiting for transfers between devices, exchange_y(): lax.ppermute(x, BOTH, route(lambda z, y, xl, r: (z, pair_of(kind, y, r),...  5.27 us
    pallas_call x1, Pallas kernels, product(): pl.pallas_call(product_kernel, out_shape=(half, half), in_specs=[pl.Block...  4.65 us
    ppermute x1, starting transfers between devices, exchange_x(): return lax.ppermute(x, BOTH, route(lambda z, y, xl, r: (z, y, xl ^ 1)))  3.95 us
    concatenate x2, other arithmetic, with_slots(): return jnp.concatenate([blocks.reshape(NNZ * WIDTH, WIDTH), tail], axis=0)  1.98 us
  transfers between devices with their start and end apart: 8, of which 5 were waited for; matrix products, arithmetic and copies ran while one was open for 3% of the time, Pallas kernels for 0%

profile of v1, /device:TPU:1, one launch (start us, length us, event | category | flops | bytes accessed | tf_op | source)
XLA Modules:
  0.0 67.8 jit_solution(15430087717814131240)
XLA Ops:
  0.0 0.8 %convert_bitcast_fusion.1 = bf16[1,8]{1,0:T(2,128)(2,1)S(1)} fusion(s32[1,1,2,8]{3,2,1,0:T(2,128)} %param.6), kind=kLoop, calls=%fused_computation.7 | loop fusion | flops 24 | bytes 80 | tf_op jit(solution)/shard_map/convert_element_type | solution.py:60
  0.8 1.0 %pad_maximum_fusion.3.hp = bf16[1040,128]{1,0:T(8,128)(2,1)S(1)} fusion(bf16[16,128]{1,0:T(8,128)(2,1)S(1)} %pad.7, bf16[1024,128]{1,0:T(8,128)(2,1)} %bitcast.10), kind=kLoop, calls=%fused_computation.3 | loop fusion | flops 532480 | bytes 532480 | tf_op jit(solution)/shard_map/concatenate | solution.py:62
  1.8 3.9 %collective-permute-start = (bf16[1040,128]{1,0:T(8,128)(2,1)S(1)}, bf16[1040,128]{1,0:T(8,128)(2,1)S(1)}, u32[]{:S(2)}, u32[]{:S(2)}) collective-permute-start(bf16[1040,128]{1,0:T(8,128)(2,1)S(1)} %pad_maximum_fusion.3.hp), channel_id=1, source_target_pairs={{0,2},{1,3},{2,0},{3,1},{4,6},{5,7},{6,4},{7,5},{8,10},{9,11},{10,... | collective-permute-start | bytes 798728 | tf_op jit(solution)/shard_map/ppermute | solution.py:56
  5.8 0.8 %convert_bitcast_fusion = bf16[1,8]{1,0:T(2,128)(2,1)S(1)} fusion(s32[1,1,2,8]{3,2,1,0:T(2,128)} %param.8), kind=kLoop, calls=%fused_computation.6 | loop fusion | flops 24 | bytes 80 | tf_op jit(solution)/shard_map/convert_element_type | solution.py:60
  6.5 1.0 %pad_maximum_fusion.4.zp = bf16[1040,128]{1,0:T(8,128)(2,1)S(1)} fusion(bf16[16,128]{1,0:T(8,128)(2,1)S(1)} %pad.8, bf16[1024,128]{1,0:T(8,128)(2,1)} %bitcast.13), kind=kLoop, calls=%fused_computation.4 | loop fusion | flops 532480 | bytes 532480 | tf_op jit(solution)/shard_map/concatenate | solution.py:62
  7.5 11.2 %collective-permute-start.3 = (bf16[1040,128]{1,0:T(8,128)(2,1)S(1)}, bf16[1040,128]{1,0:T(8,128)(2,1)S(1)}, u32[]{:S(2)}, u32[]{:S(2)}) collective-permute-start(bf16[1040,128]{1,0:T(8,128)(2,1)S(1)} %pad_maximum_fusion.4.zp), channel_id=1, source_target_pairs={{0,32},{1,225},{2,34},{3,226},{4,36},{5,228},{6,38},{7,230},{8,40}... | collective-permute-start | bytes 798728 | tf_op jit(solution)/shard_map/ppermute | solution.py:48
  18.7 0.0 collective-permute-done.h1
  18.8 4.8 %collective-permute-start.1 = (bf16[2080,128]{1,0:T(8,128)(2,1)S(1)}, bf16[2080,128]{1,0:T(8,128)(2,1)S(1)}, u32[]{:S(2)}, u32[]{:S(2)}) collective-permute-start(bf16[2080,128]{1,0:T(8,128)(2,1)S(1)} %pad_maximum_fusion.1), channel_id=1, source_target_pairs={{0,4},{1,28},{2,6},{3,30},{4,0},{5,9},{6,2},{7,11},{8,12},{9,5},{1... | collective-permute-start | bytes 1597448 | tf_op jit(solution)/shard_map/ppermute | solution.py:52
  23.6 0.0 collective-permute-done.3.z1
  23.7 0.0 copy-start
  23.7 1.9 %collective-permute-start.4 = (bf16[2080,128]{1,0:T(8,128)(2,1)S(1)}, bf16[2080,128]{1,0:T(8,128)(2,1)S(1)}, u32[]{:S(2)}, u32[]{:S(2)}) collective-permute-start(bf16[2080,128]{1,0:T(8,128)(2,1)S(1)} %pad_maximum_fusion.2), channel_id=1, source_target_pairs={{0,224},{1,33},{2,227},{3,35},{4,229},{5,37},{6,231},{7,39},{8,233... | collective-permute-start | bytes 1597448 | tf_op jit(solution)/shard_map/ppermute | solution.py:48
  25.6 5.3 %collective-permute-done.1.h2 = bf16[2080,128]{1,0:T(8,128)(2,1)S(1)} collective-permute-done((bf16[2080,128]{1,0:T(8,128)(2,1)S(1)}, bf16[2080,128]{1,0:T(8,128)(2,1)S(1)}, u32[]{:S(2)}, u32[]{:S(2)}) %collective-permute-start.1) | collective-permute-done | bytes 532512 | tf_op jit(solution)/shard_map/ppermute | solution.py:52
  30.9 0.1 pad_maximum_fusion
  31.0 1.9 %collective-permute-start.2 = (bf16[4160,128]{1,0:T(8,128)(2,1)S(1)}, bf16[4160,128]{1,0:T(8,128)(2,1)S(1)}, u32[]{:S(2)}, u32[]{:S(2)}) collective-permute-start(bf16[4160,128]{1,0:T(8,128)(2,1)S(1)} %pad_maximum_fusion), channel_id=1, source_target_pairs={{0,29},{1,5},{2,31},{3,7},{4,8},{5,1},{6,10},{7,3},{8,4},{9,13},{1... | collective-permute-start | bytes 3194888 | tf_op jit(solution)/shard_map/ppermute | solution.py:52
  32.9 1.1 %collective-permute-done.4.z2 = bf16[2080,128]{1,0:T(8,128)(2,1)S(1)} collective-permute-done((bf16[2080,128]{1,0:T(8,128)(2,1)S(1)}, bf16[2080,128]{1,0:T(8,128)(2,1)S(1)}, u32[]{:S(2)}, u32[]{:S(2)}) %collective-permute-start.4) | collective-permute-done | bytes 532512 | tf_op jit(solution)/shard_map/ppermute | solution.py:48
  34.0 4.4 %collective-permute-start.5 = (bf16[2080,128]{1,0:T(8,128)(2,1)S(1)}, bf16[2080,128]{1,0:T(8,128)(2,1)S(1)}, u32[]{:S(2)}, u32[]{:S(2)}) collective-permute-start(bf16[2080,128]{1,0:T(8,128)(2,1)S(1)} %collective-permute-done.4.z2), channel_id=1, source_target_pairs={{0,32},{1,225},{2,34},{3,226},{4,36},{5,228},{6,38},{7,230},{8,40}... | collective-permute-start | bytes 1597448 | tf_op jit(solution)/shard_map/ppermute | solution.py:48
  38.4 7.0 %collective-permute-done.5.z3 = bf16[2080,128]{1,0:T(8,128)(2,1)S(1)} collective-permute-done((bf16[2080,128]{1,0:T(8,128)(2,1)S(1)}, bf16[2080,128]{1,0:T(8,128)(2,1)S(1)}, u32[]{:S(2)}, u32[]{:S(2)}) %collective-permute-start.5) | collective-permute-done | bytes 532512 | tf_op jit(solution)/shard_map/ppermute | solution.py:48
  45.4 1.9 %collective-permute-start.6 = (bf16[2080,128]{1,0:T(8,128)(2,1)S(1)}, bf16[2080,128]{1,0:T(8,128)(2,1)S(1)}, u32[]{:S(2)}, u32[]{:S(2)}) collective-permute-start(bf16[2080,128]{1,0:T(8,128)(2,1)S(1)} %collective-permute-done.5.z3), channel_id=1, source_target_pairs={{0,224},{1,33},{2,227},{3,35},{4,229},{5,37},{6,231},{7,39},{8,233... | collective-permute-start | bytes 1597448 | tf_op jit(solution)/shard_map/ppermute | solution.py:48
  47.3 0.0 collective-permute-done.2.h3
  47.3 8.4 %collective-permute-done.6.z4 = bf16[2080,128]{1,0:T(8,128)(2,1)S(1)} collective-permute-done((bf16[2080,128]{1,0:T(8,128)(2,1)S(1)}, bf16[2080,128]{1,0:T(8,128)(2,1)S(1)}, u32[]{:S(2)}, u32[]{:S(2)}) %collective-permute-start.6) | collective-permute-done | bytes 532512 | tf_op jit(solution)/shard_map/ppermute | solution.py:48
  55.7 4.6 %product.1 = (f32[4,128,128]{2,1,0:T(8,128)S(1)}, f32[4,128,128]{2,1,0:T(8,128)S(1)}) custom-call(s32[2,8]{1,0:T(2,128)S(1)} %bitcast.9, bf16[1040,128]{1,0:T(8,128)(2,1)S(1)} %pad_maximum_fusion.3.hp, bf16[1040,128]{1,0:T(8,128)(2,1)S(1)} %collective-permute-done.h1, bf16[2080,128]{1,0:T(8,128)(2,1)S(1)} %collective-permute-done.1.h2, ...), custom_call_target="tpu_custom_call" | custom-call | flops 2147483648 | bytes 5242880 | tf_op jit(solution)/shard_map/product/pallas_call | solution.py:151
  60.3 5.6 %collective-permute-start.7 = (f32[4,128,128]{2,1,0:T(8,128)S(1)}, f32[4,128,128]{2,1,0:T(8,128)S(1)}, u32[]{:S(2)}, u32[]{:S(2)}) collective-permute-start(f32[4,128,128]{2,1,0:T(8,128)S(1)} %get-tuple-element.8), channel_id=1, source_target_pairs={{0,1},{1,0},{2,3},{3,2},{4,5},{5,4},{6,7},{7,6},{8,9},{9,8},{10,11... | collective-permute-start | bytes 786440 | tf_op jit(solution)/shard_map/ppermute | solution.py:183
  65.9 1.1 %collective-permute-done.7 = f32[4,128,128]{2,1,0:T(8,128)S(1)} collective-permute-done((f32[4,128,128]{2,1,0:T(8,128)S(1)}, f32[4,128,128]{2,1,0:T(8,128)S(1)}, u32[]{:S(2)}, u32[]{:S(2)}) %collective-permute-start.7) | collective-permute-done | bytes 262176 | tf_op jit(solution)/shard_map/ppermute | solution.py:183
  67.1 0.7 %add_bitcast_fusion = f32[1,1,4,128,128]{4,3,2,1,0:T(8,128)} fusion(f32[4,128,128]{2,1,0:T(8,128)S(1)} %get-tuple-element.7, f32[4,128,128]{2,1,0:T(8,128)S(1)} %collective-permute-done.7), kind=kLoop, calls=%fused_computation.5 | loop fusion | flops 65536 | bytes 786432 | tf_op jit(solution)/shard_map/broadcast_in_dim | solution.py:184
  (9 shorter events, 0.1 us)
Async XLA Ops:
  0.0 18.7 %copy-start.1 = (bf16[1,1,8,128,128]{4,3,2,1,0:T(8,128)(2,1)S(1)}, bf16[1,1,8,128,128]{4,3,2,1,0:T(8,128)(2,1)}, u32[]{:S(2)}) copy-start(bf16[1,1,8,128,128]{4,3,2,1,0:T(8,128)(2,1)} %param.5) | copy-start | bytes 786436
  0.8 22.9 %copy-start.2 = (bf16[1,1,8,128,128]{4,3,2,1,0:T(8,128)(2,1)S(1)}, bf16[1,1,8,128,128]{4,3,2,1,0:T(8,128)(2,1)}, u32[]{:S(2)}) copy-start(bf16[1,1,8,128,128]{4,3,2,1,0:T(8,128)(2,1)} %param.7) | copy-start | bytes 786436
  1.8 16.9 %collective-permute-start = (bf16[1040,128]{1,0:T(8,128)(2,1)S(1)}, bf16[1040,128]{1,0:T(8,128)(2,1)S(1)}, u32[]{:S(2)}, u32[]{:S(2)}) collective-permute-start(bf16[1040,128]{1,0:T(8,128)(2,1)S(1)} %pad_maximum_fusion.3.hp), channel_id=1, source_target_pairs={{0,2},{1,3},{2,0},{3,1},{4,6},{5,7},{6,4},{7,5},{8,10},{9,11},{10,... | collective-permute-start | bytes 798728 | tf_op jit(solution)/shard_map/ppermute | solution.py:56
  7.5 16.1 %collective-permute-start.3 = (bf16[1040,128]{1,0:T(8,128)(2,1)S(1)}, bf16[1040,128]{1,0:T(8,128)(2,1)S(1)}, u32[]{:S(2)}, u32[]{:S(2)}) collective-permute-start(bf16[1040,128]{1,0:T(8,128)(2,1)S(1)} %pad_maximum_fusion.4.zp), channel_id=1, source_target_pairs={{0,32},{1,225},{2,34},{3,226},{4,36},{5,228},{6,38},{7,230},{8,40}... | collective-permute-start | bytes 798728 | tf_op jit(solution)/shard_map/ppermute | solution.py:48
  18.8 12.1 %collective-permute-start.1 = (bf16[2080,128]{1,0:T(8,128)(2,1)S(1)}, bf16[2080,128]{1,0:T(8,128)(2,1)S(1)}, u32[]{:S(2)}, u32[]{:S(2)}) collective-permute-start(bf16[2080,128]{1,0:T(8,128)(2,1)S(1)} %pad_maximum_fusion.1), channel_id=1, source_target_pairs={{0,4},{1,28},{2,6},{3,30},{4,0},{5,9},{6,2},{7,11},{8,12},{9,5},{1... | collective-permute-start | bytes 1597448 | tf_op jit(solution)/shard_map/ppermute | solution.py:52
  23.7 32.0 %copy-start = (s32[1,1,2,8]{3,2,1,0:T(2,128)S(1)}, s32[1,1,2,8]{3,2,1,0:T(2,128)}, u32[]{:S(2)}) copy-start(s32[1,1,2,8]{3,2,1,0:T(2,128)} %param.9) | copy-start | bytes 196
  23.7 10.3 %collective-permute-start.4 = (bf16[2080,128]{1,0:T(8,128)(2,1)S(1)}, bf16[2080,128]{1,0:T(8,128)(2,1)S(1)}, u32[]{:S(2)}, u32[]{:S(2)}) collective-permute-start(bf16[2080,128]{1,0:T(8,128)(2,1)S(1)} %pad_maximum_fusion.2), channel_id=1, source_target_pairs={{0,224},{1,33},{2,227},{3,35},{4,229},{5,37},{6,231},{7,39},{8,233... | collective-permute-start | bytes 1597448 | tf_op jit(solution)/shard_map/ppermute | solution.py:48
  31.0 16.3 %collective-permute-start.2 = (bf16[4160,128]{1,0:T(8,128)(2,1)S(1)}, bf16[4160,128]{1,0:T(8,128)(2,1)S(1)}, u32[]{:S(2)}, u32[]{:S(2)}) collective-permute-start(bf16[4160,128]{1,0:T(8,128)(2,1)S(1)} %pad_maximum_fusion), channel_id=1, source_target_pairs={{0,29},{1,5},{2,31},{3,7},{4,8},{5,1},{6,10},{7,3},{8,4},{9,13},{1... | collective-permute-start | bytes 3194888 | tf_op jit(solution)/shard_map/ppermute | solution.py:52
  34.0 11.4 %collective-permute-start.5 = (bf16[2080,128]{1,0:T(8,128)(2,1)S(1)}, bf16[2080,128]{1,0:T(8,128)(2,1)S(1)}, u32[]{:S(2)}, u32[]{:S(2)}) collective-permute-start(bf16[2080,128]{1,0:T(8,128)(2,1)S(1)} %collective-permute-done.4.z2), channel_id=1, source_target_pairs={{0,32},{1,225},{2,34},{3,226},{4,36},{5,228},{6,38},{7,230},{8,40}... | collective-permute-start | bytes 1597448 | tf_op jit(solution)/shard_map/ppermute | solution.py:48
  45.4 10.3 %collective-permute-start.6 = (bf16[2080,128]{1,0:T(8,128)(2,1)S(1)}, bf16[2080,128]{1,0:T(8,128)(2,1)S(1)}, u32[]{:S(2)}, u32[]{:S(2)}) collective-permute-start(bf16[2080,128]{1,0:T(8,128)(2,1)S(1)} %collective-permute-done.5.z3), channel_id=1, source_target_pairs={{0,224},{1,33},{2,227},{3,35},{4,229},{5,37},{6,231},{7,39},{8,233... | collective-permute-start | bytes 1597448 | tf_op jit(solution)/shard_map/ppermute | solution.py:48
  60.3 6.7 %collective-permute-start.7 = (f32[4,128,128]{2,1,0:T(8,128)S(1)}, f32[4,128,128]{2,1,0:T(8,128)S(1)}, u32[]{:S(2)}, u32[]{:S(2)}) collective-permute-start(f32[4,128,128]{2,1,0:T(8,128)S(1)} %get-tuple-element.8), channel_id=1, source_target_pairs={{0,1},{1,0},{2,3},{3,2},{4,5},{5,4},{6,7},{7,6},{8,9},{9,8},{10,11... | collective-permute-start | bytes 786440 | tf_op jit(solution)/shard_map/ppermute | solution.py:183

commit v2 on v1

v2 whole, which is shorter than its diff:
```python
import functools

import jax
import jax.numpy as jnp
from jax import lax
from jax.experimental import pallas as pl
from jax.experimental.pallas import tpu as pltpu
from jax.sharding import PartitionSpec as P

TILE = 4
NNZ = 8
WIDTH = 128
GRID = 16
HALF = 8
SPAN = TILE * WIDTH
ROWS = NNZ * WIDTH + 16
BOTH = ("row", "col")


def even_pair(n):
    return n ^ 1


def odd_pair(n):
    return ((n - 1) ^ 1) + 1


def flat_id(i, c, role):
    layer = role ^ int((i + c) % GRID >= HALF)
    return i * 2 * GRID + c * 2 + layer


def route(step):
    pairs = []
    for i in range(GRID):
        for c in range(GRID):
            for role in range(2):
                z, y, x = step(i % HALF, c // 2, c % 2, role)
                pairs.append((flat_id(i, c, role), flat_id(i // HALF * HALF + z % HALF, (y % HALF) * 2 + x, role)))
    return pairs


def pair_of(kind, n, role):
    return even_pair(n) if kind == role else odd_pair(n)


def exchange_z(x, kind):
    return lax.ppermute(x, BOTH, route(lambda z, y, xl, r: (pair_of(kind, z, r), y, xl)))


def exchange_y(x, kind):
    return lax.ppermute(x, BOTH, route(lambda z, y, xl, r: (z, pair_of(kind, y, r), xl)))


def exchange_x(x):
    return lax.ppermute(x, BOTH, route(lambda z, y, xl, r: (z, y, xl ^ 1)))


def pack_kernel(places_z, places_h, blocks_z, blocks_h, out_z, out_h, tail, sem):
    lane = lax.broadcasted_iota(jnp.int32, tail.shape[1:], 1)
    copies = []
    for n, (blocks, out) in enumerate(((blocks_z, out_z), (blocks_h, out_h))):
        copies.append(pltpu.make_async_copy(blocks, out.at[pl.ds(0, NNZ * WIDTH)], sem.at[n]))
        copies[-1].start()
    for n, (places, out) in enumerate(((places_z, out_z), (places_h, out_h))):
        slots = jnp.zeros(lane.shape, jnp.int32)
        for k in range(NNZ):
            slots = jnp.where(lane == k, places[0, k] * TILE + places[1, k], slots)
        tail[n] = slots.astype(jnp.float32).astype(tail.dtype)
        copies.append(
            pltpu.make_async_copy(
                tail.at[n], out.at[pl.ds(NNZ * WIDTH, ROWS - NNZ * WIDTH)], sem.at[2 + n]
            )
        )
        copies[-1].start()
    for copy in copies:
        copy.wait()


def pack(places_z, places_h, blocks_z, blocks_h):
    smem = pl.BlockSpec(memory_space=pltpu.SMEM)
    hbm = pl.BlockSpec(memory_space=pl.ANY)
    return pl.pallas_call(
        pack_kernel,
        out_shape=(jax.ShapeDtypeStruct((ROWS, WIDTH), blocks_z.dtype),) * 2,
        in_specs=[smem, smem, hbm, hbm],
        out_specs=(hbm, hbm),
        scratch_shapes=[
            pltpu.VMEM((2, ROWS - NNZ * WIDTH, WIDTH), blocks_z.dtype),
            pltpu.SemaphoreType.DMA((4,)),
        ],
        cost_estimate=pl.CostEstimate(flops=0, bytes_accessed=ROWS * WIDTH * 8, transcendentals=0),
        name="pack",
    )(places_z, places_h, blocks_z.reshape(NNZ * WIDTH, WIDTH), blocks_h.reshape(NNZ * WIDTH, WIDTH))


def near(n, kind, role):
    even = n ^ 1
    odd = ((n - 1) ^ 1) + 1
    return jnp.where(role == kind, even, odd) & 7


def position():
    i = lax.axis_index("row")
    j = lax.axis_index("col")
    c = j >> 1
    layer = j & 1
    role = layer ^ (((i + c) & 15) >> 3)
    return i & 7, c >> 1, c & 1, layer, role


def arrival_order():
    z, y, xl, _, role = position()
    ya = near(y, 0, role)
    yb = near(y, 1, role)
    yab = near(yb, 0, role)
    up = near(z, 0, role) - z

    def place(yy, xx):
        ahead = (2 * yy + xx - 2 * y - xl) & 7
        ahead = jnp.where((up & 7) == 1, ahead, -ahead) & 7
        return (0x23675410 >> (4 * ahead)) & 7

    return [place(yy, xx) for yy in (y, ya, yb, yab) for xx in (xl, xl ^ 1)]


def read_slots(parts, idx_v, idx_s, sem):
    for n, (buf, part) in enumerate(parts):
        base = part * ROWS + NNZ * WIDTH
        idx_v[n : n + 1, :] = buf[base : base + 16, :].astype(jnp.float32).astype(jnp.int32)[0:1]
    copy = pltpu.make_async_copy(idx_v, idx_s, sem)
    copy.start()
    return copy


def place_h(dense, late, buf, part, slots, n, turn):
    for k in range(NNZ):
        r = pl.ds(pl.multiple_of((slots[n, k] >> 2) * WIDTH, WIDTH), WIDTH)
        q = (slots[n, k] & 3) * WIDTH
        at = part * ROWS + k * WIDTH

        @pl.when(turn < EARLY)
        def _():
            dense[r, pl.ds(pl.multiple_of(turn * SPAN + q, WIDTH), WIDTH)] = buf[at : at + WIDTH, :]

        @pl.when(turn >= EARLY)
        def _():
            late[r, pl.ds(pl.multiple_of((turn - EARLY) * SPAN + q, WIDTH), WIDTH)] = buf[at : at + WIDTH, :]


def place_z(dense, buf, part, slots, n, turn):
    for k in range(NNZ):
        r = turn * SPAN + (slots[n, k] >> 2) * WIDTH
        q = (slots[n, k] & 3) * WIDTH
        at = part * ROWS + k * WIDTH
        dense[pl.ds(pl.multiple_of(r, WIDTH), WIDTH), pl.ds(pl.multiple_of(q, WIDTH), WIDTH)] = buf[at : at + WIDTH, :]


EARLY = 6
LATE = HALF - EARLY


def early_kernel(hp, h1, h2, h3, h4, zp, z1, z2, z3, acc, late, hd, zd, idx_v, idx_s, sem):
    h_parts = [(hp, 0), (h1, 0), (h2, 0), (h2, 1), (h3, 0), (h3, 1), (h4, 0), (h4, 1)]
    z_parts = [(zp, 0), (z1, 0), (z2, 0), (z2, 1), (z3, 0), (z3, 1)]
    copy = read_slots(h_parts + z_parts, idx_v, idx_s, sem)

    late[...] = jnp.zeros_like(late)

    @pl.loop(0, EARLY)
    def _(u):
        at = pl.multiple_of(u * SPAN, SPAN)
        hd[:, pl.ds(at, SPAN)] = jnp.zeros((SPAN, SPAN), hd.dtype)
        zd[pl.ds(at, SPAN), :] = jnp.zeros((SPAN, SPAN), zd.dtype)

    turns = arrival_order()
    copy.wait()
    for n, (buf, part) in enumerate(h_parts):
        place_h(hd, late, buf, part, idx_s, n, turns[n])
    for n, (buf, part) in enumerate(z_parts):
        place_z(zd, buf, part, idx_s, HALF + n, n)
    for m in range(0, SPAN, 256):
        acc[m : m + 256, :] = jnp.dot(
            hd[m : m + 256, :], zd[...], preferred_element_type=jnp.float32
        )


def late_kernel(keep, hd, acc, z4, own, other, zd, total, idx_v, idx_s, sem):
    parts = [(z4, 0), (z4, 1)]
    copy = read_slots(parts, idx_v, idx_s, sem)
    zd[...] = jnp.zeros_like(zd)
    layer = lax.axis_index("col") & 1
    copy.wait()
    for n, (buf, part) in enumerate(parts):
        place_z(zd, buf, part, idx_s, n, n)
    for m in range(0, SPAN, 256):
        total[m : m + 256, :] = acc[m : m + 256, :] + jnp.dot(
            hd[m : m + 256, :], zd[...], preferred_element_type=jnp.float32
        )
    for q in range(TILE):
        for dst, first in ((own, layer * TILE), (other, (1 - layer) * TILE)):
            r = pl.multiple_of(keep[0, first + q] * WIDTH, WIDTH)
            s = pl.multiple_of(keep[1, first + q] * WIDTH, WIDTH)
            dst[q] = total[pl.ds(r, WIDTH), pl.ds(s, WIDTH)]


def slot_scratch(rows):
    return [
        pltpu.VMEM((rows, WIDTH), jnp.int32),
        pltpu.SMEM((rows, WIDTH), jnp.int32),
        pltpu.SemaphoreType.DMA,
    ]


def early_product(*tiles):
    vmem = pl.BlockSpec(memory_space=pltpu.VMEM)
    return pl.pallas_call(
        early_kernel,
        out_shape=(
            jax.ShapeDtypeStruct((SPAN, SPAN), jnp.float32),
            jax.ShapeDtypeStruct((SPAN, LATE * SPAN), jnp.bfloat16),
        ),
        in_specs=[vmem] * len(tiles),
        out_specs=(vmem, vmem),
        scratch_shapes=[
            pltpu.VMEM((SPAN, EARLY * SPAN), jnp.bfloat16),
            pltpu.VMEM((EARLY * SPAN, SPAN), jnp.bfloat16),
        ]
        + slot_scratch(GRID),
        compiler_params=pltpu.CompilerParams(vmem_limit_bytes=12 * 1024 * 1024),
        cost_estimate=pl.CostEstimate(
            flops=2 * SPAN * SPAN * SPAN * EARLY, bytes_accessed=5 * 1024 * 1024, transcendentals=0
        ),
        name="early",
    )(*tiles)


def late_product(keep, hd, acc, z4):
    vmem = pl.BlockSpec(memory_space=pltpu.VMEM)
    half = jax.ShapeDtypeStruct((TILE, WIDTH, WIDTH), jnp.float32)
    return pl.pallas_call(
        late_kernel,
        out_shape=(half, half),
        in_specs=[pl.BlockSpec(memory_space=pltpu.SMEM), vmem, vmem, vmem],
        out_specs=(vmem, vmem),
        scratch_shapes=[
            pltpu.VMEM((LATE * SPAN, SPAN), jnp.bfloat16),
            pltpu.VMEM((SPAN, SPAN), jnp.float32),
        ]
        + slot_scratch(8),
        compiler_params=pltpu.CompilerParams(vmem_limit_bytes=4 * 1024 * 1024),
        cost_estimate=pl.CostEstimate(
            flops=2 * SPAN * SPAN * SPAN * LATE, bytes_accessed=2 * 1024 * 1024, transcendentals=0
        ),
        name="late",
    )(keep, hd, acc, z4)


def per_device(h_blocks, h_index, z_blocks, z_index, keep_index):
    zp, hp = pack(z_index[0, 0], h_index[0, 0], z_blocks[0, 0], h_blocks[0, 0])
    z1 = exchange_z(zp, 0)
    h1 = exchange_x(hp)
    z2 = exchange_z(jnp.concatenate([zp, z1], axis=0), 1)
    h01 = jnp.concatenate([hp, h1], axis=0)
    h2 = exchange_y(h01, 0)
    h3 = exchange_y(h01, 1)
    z3 = exchange_z(z2, 0)
    h4 = exchange_y(h2, 1)
    z4 = exchange_z(z3, 1)
    acc, hd = early_product(hp, h1, h2, h3, h4, zp, z1, z2, z3)
    own, other = late_product(keep_index[0, 0], hd, acc, z4)
    both = lax.all_gather(
        other, "col", axis_index_groups=[[2 * c, 2 * c + 1] for c in range(GRID)], tiled=False
    )
    partner = lax.dynamic_index_in_dim(both, 1 - (lax.axis_index("col") & 1), 0, keepdims=False)
    return (own + partner)[None, None]


def solution(mesh):
    return jax.shard_map(
        per_device,
        mesh=mesh,
        in_specs=(
            P("row", "col", None, None, None),
            P("row", "col", None, None),
            P("row", "col", None, None, None),
            P("row", "col", None, None),
            P("row", "col", None, None),
        ),
        out_specs=P("row", "col", None, None, None),
        check_vma=False,
    )
```

time: 68.2 us -> 78.6 us (1.15); the launches traced: 67.8 us -> 77.3 us
  Pallas kernels: 4.65 us -> 24.8 us
  waiting for transfers between devices: 22.9 us -> 10.1 us
  other arithmetic: 4.38 us -> 1.72 us
  blocking collectives: 0 us -> 2.18 us
  local copies, waits for them, and re-layouts: 0.03 us -> 1.48 us
  starting transfers between devices: 35.7 us -> 36.9 us
    pallas_call x1 -> x3, Pallas kernels: 4.65 us -> 24.8 us  [the longest x1 17.7 us: pack(): pl.pallas_call(pack_kernel, out_shape=(jax.ShapeDtypeStruct((ROWS, WIDTH)...]
    ppermute x4, waiting for transfers between devices: 16.5 us -> 0.72 us  [exchange_z(): lax.ppermute(x, BOTH, route(lambda z, y, xl, r: (pair_of(kind, z, r), y,...]
    ppermute x2 -> x3, starting transfers between devices: 6.74 us -> 13 us  [exchange_y(): lax.ppermute(x, BOTH, route(lambda z, y, xl, r: (z, pair_of(kind, y, r),...]
    ppermute x1 -> x0, starting transfers between devices: 5.58 us -> none  [per_device(): partner = lax.ppermute(other, 'col', [(j, j ^ 1) for j in range(2 * GRID)])]
    ppermute x2 -> x3, waiting for transfers between devices: 5.27 us -> 8.96 us  [exchange_y(): lax.ppermute(x, BOTH, route(lambda z, y, xl, r: (z, pair_of(kind, y, r),...]
    all_gather x0 -> x1, blocking collectives: none -> 2.18 us  [per_device(): lax.all_gather(other, 'col', axis_index_groups=[[2 * c, 2 * c + 1] for c...]
    concatenate x4 -> x0, other arithmetic: 2.09 us -> none  [the longest x2 1.98 us: with_slots(): return jnp.concatenate([blocks.reshape(NNZ * WIDTH, WIDTH), tail], axis=0)]
    convert_element_type x2 -> x0, other arithmetic: 1.52 us -> none  [with_slots(): slots = (places[0] * TILE + places[1]).astype(blocks.dtype)]
  transfers between devices with their start and end apart: 8 -> 8, of which waited for: 5 -> 5; matrix products, arithmetic and copies ran while one was open for 3% -> 3% of each run, Pallas kernels for 0% -> 6%
where the time goes in v2:
time: 78.6 us; the launch traced here: 77.3 us
  starting transfers between devices  36.9 us (47%)
  Pallas kernels  24.8 us (32%)
  waiting for transfers between devices  10.1 us (13%)
  blocking collectives  2.18 us (3%)
  other arithmetic  1.72 us (2%)
  local copies, waits for them, and re-layouts  1.48 us (2%)
    ppermute x4, starting transfers between devices, exchange_z(): lax.ppermute(x, BOTH, route(lambda z, y, xl, r: (pair_of(kind, z, r), y,...  20 us
    pallas_call x1, Pallas kernels, pack(): pl.pallas_call(pack_kernel, out_shape=(jax.ShapeDtypeStruct((ROWS, WIDTH)...  17.7 us
    ppermute x3, starting transfers between devices, exchange_y(): lax.ppermute(x, BOTH, route(lambda z, y, xl, r: (z, pair_of(kind, y, r),...  13 us
    ppermute x3, waiting for transfers between devices, exchange_y(): lax.ppermute(x, BOTH, route(lambda z, y, xl, r: (z, pair_of(kind, y, r),...  8.96 us
    pallas_call x1, Pallas kernels, early_product(): pl.pallas_call(early_kernel, out_shape=(jax.ShapeDtypeStruct((SPAN, SPAN)...  4.94 us
    ppermute x1, starting transfers between devices, exchange_x(): return lax.ppermute(x, BOTH, route(lambda z, y, xl, r: (z, y, xl ^ 1)))  3.81 us
    all_gather x1, blocking collectives, per_device(): lax.all_gather(other, 'col', axis_index_groups=[[2 * c, 2 * c + 1] for c...  2.18 us
    pallas_call x1, Pallas kernels, late_product(): pl.pallas_call(late_kernel, out_shape=(half, half), in_specs=[pl.BlockSpe...  2.11 us
  transfers between devices with their start and end apart: 8, of which 5 were waited for; matrix products, arithmetic and copies ran while one was open for 3% of the time, Pallas kernels for 6%

profile of v2, /device:TPU:1, one launch (start us, length us, event | category | flops | bytes accessed | tf_op | source)
XLA Modules:
  0.0 77.3 jit_solution(3189516827561282207)
XLA Ops:
  0.0 17.7 %pack.1 = (bf16[1040,128]{1,0:T(8,128)(2,1)}, bf16[1040,128]{1,0:T(8,128)(2,1)}) custom-call(s32[2,8]{1,0:T(2,128)} %bitcast.16, s32[2,8]{1,0:T(2,128)} %bitcast.17, bf16[1024,128]{1,0:T(8,128)(2,1)} %bitcast.14, bf16[1024,128]{1,0:T(8,128)(2,1)} %bitcast.15), custom_call_target="tpu_custom_call" | custom-call | bytes 1064960 | tf_op jit(solution)/shard_map/pack/pallas_call | solution.py:83
  17.7 11.6 %collective-permute-start.4 = (bf16[1040,128]{1,0:T(8,128)(2,1)}, bf16[1040,128]{1,0:T(8,128)(2,1)S(1)}, u32[]{:S(2)}, u32[]{:S(2)}) collective-permute-start(bf16[1040,128]{1,0:T(8,128)(2,1)} %get-tuple-element.12.zp), channel_id=1, source_target_pairs={{0,32},{1,225},{2,34},{3,226},{4,36},{5,228},{6,38},{7,230},{8,40}... | collective-permute-start | bytes 798728 | tf_op jit(solution)/shard_map/ppermute | solution.py:48
  29.4 3.8 %collective-permute-start = (bf16[1040,128]{1,0:T(8,128)(2,1)}, bf16[1040,128]{1,0:T(8,128)(2,1)S(1)}, u32[]{:S(2)}, u32[]{:S(2)}) collective-permute-start(bf16[1040,128]{1,0:T(8,128)(2,1)} %get-tuple-element.11.hp), channel_id=1, source_target_pairs={{0,2},{1,3},{2,0},{3,1},{4,6},{5,7},{6,4},{7,5},{8,10},{9,11},{10,... | collective-permute-start | bytes 798728 | tf_op jit(solution)/shard_map/ppermute | solution.py:56
  33.2 0.2 collective-permute-done.4.z1
  33.4 1.0 %pad_maximum_fusion = bf16[2080,128]{1,0:T(8,128)(2,1)S(1)} fusion(bf16[1040,128]{1,0:T(8,128)(2,1)S(1)} %collective-permute-done.4.z1, bf16[1040,128]{1,0:T(8,128)(2,1)} %get-tuple-element.12.zp), kind=kLoop, calls=%fused_computation | loop fusion | flops 1064960 | bytes 1064960 | tf_op jit(solution)/shard_map/concatenate | solution.py:263
  34.4 1.9 %collective-permute-start.5 = (bf16[2080,128]{1,0:T(8,128)(2,1)S(1)}, bf16[2080,128]{1,0:T(8,128)(2,1)S(1)}, u32[]{:S(2)}, u32[]{:S(2)}) collective-permute-start(bf16[2080,128]{1,0:T(8,128)(2,1)S(1)} %pad_maximum_fusion), channel_id=1, source_target_pairs={{0,224},{1,33},{2,227},{3,35},{4,229},{5,37},{6,231},{7,39},{8,233... | collective-permute-start | bytes 1597448 | tf_op jit(solution)/shard_map/ppermute | solution.py:48
  36.3 0.7 constant_dynamic-update-slice_fusion.1
  37.0 0.5 collective-permute-done.h1
  37.5 0.7 constant_dynamic-update-slice_fusion
  38.2 5.9 %collective-permute-start.1 = (bf16[2080,128]{1,0:T(8,128)(2,1)}, bf16[2080,128]{1,0:T(8,128)(2,1)S(1)}, u32[]{:S(2)}, u32[]{:S(2)}) collective-permute-start(bf16[2080,128]{1,0:T(8,128)(2,1)} %constant_dynamic-update-slice_fusion), channel_id=1, source_target_pairs={{0,4},{1,28},{2,6},{3,30},{4,0},{5,9},{6,2},{7,11},{8,12},{9,5},{1... | collective-permute-start | bytes 1597448 | tf_op jit(solution)/shard_map/ppermute | solution.py:52
  44.1 0.5 collective-permute-done.5.z2
  44.7 4.6 %collective-permute-start.6 = (bf16[2080,128]{1,0:T(8,128)(2,1)S(1)}, bf16[2080,128]{1,0:T(8,128)(2,1)S(1)}, u32[]{:S(2)}, u32[]{:S(2)}) collective-permute-start(bf16[2080,128]{1,0:T(8,128)(2,1)S(1)} %collective-permute-done.5.z2), channel_id=1, source_target_pairs={{0,32},{1,225},{2,34},{3,226},{4,36},{5,228},{6,38},{7,230},{8,40}... | collective-permute-start | bytes 1597448 | tf_op jit(solution)/shard_map/ppermute | solution.py:48
  49.2 5.2 %collective-permute-start.2 = (bf16[2080,128]{1,0:T(8,128)(2,1)}, bf16[2080,128]{1,0:T(8,128)(2,1)}, u32[]{:S(2)}, u32[]{:S(2)}) collective-permute-start(bf16[2080,128]{1,0:T(8,128)(2,1)} %constant_dynamic-update-slice_fusion), channel_id=1, source_target_pairs={{0,29},{1,5},{2,31},{3,7},{4,8},{5,1},{6,10},{7,3},{8,4},{9,13},{1... | collective-permute-start | bytes 1597448 | tf_op jit(solution)/shard_map/ppermute | solution.py:52
  54.5 0.0 collective-permute-done.1.h2
  54.5 1.9 %collective-permute-start.3 = (bf16[2080,128]{1,0:T(8,128)(2,1)S(1)}, bf16[2080,128]{1,0:T(8,128)(2,1)}, u32[]{:S(2)}, u32[]{:S(2)}) collective-permute-start(bf16[2080,128]{1,0:T(8,128)(2,1)S(1)} %collective-permute-done.1.h2), channel_id=1, source_target_pairs={{0,29},{1,5},{2,31},{3,7},{4,8},{5,1},{6,10},{7,3},{8,4},{9,13},{1... | collective-permute-start | bytes 1597448 | tf_op jit(solution)/shard_map/ppermute | solution.py:52
  56.4 0.0 collective-permute-done.6.z3
  56.4 1.9 %collective-permute-start.7 = (bf16[2080,128]{1,0:T(8,128)(2,1)S(1)}, bf16[2080,128]{1,0:T(8,128)(2,1)S(1)}, u32[]{:S(2)}, u32[]{:S(2)}) collective-permute-start(bf16[2080,128]{1,0:T(8,128)(2,1)S(1)} %collective-permute-done.6.z3), channel_id=1, source_target_pairs={{0,224},{1,33},{2,227},{3,35},{4,229},{5,37},{6,231},{7,39},{8,233... | collective-permute-start | bytes 1597448 | tf_op jit(solution)/shard_map/ppermute | solution.py:48
  58.3 0.0 copy-start.2
  58.3 3.4 %collective-permute-done.2.h3 = bf16[2080,128]{1,0:T(8,128)(2,1)} collective-permute-done((bf16[2080,128]{1,0:T(8,128)(2,1)}, bf16[2080,128]{1,0:T(8,128)(2,1)}, u32[]{:S(2)}, u32[]{:S(2)}) %collective-permute-start.2) | collective-permute-done | bytes 532512 | tf_op jit(solution)/shard_map/ppermute | solution.py:52
  61.7 5.6 %collective-permute-done.3.h4 = bf16[2080,128]{1,0:T(8,128)(2,1)} collective-permute-done((bf16[2080,128]{1,0:T(8,128)(2,1)S(1)}, bf16[2080,128]{1,0:T(8,128)(2,1)}, u32[]{:S(2)}, u32[]{:S(2)}) %collective-permute-start.3) | collective-permute-done | bytes 532512 | tf_op jit(solution)/shard_map/ppermute | solution.py:52
  67.3 4.9 %early.1 = (f32[512,512]{1,0:T(8,128)S(1)}, bf16[512,1024]{1,0:T(8,128)(2,1)S(1)}) custom-call(bf16[1040,128]{1,0:T(8,128)(2,1)S(1)} %copy-done, bf16[1040,128]{1,0:T(8,128)(2,1)S(1)} %collective-permute-done.h1, bf16[2080,128]{1,0:T(8,128)(2,1)S(1)} %collective-permute-done.1.h2, bf16[2080,128]{1,0:T(8,128)(2,1)} %collective-permute-done.2.h3, ...), custom_call_target="tpu_custom_call" | custom-call | flops 1610612736 | bytes 5242880 | tf_op jit(solution)/shard_map/early/pallas_call | solution.py:217
  72.3 2.1 %late.1 = (f32[4,128,128]{2,1,0:T(8,128)S(1)}, f32[4,128,128]{2,1,0:T(8,128)S(1)}) custom-call(s32[2,8]{1,0:T(2,128)S(1)} %bitcast.12, bf16[512,1024]{1,0:T(8,128)(2,1)S(1)} %get-tuple-element.13.hd, f32[512,512]{1,0:T(8,128)S(1)} %get-tuple-element.14.acc, bf16[2080,128]{1,0:T(8,128)(2,1)S(1)} %collective-permute-done.7.z4), custom_call_target="tpu_custom_call" | custom-call | flops 536870912 | bytes 2097152 | tf_op jit(solution)/shard_map/late/pallas_call | solution.py:241
  74.4 2.2 %all-gather = f32[8,128,128]{2,1,0:T(8,128)S(1)} all-gather(f32[4,128,128]{2,1,0:T(8,128)S(1)} %get-tuple-element.16), channel_id=2, replica_groups={{0,1},{2,3},{4,5},{6,7},{8,9},{10,11},{12,13},{14,15},{16,17},{18,19},{..., dimensions={0}, use_global_device_ids=true | all-gather | bytes 786432 | tf_op jit(solution)/shard_map/all_gather | solution.py:272
  76.6 0.7 fusion
  (6 shorter events, 0.0 us)
Async XLA Ops:
  17.7 18.6 %copy-start = (bf16[1040,128]{1,0:T(8,128)(2,1)S(1)}, bf16[1040,128]{1,0:T(8,128)(2,1)}, u32[]{:S(2)}) copy-start(bf16[1040,128]{1,0:T(8,128)(2,1)} %get-tuple-element.11.hp) | copy-start | bytes 798724
  17.7 15.6 %collective-permute-start.4 = (bf16[1040,128]{1,0:T(8,128)(2,1)}, bf16[1040,128]{1,0:T(8,128)(2,1)S(1)}, u32[]{:S(2)}, u32[]{:S(2)}) collective-permute-start(bf16[1040,128]{1,0:T(8,128)(2,1)} %get-tuple-element.12.zp), channel_id=1, source_target_pairs={{0,32},{1,225},{2,34},{3,226},{4,36},{5,228},{6,38},{7,230},{8,40}... | collective-permute-start | bytes 798728 | tf_op jit(solution)/shard_map/ppermute | solution.py:48
  29.4 37.9 %copy-start.1 = (bf16[1040,128]{1,0:T(8,128)(2,1)S(1)}, bf16[1040,128]{1,0:T(8,128)(2,1)}, u32[]{:S(2)}) copy-start(bf16[1040,128]{1,0:T(8,128)(2,1)} %get-tuple-element.12.zp) | copy-start | bytes 798724
  29.4 8.1 %collective-permute-start = (bf16[1040,128]{1,0:T(8,128)(2,1)}, bf16[1040,128]{1,0:T(8,128)(2,1)S(1)}, u32[]{:S(2)}, u32[]{:S(2)}) collective-permute-start(bf16[1040,128]{1,0:T(8,128)(2,1)} %get-tuple-element.11.hp), channel_id=1, source_target_pairs={{0,2},{1,3},{2,0},{3,1},{4,6},{5,7},{6,4},{7,5},{8,10},{9,11},{10,... | collective-permute-start | bytes 798728 | tf_op jit(solution)/shard_map/ppermute | solution.py:56
  34.4 10.3 %collective-permute-start.5 = (bf16[2080,128]{1,0:T(8,128)(2,1)S(1)}, bf16[2080,128]{1,0:T(8,128)(2,1)S(1)}, u32[]{:S(2)}, u32[]{:S(2)}) collective-permute-start(bf16[2080,128]{1,0:T(8,128)(2,1)S(1)} %pad_maximum_fusion), channel_id=1, source_target_pairs={{0,224},{1,33},{2,227},{3,35},{4,229},{5,37},{6,231},{7,39},{8,233... | collective-permute-start | bytes 1597448 | tf_op jit(solution)/shard_map/ppermute | solution.py:48
  38.2 16.2 %collective-permute-start.1 = (bf16[2080,128]{1,0:T(8,128)(2,1)}, bf16[2080,128]{1,0:T(8,128)(2,1)S(1)}, u32[]{:S(2)}, u32[]{:S(2)}) collective-permute-start(bf16[2080,128]{1,0:T(8,128)(2,1)} %constant_dynamic-update-slice_fusion), channel_id=1, source_target_pairs={{0,4},{1,28},{2,6},{3,30},{4,0},{5,9},{6,2},{7,11},{8,12},{9,5},{1... | collective-permute-start | bytes 1597448 | tf_op jit(solution)/shard_map/ppermute | solution.py:52
  44.7 11.7 %collective-permute-start.6 = (bf16[2080,128]{1,0:T(8,128)(2,1)S(1)}, bf16[2080,128]{1,0:T(8,128)(2,1)S(1)}, u32[]{:S(2)}, u32[]{:S(2)}) collective-permute-start(bf16[2080,128]{1,0:T(8,128)(2,1)S(1)} %collective-permute-done.5.z2), channel_id=1, source_target_pairs={{0,32},{1,225},{2,34},{3,226},{4,36},{5,228},{6,38},{7,230},{8,40}... | collective-permute-start | bytes 1597448 | tf_op jit(solution)/shard_map/ppermute | solution.py:48
  49.2 12.5 %collective-permute-start.2 = (bf16[2080,128]{1,0:T(8,128)(2,1)}, bf16[2080,128]{1,0:T(8,128)(2,1)}, u32[]{:S(2)}, u32[]{:S(2)}) collective-permute-start(bf16[2080,128]{1,0:T(8,128)(2,1)} %constant_dynamic-update-slice_fusion), channel_id=1, source_target_pairs={{0,29},{1,5},{2,31},{3,7},{4,8},{5,1},{6,10},{7,3},{8,4},{9,13},{1... | collective-permute-start | bytes 1597448 | tf_op jit(solution)/shard_map/ppermute | solution.py:52
  54.5 12.8 %collective-permute-start.3 = (bf16[2080,128]{1,0:T(8,128)(2,1)S(1)}, bf16[2080,128]{1,0:T(8,128)(2,1)}, u32[]{:S(2)}, u32[]{:S(2)}) collective-permute-start(bf16[2080,128]{1,0:T(8,128)(2,1)S(1)} %collective-permute-done.1.h2), channel_id=1, source_target_pairs={{0,29},{1,5},{2,31},{3,7},{4,8},{5,1},{6,10},{7,3},{8,4},{9,13},{1... | collective-permute-start | bytes 1597448 | tf_op jit(solution)/shard_map/ppermute | solution.py:52
  56.4 15.9 %collective-permute-start.7 = (bf16[2080,128]{1,0:T(8,128)(2,1)S(1)}, bf16[2080,128]{1,0:T(8,128)(2,1)S(1)}, u32[]{:S(2)}, u32[]{:S(2)}) collective-permute-start(bf16[2080,128]{1,0:T(8,128)(2,1)S(1)} %collective-permute-done.6.z3), channel_id=1, source_target_pairs={{0,224},{1,33},{2,227},{3,35},{4,229},{5,37},{6,231},{7,39},{8,233... | collective-permute-start | bytes 1597448 | tf_op jit(solution)/shard_map/ppermute | solution.py:48
  58.3 13.9 %copy-start.2 = (s32[1,1,2,8]{3,2,1,0:T(2,128)S(1)}, s32[1,1,2,8]{3,2,1,0:T(2,128)}, u32[]{:S(2)}) copy-start(s32[1,1,2,8]{3,2,1,0:T(2,128)} %param.9) | copy-start | bytes 196

commit v3 on v2

v3 whole, which is shorter than its diff:
```python
import functools

import jax
import jax.numpy as jnp
from jax import lax
from jax.experimental import pallas as pl
from jax.experimental.pallas import tpu as pltpu
from jax.sharding import PartitionSpec as P

TILE = 4
NNZ = 8
WIDTH = 128
GRID = 16
HALF = 8
SPAN = TILE * WIDTH
ROWS = NNZ * WIDTH + 16
BOTH = ("row", "col")


def even_pair(n):
    return n ^ 1


def odd_pair(n):
    return ((n - 1) ^ 1) + 1


def flat_id(i, c, role):
    layer = role ^ int((i + c) % GRID >= HALF)
    return i * 2 * GRID + c * 2 + layer


def route(step):
    pairs = []
    for i in range(GRID):
        for c in range(GRID):
            for role in range(2):
                z, y, x = step(i % HALF, c // 2, c % 2, role)
                pairs.append((flat_id(i, c, role), flat_id(i // HALF * HALF + z % HALF, (y % HALF) * 2 + x, role)))
    return pairs


def pair_of(kind, n, role):
    return even_pair(n) if kind == role else odd_pair(n)


def exchange_z(x, kind):
    return lax.ppermute(x, BOTH, route(lambda z, y, xl, r: (pair_of(kind, z, r), y, xl)))


def exchange_y(x, kind):
    return lax.ppermute(x, BOTH, route(lambda z, y, xl, r: (z, pair_of(kind, y, r), xl)))


def exchange_x(x):
    return lax.ppermute(x, BOTH, route(lambda z, y, xl, r: (z, y, xl ^ 1)))


def pack_kernel(places_z, places_h, blocks_z, blocks_h, out_z, out_h, sem):
    lane = lax.broadcasted_iota(jnp.int32, (ROWS - NNZ * WIDTH, WIDTH), 1)
    copies = []
    for n, (blocks, out) in enumerate(((blocks_z, out_z), (blocks_h, out_h))):
        copies.append(pltpu.make_async_copy(blocks, out.at[pl.ds(0, NNZ * WIDTH)], sem.at[n]))
        copies[-1].start()
    for places, out in ((places_z, out_z), (places_h, out_h)):
        slots = jnp.zeros(lane.shape, jnp.int32)
        for k in range(NNZ):
            slots = jnp.where(lane == k, places[0, k] * TILE + places[1, k], slots)
        out[pl.ds(NNZ * WIDTH, ROWS - NNZ * WIDTH), :] = slots.astype(jnp.float32).astype(out.dtype)
    for copy in copies:
        copy.wait()


PACK_LIMIT = 56 * 1024 * 1024


def pack(places_z, places_h, blocks_z, blocks_h):
    smem = pl.BlockSpec(memory_space=pltpu.SMEM)
    hbm = pl.BlockSpec(memory_space=pl.ANY)
    vmem = pl.BlockSpec(memory_space=pltpu.VMEM)
    return pl.pallas_call(
        pack_kernel,
        out_shape=(jax.ShapeDtypeStruct((ROWS, WIDTH), blocks_z.dtype),) * 2,
        in_specs=[smem, smem, hbm, hbm],
        out_specs=(vmem, vmem),
        scratch_shapes=[pltpu.SemaphoreType.DMA((2,))],
        compiler_params=pltpu.CompilerParams(vmem_limit_bytes=PACK_LIMIT),
        cost_estimate=pl.CostEstimate(flops=0, bytes_accessed=ROWS * WIDTH * 8, transcendentals=0),
        name="pack",
    )(places_z, places_h, blocks_z.reshape(NNZ * WIDTH, WIDTH), blocks_h.reshape(NNZ * WIDTH, WIDTH))


def near(n, kind, role):
    even = n ^ 1
    odd = ((n - 1) ^ 1) + 1
    return jnp.where(role == kind, even, odd) & 7


def position():
    i = lax.axis_index("row")
    j = lax.axis_index("col")
    c = j >> 1
    layer = j & 1
    role = layer ^ (((i + c) & 15) >> 3)
    return i & 7, c >> 1, c & 1, layer, role


def offsets():
    z, y, xl, _, role = position()
    ya = near(y, 0, role)
    yb = near(y, 1, role)
    yab = near(yb, 0, role)
    up = near(z, 0, role) - z
    of_h = [(2 * (yy - y) + xx - xl) & 7 for yy in (y, ya, yb, yab) for xx in (xl, xl ^ 1)]
    of_z = [(up * n) & 7 for n in (0, 1, -1, -2, 2, 3, -3, 4)]
    return of_h, of_z


def read_slots(parts, idx_v, idx_s, sem):
    for n, (buf, part) in enumerate(parts):
        base = part * ROWS + NNZ * WIDTH
        idx_v[n : n + 1, :] = buf[base : base + 16, :].astype(jnp.float32).astype(jnp.int32)[0:1]
    copy = pltpu.make_async_copy(idx_v, idx_s, sem)
    copy.start()
    return copy


def place(buf, part, slots, n, put):
    for k in range(NNZ):
        row = pl.multiple_of((slots[n, k] >> 2) * WIDTH, WIDTH)
        col = pl.multiple_of((slots[n, k] & 3) * WIDTH, WIDTH)
        at = part * ROWS + k * WIDTH
        put(row, col, buf[at : at + WIDTH, :])


def into_h(dense, turn):
    def put(row, col, block):
        dense[pl.ds(row, WIDTH), pl.ds(pl.multiple_of(turn * SPAN + col, WIDTH), WIDTH)] = block

    return put


def into_z(dense, turn):
    def put(row, col, block):
        dense[pl.ds(pl.multiple_of(turn * SPAN + row, WIDTH), WIDTH), pl.ds(col, WIDTH)] = block

    return put


LATE = 3
EARLY = HALF - LATE


def early_turn(ahead):
    return jnp.where(ahead < 3, ahead, ahead - 3)


def early_kernel(hp, h1, h2, h3, zp, z1, z2, z3, acc, late_h, late_z, hd, zd, idx_v, idx_s, sem):
    h_parts = [(hp, 0), (h1, 0), (h2, 0), (h2, 1), (h3, 0), (h3, 1)]
    z_parts = [(zp, 0), (z1, 0), (z2, 0), (z2, 1), (z3, 0), (z3, 1)]
    copy = read_slots(h_parts + z_parts, idx_v, idx_s, sem)
    late_h[...] = jnp.zeros_like(late_h)
    late_z[...] = jnp.zeros_like(late_z)

    @pl.loop(0, EARLY)
    def _(u):
        at = pl.multiple_of(u * SPAN, SPAN)
        hd[:, pl.ds(at, SPAN)] = jnp.zeros((SPAN, SPAN), hd.dtype)
        zd[pl.ds(at, SPAN), :] = jnp.zeros((SPAN, SPAN), zd.dtype)

    of_h, of_z = offsets()
    copy.wait()
    for n, (buf, part) in enumerate(h_parts):
        ahead = of_h[n]
        if n in (3, 5):
            is_late = (ahead >= 3) & (ahead <= 5)

            @pl.when(is_late)
            def _():
                place(buf, part, idx_s, n, into_h(late_h, ahead - 3))

            @pl.when(jnp.logical_not(is_late))
            def _():
                place(buf, part, idx_s, n, into_h(hd, early_turn(ahead)))
        else:
            place(buf, part, idx_s, n, into_h(hd, early_turn(ahead)))
    for n, (buf, part) in enumerate(z_parts):
        if n == 5:
            put = into_z(late_z, of_z[n] - 3)
        else:
            put = into_z(zd, early_turn(of_z[n]))
        place(buf, part, idx_s, len(h_parts) + n, put)
    for m in range(0, SPAN, 256):
        acc[m : m + 256, :] = jnp.dot(hd[m : m + 256, :], zd[...], preferred_element_type=jnp.float32)


def middle_kernel(h4, late_h, out_h, idx_v, idx_s, sem):
    parts = [(h4, 0), (h4, 1)]
    copy = read_slots(parts, idx_v, idx_s, sem)
    of_h, _ = offsets()
    copy.wait()
    for n, (buf, part) in enumerate(parts):
        place(buf, part, idx_s, n, into_h(out_h, of_h[6 + n] - 3))


def late_kernel(keep, acc, hd, late_z, z4, own, other, zd, total, idx_v, idx_s, sem):
    parts = [(z4, 0), (z4, 1)]
    copy = read_slots(parts, idx_v, idx_s, sem)
    _, of_z = offsets()
    layer = lax.axis_index("col") & 1
    copy.wait()
    for n, (buf, part) in enumerate(parts):
        place(buf, part, idx_s, n, into_z(zd, of_z[6 + n] - 3))
    for m in range(0, SPAN, 256):
        total[m : m + 256, :] = acc[m : m + 256, :] + jnp.dot(
            hd[m : m + 256, :], zd[...], preferred_element_type=jnp.float32
        )
    for q in range(TILE):
        for dst, first in ((own, layer * TILE), (other, (1 - layer) * TILE)):
            r = pl.multiple_of(keep[0, first + q] * WIDTH, WIDTH)
            s = pl.multiple_of(keep[1, first + q] * WIDTH, WIDTH)
            dst[q] = total[pl.ds(r, WIDTH), pl.ds(s, WIDTH)]


def slot_scratch(rows):
    return [
        pltpu.VMEM((rows, WIDTH), jnp.int32),
        pltpu.SMEM((rows, WIDTH), jnp.int32),
        pltpu.SemaphoreType.DMA,
    ]


VMEM = pl.BlockSpec(memory_space=pltpu.VMEM)
MIDDLE_FLOPS = 2 * SPAN * SPAN * SPAN * 32
LATE_H = jax.ShapeDtypeStruct((SPAN, LATE * SPAN), jnp.bfloat16)
LATE_Z = jax.ShapeDtypeStruct((LATE * SPAN, SPAN), jnp.bfloat16)


def early_product(*tiles):
    return pl.pallas_call(
        early_kernel,
        out_shape=(jax.ShapeDtypeStruct((SPAN, SPAN), jnp.float32), LATE_H, LATE_Z),
        in_specs=[VMEM] * len(tiles),
        out_specs=(VMEM, VMEM, VMEM),
        scratch_shapes=[
            pltpu.VMEM((SPAN, EARLY * SPAN), jnp.bfloat16),
            pltpu.VMEM((EARLY * SPAN, SPAN), jnp.bfloat16),
        ]
        + slot_scratch(GRID),
        compiler_params=pltpu.CompilerParams(vmem_limit_bytes=14 * 1024 * 1024),
        cost_estimate=pl.CostEstimate(
            flops=2 * SPAN * SPAN * SPAN * EARLY, bytes_accessed=5 * 1024 * 1024, transcendentals=0
        ),
        name="early",
    )(*tiles)


def middle_product(h4, late_h):
    return pl.pallas_call(
        middle_kernel,
        out_shape=LATE_H,
        in_specs=[VMEM] * 2,
        out_specs=VMEM,
        input_output_aliases={1: 0},
        scratch_shapes=slot_scratch(8),
        compiler_params=pltpu.CompilerParams(vmem_limit_bytes=8 * 1024 * 1024),
        cost_estimate=pl.CostEstimate(flops=MIDDLE_FLOPS, bytes_accessed=1024 * 1024, transcendentals=0),
        name="middle",
    )(h4, late_h)


def late_product(keep, acc, late_h, late_z, z4):
    half = jax.ShapeDtypeStruct((TILE, WIDTH, WIDTH), jnp.float32)
    own, other, _ = pl.pallas_call(
        late_kernel,
        out_shape=(half, half, LATE_Z),
        in_specs=[pl.BlockSpec(memory_space=pltpu.SMEM)] + [VMEM] * 4,
        out_specs=(VMEM,) * 3,
        input_output_aliases={3: 2},
        scratch_shapes=[pltpu.VMEM((SPAN, SPAN), jnp.float32)] + slot_scratch(8),
        compiler_params=pltpu.CompilerParams(vmem_limit_bytes=10 * 1024 * 1024),
        cost_estimate=pl.CostEstimate(
            flops=2 * SPAN * SPAN * SPAN * LATE, bytes_accessed=2 * 1024 * 1024, transcendentals=0
        ),
        name="late",
    )(keep, acc, late_h, late_z, z4)
    return own, other


def per_device(h_blocks, h_index, z_blocks, z_index, keep_index):
    zp, hp = pack(z_index[0, 0], h_index[0, 0], z_blocks[0, 0], h_blocks[0, 0])
    z1 = exchange_z(zp, 0)
    h1 = exchange_x(hp)
    z2 = exchange_z(jnp.concatenate([zp, z1], axis=0), 1)
    h01 = jnp.concatenate([hp, h1], axis=0)
    h2 = exchange_y(h01, 0)
    h3 = exchange_y(h01, 1)
    z3 = exchange_z(z2, 0)
    h4 = exchange_y(h2, 1)
    z4 = exchange_z(z3, 1)
    acc, late_h, late_z = early_product(hp, h1, h2, h3, zp, z1, z2, z3)
    late_h = middle_product(h4, late_h)
    own, other = late_product(keep_index[0, 0], acc, late_h, late_z, z4)
    both = lax.all_gather(
        other, "col", axis_index_groups=[[2 * c, 2 * c + 1] for c in range(GRID)], tiled=False
    )
    partner = lax.dynamic_index_in_dim(both, 1 - (lax.axis_index("col") & 1), 0, keepdims=False)
    return (own + partner)[None, None]


def solution(mesh):
    return jax.shard_map(
        per_device,
        mesh=mesh,
        in_specs=(
            P("row", "col", None, None, None),
            P("row", "col", None, None),
            P("row", "col", None, None, None),
            P("row", "col", None, None),
            P("row", "col", None, None),
        ),
        out_specs=P("row", "col", None, None, None),
        check_vma=False,
    )
```

time: 78.6 us -> 60.8 us (0.77); the launches traced: 77.3 us -> 60.3 us
  Pallas kernels: 24.8 us -> 9.74 us
  waiting for transfers between devices: 10.1 us -> 7.97 us
  starting transfers between devices: 36.9 us -> 35 us
  blocking collectives: 2.18 us -> 3.29 us
  local copies, waits for them, and re-layouts: 1.48 us -> 2.45 us
    pallas_call x1, Pallas kernels: 17.7 us -> 2.58 us  [pack(): pl.pallas_call(pack_kernel, out_shape=(jax.ShapeDtypeStruct((ROWS, WIDTH)...]
    ppermute x3, waiting for transfers between devices: 8.96 us -> 4.74 us  [exchange_y(): lax.ppermute(x, BOTH, route(lambda z, y, xl, r: (z, pair_of(kind, y, r),...]
    ppermute x4, waiting for transfers between devices: 0.72 us -> 3.23 us  [exchange_z(): lax.ppermute(x, BOTH, route(lambda z, y, xl, r: (pair_of(kind, z, r), y,...]
    pallas_call x1 -> x2, Pallas kernels: 2.11 us -> 4.09 us  [the longest x1 2.32 us: late_product(): pl.pallas_call(late_kernel, out_shape=(half, half, LATE_Z), in_specs=[pl....]
    pallas_call x1, Pallas kernels: 4.94 us -> 3.07 us  [early_product(): pl.pallas_call(early_kernel, out_shape=(jax.ShapeDtypeStruct((SPAN, SPAN)...]
    ppermute x4, starting transfers between devices: 20 us -> 18.6 us  [exchange_z(): lax.ppermute(x, BOTH, route(lambda z, y, xl, r: (pair_of(kind, z, r), y,...]
    all_gather x1, blocking collectives: 2.18 us -> 3.29 us  [per_device(): lax.all_gather(other, 'col', axis_index_groups=[[2 * c, 2 * c + 1] for c...]
    unnamed x7, local copies, waits for them, and re-layouts: 0.75 us -> 1.71 us
  transfers between devices with their start and end apart: 8 -> 8, of which waited for: 5 -> 4; matrix products, arithmetic and copies ran while one was open for 3% -> 6% of each run, Pallas kernels for 6% -> 8%
where the time goes in v3:
time: 60.8 us; the launch traced here: 60.3 us
  starting transfers between devices  35 us (58%)
  Pallas kernels  9.74 us (16%)
  waiting for transfers between devices  7.97 us (13%)
  blocking collectives  3.29 us (5%)
  local copies, waits for them, and re-layouts  2.45 us (4%)
  other arithmetic  1.72 us (3%)
    ppermute x4, starting transfers between devices, exchange_z(): lax.ppermute(x, BOTH, route(lambda z, y, xl, r: (pair_of(kind, z, r), y,...  18.6 us
    ppermute x3, starting transfers between devices, exchange_y(): lax.ppermute(x, BOTH, route(lambda z, y, xl, r: (z, pair_of(kind, y, r),...  12.7 us
    ppermute x3, waiting for transfers between devices, exchange_y(): lax.ppermute(x, BOTH, route(lambda z, y, xl, r: (z, pair_of(kind, y, r),...  4.74 us
    ppermute x1, starting transfers between devices, exchange_x(): return lax.ppermute(x, BOTH, route(lambda z, y, xl, r: (z, y, xl ^ 1)))  3.68 us
    all_gather x1, blocking collectives, per_device(): lax.all_gather(other, 'col', axis_index_groups=[[2 * c, 2 * c + 1] for c...  3.29 us
    ppermute x4, waiting for transfers between devices, exchange_z(): lax.ppermute(x, BOTH, route(lambda z, y, xl, r: (pair_of(kind, z, r), y,...  3.23 us
    pallas_call x1, Pallas kernels, early_product(): pl.pallas_call(early_kernel, out_shape=(jax.ShapeDtypeStruct((SPAN, SPAN)...  3.07 us
    pallas_call x1, Pallas kernels, pack(): pl.pallas_call(pack_kernel, out_shape=(jax.ShapeDtypeStruct((ROWS, WIDTH)...  2.58 us
  transfers between devices with their start and end apart: 8, of which 4 were waited for; matrix products, arithmetic and copies ran while one was open for 6% of the time, Pallas kernels for 8%

profile of v3, /device:TPU:1, one launch (start us, length us, event | category | flops | bytes accessed | tf_op | source)
XLA Modules:
  0.0 60.3 jit_solution(15553153639440839986)
XLA Ops:
  0.0 2.6 %pack.1 = (bf16[1040,128]{1,0:T(8,128)(2,1)}, bf16[1040,128]{1,0:T(8,128)(2,1)}) custom-call(s32[2,8]{1,0:T(2,128)} %bitcast.16, s32[2,8]{1,0:T(2,128)} %bitcast.17, bf16[1024,128]{1,0:T(8,128)(2,1)} %bitcast.14, bf16[1024,128]{1,0:T(8,128)(2,1)} %bitcast.15), custom_call_target="tpu_custom_call" | custom-call | bytes 1064960 | tf_op jit(solution)/shard_map/pack/pallas_call | solution.py:81
  2.6 11.6 %collective-permute-start.3 = (bf16[1040,128]{1,0:T(8,128)(2,1)}, bf16[1040,128]{1,0:T(8,128)(2,1)S(1)}, u32[]{:S(2)}, u32[]{:S(2)}) collective-permute-start(bf16[1040,128]{1,0:T(8,128)(2,1)} %get-tuple-element.13.zp), channel_id=1, source_target_pairs={{0,32},{1,225},{2,34},{3,226},{4,36},{5,228},{6,38},{7,230},{8,40}... | collective-permute-start | bytes 798728 | tf_op jit(solution)/shard_map/ppermute | solution.py:48
  14.2 3.7 %collective-permute-start = (bf16[1040,128]{1,0:T(8,128)(2,1)}, bf16[1040,128]{1,0:T(8,128)(2,1)S(1)}, u32[]{:S(2)}, u32[]{:S(2)}) collective-permute-start(bf16[1040,128]{1,0:T(8,128)(2,1)} %get-tuple-element.12.hp), channel_id=1, source_target_pairs={{0,2},{1,3},{2,0},{3,1},{4,6},{5,7},{6,4},{7,5},{8,10},{9,11},{10,... | collective-permute-start | bytes 798728 | tf_op jit(solution)/shard_map/ppermute | solution.py:56
  17.9 1.7 %constant_dynamic-update-slice_fusion.1 = bf16[2080,128]{1,0:T(8,128)(2,1)} fusion(bf16[1040,128]{1,0:T(8,128)(2,1)} %get-tuple-element.12.hp), kind=kLoop, calls=%fused_computation.4 | loop fusion | bytes 532480
  19.6 0.0 collective-permute-done.3.z1
  19.6 1.0 %pad_maximum_fusion = bf16[2080,128]{1,0:T(8,128)(2,1)S(1)} fusion(bf16[1040,128]{1,0:T(8,128)(2,1)S(1)} %collective-permute-done.3.z1, bf16[1040,128]{1,0:T(8,128)(2,1)} %get-tuple-element.13.zp), kind=kLoop, calls=%fused_computation | loop fusion | flops 1064960 | bytes 1064960 | tf_op jit(solution)/shard_map/concatenate | solution.py:294
  20.6 1.9 %collective-permute-start.4 = (bf16[2080,128]{1,0:T(8,128)(2,1)S(1)}, bf16[2080,128]{1,0:T(8,128)(2,1)S(1)}, u32[]{:S(2)}, u32[]{:S(2)}) collective-permute-start(bf16[2080,128]{1,0:T(8,128)(2,1)S(1)} %pad_maximum_fusion), channel_id=1, source_target_pairs={{0,224},{1,33},{2,227},{3,35},{4,229},{5,37},{6,231},{7,39},{8,233... | collective-permute-start | bytes 1597448 | tf_op jit(solution)/shard_map/ppermute | solution.py:48
  22.5 0.0 collective-permute-done.h1
  22.6 0.7 %constant_dynamic-update-slice_fusion = bf16[2080,128]{1,0:T(8,128)(2,1)} fusion(bf16[2080,128]{1,0:T(8,128)(2,1)} %constant_dynamic-update-slice_fusion.1, bf16[1040,128]{1,0:T(8,128)(2,1)S(1)} %collective-permute-done.h1), kind=kLoop, calls=%fused_computation.3 | loop fusion | bytes 532480 | tf_op jit(solution)/shard_map/concatenate | solution.py:295
  23.3 5.6 %collective-permute-start.1 = (bf16[2080,128]{1,0:T(8,128)(2,1)}, bf16[2080,128]{1,0:T(8,128)(2,1)S(1)}, u32[]{:S(2)}, u32[]{:S(2)}) collective-permute-start(bf16[2080,128]{1,0:T(8,128)(2,1)} %constant_dynamic-update-slice_fusion), channel_id=1, source_target_pairs={{0,4},{1,28},{2,6},{3,30},{4,0},{5,9},{6,2},{7,11},{8,12},{9,5},{1... | collective-permute-start | bytes 1597448 | tf_op jit(solution)/shard_map/ppermute | solution.py:52
  28.9 2.1 %collective-permute-done.4.z2 = bf16[2080,128]{1,0:T(8,128)(2,1)S(1)} collective-permute-done((bf16[2080,128]{1,0:T(8,128)(2,1)S(1)}, bf16[2080,128]{1,0:T(8,128)(2,1)S(1)}, u32[]{:S(2)}, u32[]{:S(2)}) %collective-permute-start.4) | collective-permute-done | bytes 532512 | tf_op jit(solution)/shard_map/ppermute | solution.py:48
  30.9 3.2 %collective-permute-start.5 = (bf16[2080,128]{1,0:T(8,128)(2,1)S(1)}, bf16[2080,128]{1,0:T(8,128)(2,1)S(1)}, u32[]{:S(2)}, u32[]{:S(2)}) collective-permute-start(bf16[2080,128]{1,0:T(8,128)(2,1)S(1)} %collective-permute-done.4.z2), channel_id=1, source_target_pairs={{0,32},{1,225},{2,34},{3,226},{4,36},{5,228},{6,38},{7,230},{8,40}... | collective-permute-start | bytes 1597448 | tf_op jit(solution)/shard_map/ppermute | solution.py:48
  34.1 5.2 %collective-permute-start.2 = (bf16[2080,128]{1,0:T(8,128)(2,1)}, bf16[2080,128]{1,0:T(8,128)(2,1)S(1)}, u32[]{:S(2)}, u32[]{:S(2)}) collective-permute-start(bf16[2080,128]{1,0:T(8,128)(2,1)} %constant_dynamic-update-slice_fusion), channel_id=1, source_target_pairs={{0,29},{1,5},{2,31},{3,7},{4,8},{5,1},{6,10},{7,3},{8,4},{9,13},{1... | collective-permute-start | bytes 1597448 | tf_op jit(solution)/shard_map/ppermute | solution.py:52
  39.3 0.0 collective-permute-done.1.h2
  39.3 1.9 %collective-permute-start.6 = (bf16[2080,128]{1,0:T(8,128)(2,1)S(1)}, bf16[2080,128]{1,0:T(8,128)(2,1)}, u32[]{:S(2)}, u32[]{:S(2)}) collective-permute-start(bf16[2080,128]{1,0:T(8,128)(2,1)S(1)} %collective-permute-done.1.h2), channel_id=1, source_target_pairs={{0,29},{1,5},{2,31},{3,7},{4,8},{5,1},{6,10},{7,3},{8,4},{9,13},{1... | collective-permute-start | bytes 1597448 | tf_op jit(solution)/shard_map/ppermute | solution.py:52
  41.3 1.2 %collective-permute-done.5.z3 = bf16[2080,128]{1,0:T(8,128)(2,1)S(1)} collective-permute-done((bf16[2080,128]{1,0:T(8,128)(2,1)S(1)}, bf16[2080,128]{1,0:T(8,128)(2,1)S(1)}, u32[]{:S(2)}, u32[]{:S(2)}) %collective-permute-start.5) | collective-permute-done | bytes 532512 | tf_op jit(solution)/shard_map/ppermute | solution.py:48
  42.4 1.9 %collective-permute-start.7 = (bf16[2080,128]{1,0:T(8,128)(2,1)S(1)}, bf16[2080,128]{1,0:T(8,128)(2,1)S(1)}, u32[]{:S(2)}, u32[]{:S(2)}) collective-permute-start(bf16[2080,128]{1,0:T(8,128)(2,1)S(1)} %collective-permute-done.5.z3), channel_id=1, source_target_pairs={{0,224},{1,33},{2,227},{3,35},{4,229},{5,37},{6,231},{7,39},{8,233... | collective-permute-start | bytes 1597448 | tf_op jit(solution)/shard_map/ppermute | solution.py:48
  44.4 2.2 %collective-permute-done.2.h3 = bf16[2080,128]{1,0:T(8,128)(2,1)S(1)} collective-permute-done((bf16[2080,128]{1,0:T(8,128)(2,1)}, bf16[2080,128]{1,0:T(8,128)(2,1)S(1)}, u32[]{:S(2)}, u32[]{:S(2)}) %collective-permute-start.2) | collective-permute-done | bytes 532512 | tf_op jit(solution)/shard_map/ppermute | solution.py:52
  46.6 3.1 %early.1 = (f32[512,512]{1,0:T(8,128)S(1)}, bf16[512,1536]{1,0:T(8,128)(2,1)S(1)}, bf16[1536,512]{1,0:T(8,128)(2,1)S(1)}) custom-call(bf16[1040,128]{1,0:T(8,128)(2,1)S(1)} %copy-done, bf16[1040,128]{1,0:T(8,128)(2,1)S(1)} %collective-permute-done.h1, bf16[2080,128]{1,0:T(8,128)(2,1)S(1)} %collective-permute-done.1.h2, ...), custom_call_target="tpu_custom_call" | custom-call | flops 1342177280 | bytes 5242880 | tf_op jit(solution)/shard_map/early/pallas_call | solution.py:240
  49.6 2.5 %collective-permute-done.6.h4 = bf16[2080,128]{1,0:T(8,128)(2,1)} collective-permute-done((bf16[2080,128]{1,0:T(8,128)(2,1)S(1)}, bf16[2080,128]{1,0:T(8,128)(2,1)}, u32[]{:S(2)}, u32[]{:S(2)}) %collective-permute-start.6) | collective-permute-done | bytes 532512 | tf_op jit(solution)/shard_map/ppermute | solution.py:52
  52.2 1.8 %middle.1.hd = bf16[512,1536]{1,0:T(8,128)(2,1)S(1)} custom-call(bf16[2080,128]{1,0:T(8,128)(2,1)} %collective-permute-done.6.h4, bf16[512,1536]{1,0:T(8,128)(2,1)S(1)} %get-tuple-element.15.late_h), custom_call_target="tpu_custom_call", output_to_operand_aliasing={{}: (1, {})} | custom-call | flops 8589934592 | bytes 1048576 | tf_op jit(solution)/shard_map/middle/pallas_call | solution.py:259
  54.0 2.3 %late.1 = (f32[4,128,128]{2,1,0:T(8,128)S(1)}, f32[4,128,128]{2,1,0:T(8,128)S(1)}, bf16[1536,512]{1,0:T(8,128)(2,1)S(1)}) custom-call(s32[2,8]{1,0:T(2,128)S(1)} %bitcast.12, f32[512,512]{1,0:T(8,128)S(1)} %get-tuple-element.14.acc, bf16[512,1536]{1,0:T(8,128)(2,1)S(1)} %middle.1.hd, ...), custom_call_target="tpu_custom_call", output_to_operand_aliasing={{2}: (3, {})} | custom-call | flops 805306368 | bytes 2097152 | tf_op jit(solution)/shard_map/late/pallas_call | solution.py:274
  56.3 3.3 %all-gather = f32[8,128,128]{2,1,0:T(8,128)S(1)} all-gather(f32[4,128,128]{2,1,0:T(8,128)S(1)} %get-tuple-element.18), channel_id=2, replica_groups={{0,1},{2,3},{4,5},{6,7},{8,9},{10,11},{12,13},{14,15},{16,17},{18,19},{..., dimensions={0}, use_global_device_ids=true | all-gather | bytes 786432 | tf_op jit(solution)/shard_map/all_gather | solution.py:304
  59.6 0.7 %fusion = f32[1,1,4,128,128]{4,3,2,1,0:T(8,128)} fusion(f32[4,128,128]{2,1,0:T(8,128)S(1)} %get-tuple-element.17, f32[2,4,128,128]{3,2,1,0:T(8,128)S(1)} %bitcast.13, s32[]{:T(128)S(6)} %select_n.4), kind=kLoop, calls=%fused_computation.2 | loop fusion | flops 65536 | bytes 786436 | tf_op jit(solution)/shard_map/broadcast_in_dim | solution.py:308
  (7 shorter events, 0.0 us)
Async XLA Ops:
  2.6 44.0 %copy-start = (bf16[1040,128]{1,0:T(8,128)(2,1)S(1)}, bf16[1040,128]{1,0:T(8,128)(2,1)}, u32[]{:S(2)}) copy-start(bf16[1040,128]{1,0:T(8,128)(2,1)} %get-tuple-element.12.hp) | copy-start | bytes 798724
  2.6 44.0 %copy-start.1 = (bf16[1040,128]{1,0:T(8,128)(2,1)S(1)}, bf16[1040,128]{1,0:T(8,128)(2,1)}, u32[]{:S(2)}) copy-start(bf16[1040,128]{1,0:T(8,128)(2,1)} %get-tuple-element.13.zp) | copy-start | bytes 798724
  2.6 17.0 %collective-permute-start.3 = (bf16[1040,128]{1,0:T(8,128)(2,1)}, bf16[1040,128]{1,0:T(8,128)(2,1)S(1)}, u32[]{:S(2)}, u32[]{:S(2)}) collective-permute-start(bf16[1040,128]{1,0:T(8,128)(2,1)} %get-tuple-element.13.zp), channel_id=1, source_target_pairs={{0,32},{1,225},{2,34},{3,226},{4,36},{5,228},{6,38},{7,230},{8,40}... | collective-permute-start | bytes 798728 | tf_op jit(solution)/shard_map/ppermute | solution.py:48
  14.2 8.3 %collective-permute-start = (bf16[1040,128]{1,0:T(8,128)(2,1)}, bf16[1040,128]{1,0:T(8,128)(2,1)S(1)}, u32[]{:S(2)}, u32[]{:S(2)}) collective-permute-start(bf16[1040,128]{1,0:T(8,128)(2,1)} %get-tuple-element.12.hp), channel_id=1, source_target_pairs={{0,2},{1,3},{2,0},{3,1},{4,6},{5,7},{6,4},{7,5},{8,10},{9,11},{10,... | collective-permute-start | bytes 798728 | tf_op jit(solution)/shard_map/ppermute | solution.py:56
  20.6 10.3 %collective-permute-start.4 = (bf16[2080,128]{1,0:T(8,128)(2,1)S(1)}, bf16[2080,128]{1,0:T(8,128)(2,1)S(1)}, u32[]{:S(2)}, u32[]{:S(2)}) collective-permute-start(bf16[2080,128]{1,0:T(8,128)(2,1)S(1)} %pad_maximum_fusion), channel_id=1, source_target_pairs={{0,224},{1,33},{2,227},{3,35},{4,229},{5,37},{6,231},{7,39},{8,233... | collective-permute-start | bytes 1597448 | tf_op jit(solution)/shard_map/ppermute | solution.py:48
  23.3 16.0 %collective-permute-start.1 = (bf16[2080,128]{1,0:T(8,128)(2,1)}, bf16[2080,128]{1,0:T(8,128)(2,1)S(1)}, u32[]{:S(2)}, u32[]{:S(2)}) collective-permute-start(bf16[2080,128]{1,0:T(8,128)(2,1)} %constant_dynamic-update-slice_fusion), channel_id=1, source_target_pairs={{0,4},{1,28},{2,6},{3,30},{4,0},{5,9},{6,2},{7,11},{8,12},{9,5},{1... | collective-permute-start | bytes 1597448 | tf_op jit(solution)/shard_map/ppermute | solution.py:52
  30.9 11.5 %collective-permute-start.5 = (bf16[2080,128]{1,0:T(8,128)(2,1)S(1)}, bf16[2080,128]{1,0:T(8,128)(2,1)S(1)}, u32[]{:S(2)}, u32[]{:S(2)}) collective-permute-start(bf16[2080,128]{1,0:T(8,128)(2,1)S(1)} %collective-permute-done.4.z2), channel_id=1, source_target_pairs={{0,32},{1,225},{2,34},{3,226},{4,36},{5,228},{6,38},{7,230},{8,40}... | collective-permute-start | bytes 1597448 | tf_op jit(solution)/shard_map/ppermute | solution.py:48
  34.1 12.5 %collective-permute-start.2 = (bf16[2080,128]{1,0:T(8,128)(2,1)}, bf16[2080,128]{1,0:T(8,128)(2,1)S(1)}, u32[]{:S(2)}, u32[]{:S(2)}) collective-permute-start(bf16[2080,128]{1,0:T(8,128)(2,1)} %constant_dynamic-update-slice_fusion), channel_id=1, source_target_pairs={{0,29},{1,5},{2,31},{3,7},{4,8},{5,1},{6,10},{7,3},{8,4},{9,13},{1... | collective-permute-start | bytes 1597448 | tf_op jit(solution)/shard_map/ppermute | solution.py:52
  39.3 12.8 %collective-permute-start.6 = (bf16[2080,128]{1,0:T(8,128)(2,1)S(1)}, bf16[2080,128]{1,0:T(8,128)(2,1)}, u32[]{:S(2)}, u32[]{:S(2)}) collective-permute-start(bf16[2080,128]{1,0:T(8,128)(2,1)S(1)} %collective-permute-done.1.h2), channel_id=1, source_target_pairs={{0,29},{1,5},{2,31},{3,7},{4,8},{5,1},{6,10},{7,3},{8,4},{9,13},{1... | collective-permute-start | bytes 1597448 | tf_op jit(solution)/shard_map/ppermute | solution.py:52
  42.4 11.5 %collective-permute-start.7 = (bf16[2080,128]{1,0:T(8,128)(2,1)S(1)}, bf16[2080,128]{1,0:T(8,128)(2,1)S(1)}, u32[]{:S(2)}, u32[]{:S(2)}) collective-permute-start(bf16[2080,128]{1,0:T(8,128)(2,1)S(1)} %collective-permute-done.5.z3), channel_id=1, source_target_pairs={{0,224},{1,33},{2,227},{3,35},{4,229},{5,37},{6,231},{7,39},{8,233... | collective-permute-start | bytes 1597448 | tf_op jit(solution)/shard_map/ppermute | solution.py:48
  52.2 1.8 %copy-start.2 = (s32[1,1,2,8]{3,2,1,0:T(2,128)S(1)}, s32[1,1,2,8]{3,2,1,0:T(2,128)}, u32[]{:S(2)}) copy-start(s32[1,1,2,8]{3,2,1,0:T(2,128)} %param.9) | copy-start | bytes 196

commit v4 on v3

--- a/solution.py
+++ b/solution.py
@@ -80,7 +80,7 @@
     vmem = pl.BlockSpec(memory_space=pltpu.VMEM)
     return pl.pallas_call(
         pack_kernel,
-        out_shape=(jax.ShapeDtypeStruct((ROWS, WIDTH), blocks_z.dtype),) * 2,
+        out_shape=(pltpu.VMEM((ROWS, WIDTH), blocks_z.dtype),) * 2,
         in_specs=[smem, smem, hbm, hbm],
         out_specs=(vmem, vmem),
         scratch_shapes=[pltpu.SemaphoreType.DMA((2,))],
@@ -88,6 +88,25 @@
         cost_estimate=pl.CostEstimate(flops=0, bytes_accessed=ROWS * WIDTH * 8, transcendentals=0),
         name="pack",
     )(places_z, places_h, blocks_z.reshape(NNZ * WIDTH, WIDTH), blocks_h.reshape(NNZ * WIDTH, WIDTH))
+
+
+def join_kernel(a, b, out):
+    out[: a.shape[0], :] = a[...]
+    out[a.shape[0] :, :] = b[...]
+
+
+def join(a, b):
+    vmem = pl.BlockSpec(memory_space=pltpu.VMEM)
+    rows = a.shape[0] + b.shape[0]
+    return pl.pallas_call(
+        join_kernel,
+        out_shape=jax.ShapeDtypeStruct((rows, WIDTH), a.dtype),
+        in_specs=[vmem, vmem],
+        out_specs=vmem,
+        compiler_params=pltpu.CompilerParams(vmem_limit_bytes=4 * 1024 * 1024),
+        cost_estimate=pl.CostEstimate(flops=0, bytes_accessed=rows * WIDTH * 4, transcendentals=0),
+        name="join",
+    )(a, b)
 
 
 def near(n, kind, role):
@@ -116,13 +135,16 @@
     return of_h, of_z
 
 
-def read_slots(parts, idx_v, idx_s, sem):
-    for n, (buf, part) in enumerate(parts):
-        base = part * ROWS + NNZ * WIDTH
-        idx_v[n : n + 1, :] = buf[base : base + 16, :].astype(jnp.float32).astype(jnp.int32)[0:1]
-    copy = pltpu.make_async_copy(idx_v, idx_s, sem)
-    copy.start()
-    return copy
+class Slots:
+    def __init__(self, parts):
+        self.rows = []
+        for buf, part in parts:
+            base = part * ROWS + NNZ * WIDTH
+            self.rows.append(buf[base : base + 16, :].astype(jnp.float32).astype(jnp.int32))
+
+    def __getitem__(self, at):
+        n, k = at
+        return self.rows[n][0, k]
 
 
 def place(buf, part, slots, n, put):
@@ -155,10 +177,10 @@
     return jnp.where(ahead < 3, ahead, ahead - 3)
 
 
-def early_kernel(hp, h1, h2, h3, zp, z1, z2, z3, acc, late_h, late_z, hd, zd, idx_v, idx_s, sem):
+def early_kernel(hp, h1, h2, h3, zp, z1, z2, z3, acc, late_h, late_z, hd, zd):
     h_parts = [(hp, 0), (h1, 0), (h2, 0), (h2, 1), (h3, 0), (h3, 1)]
     z_parts = [(zp, 0), (z1, 0), (z2, 0), (z2, 1), (z3, 0), (z3, 1)]
-    copy = read_slots(h_parts + z_parts, idx_v, idx_s, sem)
+    slots = Slots(h_parts + z_parts)
     late_h[...] = jnp.zeros_like(late_h)
     late_z[...] = jnp.zeros_like(late_z)
 
@@ -169,7 +191,6 @@
         zd[pl.ds(at, SPAN), :] = jnp.zeros((SPAN, SPAN), zd.dtype)
 
     of_h, of_z = offsets()
-    copy.wait()
     for n, (buf, part) in enumerate(h_parts):
         ahead = of_h[n]
         if n in (3, 5):
@@ -177,40 +198,38 @@
 
             @pl.when(is_late)
             def _():
-                place(buf, part, idx_s, n, into_h(late_h, ahead - 3))
+                place(buf, part, slots, n, into_h(late_h, ahead - 3))
 
             @pl.when(jnp.logical_not(is_late))
             def _():
-                place(buf, part, idx_s, n, into_h(hd, early_turn(ahead)))
+                place(buf, part, slots, n, into_h(hd, early_turn(ahead)))
         else:
-            place(buf, part, idx_s, n, into_h(hd, early_turn(ahead)))
+            place(buf, part, slots, n, into_h(hd, early_turn(ahead)))
     for n, (buf, part) in enumerate(z_parts):
         if n == 5:
             put = into_z(late_z, of_z[n] - 3)
         else:
             put = into_z(zd, early_turn(of_z[n]))
-        place(buf, part, idx_s, len(h_parts) + n, put)
+        place(buf, part, slots, len(h_parts) + n, put)
     for m in range(0, SPAN, 256):
         acc[m : m + 256, :] = jnp.dot(hd[m : m + 256, :], zd[...], preferred_element_type=jnp.float32)
 
 
-def middle_kernel(h4, late_h, out_h, idx_v, idx_s, sem):
+def middle_kernel(h4, late_h, out_h):
     parts = [(h4, 0), (h4, 1)]
-    copy = read_slots(parts, idx_v, idx_s, sem)
+    slots = Slots(parts)
     of_h, _ = offsets()
-    copy.wait()
     for n, (buf, part) in enumerate(parts):
-        place(buf, part, idx_s, n, into_h(out_h, of_h[6 + n] - 3))
-
-
-def late_kernel(keep, acc, hd, late_z, z4, own, other, zd, total, idx_v, idx_s, sem):
+        place(buf, part, slots, n, into_h(out_h, of_h[6 + n] - 3))
+
+
+def late_kernel(keep, acc, hd, late_z, z4, own, other, zd, total):
     parts = [(z4, 0), (z4, 1)]
-    copy = read_slots(parts, idx_v, idx_s, sem)
+    slots = Slots(parts)
     _, of_z = offsets()
     layer = lax.axis_index("col") & 1
-    copy.wait()
     for n, (buf, part) in enumerate(parts):
-        place(buf, part, idx_s, n, into_z(zd, of_z[6 + n] - 3))
+        place(buf, part, slots, n, into_z(zd, of_z[6 + n] - 3))
     for m in range(0, SPAN, 256):
         total[m : m + 256, :] = acc[m : m + 256, :] + jnp.dot(
             hd[m : m + 256, :], zd[...], preferred_element_type=jnp.float32
@@ -222,14 +241,6 @@
             dst[q] = total[pl.ds(r, WIDTH), pl.ds(s, WIDTH)]
 
 
-def slot_scratch(rows):
-    return [
-        pltpu.VMEM((rows, WIDTH), jnp.int32),
-        pltpu.SMEM((rows, WIDTH), jnp.int32),
-        pltpu.SemaphoreType.DMA,
-    ]
-
-
 VMEM = pl.BlockSpec(memory_space=pltpu.VMEM)
 MIDDLE_FLOPS = 2 * SPAN * SPAN * SPAN * 32
 LATE_H = jax.ShapeDtypeStruct((SPAN, LATE * SPAN), jnp.bfloat16)
@@ -245,8 +256,7 @@
         scratch_shapes=[
             pltpu.VMEM((SPAN, EARLY * SPAN), jnp.bfloat16),
             pltpu.VMEM((EARLY * SPAN, SPAN), jnp.bfloat16),
-        ]
-        + slot_scratch(GRID),
+        ],
         compiler_params=pltpu.CompilerParams(vmem_limit_bytes=14 * 1024 * 1024),
         cost_estimate=pl.CostEstimate(
             flops=2 * SPAN * SPAN * SPAN * EARLY, bytes_accessed=5 * 1024 * 1024, transcendentals=0
@@ -262,7 +272,6 @@
         in_specs=[VMEM] * 2,
         out_specs=VMEM,
         input_output_aliases={1: 0},
-        scratch_shapes=slot_scratch(8),
         compiler_params=pltpu.CompilerParams(vmem_limit_bytes=8 * 1024 * 1024),
         cost_estimate=pl.CostEstimate(flops=MIDDLE_FLOPS, bytes_accessed=1024 * 1024, transcendentals=0),
         name="middle",
@@ -277,7 +286,7 @@
         in_specs=[pl.BlockSpec(memory_space=pltpu.SMEM)] + [VMEM] * 4,
         out_specs=(VMEM,) * 3,
         input_output_aliases={3: 2},
-        scratch_shapes=[pltpu.VMEM((SPAN, SPAN), jnp.float32)] + slot_scratch(8),
+        scratch_shapes=[pltpu.VMEM((SPAN, SPAN), jnp.float32)],
         compiler_params=pltpu.CompilerParams(vmem_limit_bytes=10 * 1024 * 1024),
         cost_estimate=pl.CostEstimate(
             flops=2 * SPAN * SPAN * SPAN * LATE, bytes_accessed=2 * 1024 * 1024, transcendentals=0
@@ -291,8 +300,8 @@
     zp, hp = pack(z_index[0, 0], h_index[0, 0], z_blocks[0, 0], h_blocks[0, 0])
     z1 = exchange_z(zp, 0)
     h1 = exchange_x(hp)
-    z2 = exchange_z(jnp.concatenate([zp, z1], axis=0), 1)
-    h01 = jnp.concatenate([hp, h1], axis=0)
+    z2 = exchange_z(join(zp, z1), 1)
+    h01 = join(hp, h1)
     h2 = exchange_y(h01, 0)
     h3 = exchange_y(h01, 1)
     z3 = exchange_z(z2, 0)

time: 60.8 us -> 58.1 us (0.956)
  local copies, waits for them, and re-layouts: 2.45 us -> 0.01 us
  starting transfers between devices: 35 us -> 36.6 us
  other arithmetic: 1.72 us -> 0.73 us
  waiting for transfers between devices: 7.97 us -> 7.17 us
  Pallas kernels: 9.74 us -> 8.98 us
  blocking collectives: 3.29 us -> 4.02 us
    ppermute x4, waiting for transfers between devices: 3.23 us -> 0.51 us  [exchange_z(): lax.ppermute(x, BOTH, route(lambda z, y, xl, r: (pair_of(kind, z, r), y,...]
    ppermute x1, waiting for transfers between devices: 0.01 us -> 2.02 us  [exchange_x(): return lax.ppermute(x, BOTH, route(lambda z, y, xl, r: (z, y, xl ^ 1)))]
    unnamed x7 -> x2, local copies, waits for them, and re-layouts: 1.71 us -> 0.01 us
    ppermute x4, starting transfers between devices: 18.6 us -> 19.9 us  [exchange_z(): lax.ppermute(x, BOTH, route(lambda z, y, xl, r: (pair_of(kind, z, r), y,...]
    pallas_call x1, Pallas kernels: 3.07 us -> 4.12 us  [early_product(): pl.pallas_call(early_kernel, out_shape=(jax.ShapeDtypeStruct((SPAN, SPAN)...]
    concatenate x1 -> x0, other arithmetic: 0.99 us -> none  [per_device(): z2 = exchange_z(jnp.concatenate([zp, z1], axis=0), 1)]
    pallas_call x1 -> x3, Pallas kernels: 2.58 us -> 1.82 us  [the longest x1 1.75 us: pack(): pl.pallas_call(pack_kernel, out_shape=(pltpu.VMEM((ROWS, WIDTH), blocks_z...]
    concatenate x1 -> x0, local copies, waits for them, and re-layouts: 0.74 us -> none  [per_device(): h01 = jnp.concatenate([hp, h1], axis=0)]
  transfers between devices with their start and end apart: 8 -> 8, of which waited for: 4 -> 5; matrix products, arithmetic and copies ran while one was open for 6% -> 0% of each run, Pallas kernels for 8% -> 9%
where the time goes in v4:
time: 58.1 us; the launch traced here: 57.7 us
  starting transfers between devices  36.6 us (63%)
  Pallas kernels  8.98 us (15%)
  waiting for transfers between devices  7.17 us (12%)
  blocking collectives  4.02 us (7%)
  other arithmetic  0.73 us (1%)
    ppermute x4, starting transfers between devices, exchange_z(): lax.ppermute(x, BOTH, route(lambda z, y, xl, r: (pair_of(kind, z, r), y,...  19.9 us
    ppermute x3, starting transfers between devices, exchange_y(): lax.ppermute(x, BOTH, route(lambda z, y, xl, r: (z, pair_of(kind, y, r),...  13 us
    ppermute x3, waiting for transfers between devices, exchange_y(): lax.ppermute(x, BOTH, route(lambda z, y, xl, r: (z, pair_of(kind, y, r),...  4.64 us
    pallas_call x1, Pallas kernels, early_product(): pl.pallas_call(early_kernel, out_shape=(jax.ShapeDtypeStruct((SPAN, SPAN)...  4.12 us
    all_gather x1, blocking collectives, per_device(): lax.all_gather(other, 'col', axis_index_groups=[[2 * c, 2 * c + 1] for c...  4.02 us
    ppermute x1, starting transfers between devices, exchange_x(): return lax.ppermute(x, BOTH, route(lambda z, y, xl, r: (z, y, xl ^ 1)))  3.68 us
    ppermute x1, waiting for transfers between devices, exchange_x(): return lax.ppermute(x, BOTH, route(lambda z, y, xl, r: (z, y, xl ^ 1)))  2.02 us
    pallas_call x1, Pallas kernels, late_product(): pl.pallas_call(late_kernel, out_shape=(half, half, LATE_Z), in_specs=[pl....  1.79 us
  transfers between devices with their start and end apart: 8, of which 5 were waited for; matrix products, arithmetic and copies ran while one was open for 0% of the time, Pallas kernels for 9%

profile of v4, /device:TPU:1, one launch (start us, length us, event | category | flops | bytes accessed | tf_op | source)
XLA Modules:
  0.0 57.7 jit_solution(12696801242548436069)
XLA Ops:
  0.0 1.7 %pack.1 = (bf16[1040,128]{1,0:T(8,128)(2,1)S(1)}, bf16[1040,128]{1,0:T(8,128)(2,1)S(1)}) custom-call(s32[2,8]{1,0:T(2,128)} %bitcast.16, s32[2,8]{1,0:T(2,128)} %bitcast.17, bf16[1024,128]{1,0:T(8,128)(2,1)} %bitcast.14, bf16[1024,128]{1,0:T(8,128)(2,1)} %bitcast.15), custom_call_target="tpu_custom_call" | custom-call | bytes 1064960 | tf_op jit(solution)/shard_map/pack/pallas_call | solution.py:81
  1.8 11.5 %collective-permute-start.3 = (bf16[1040,128]{1,0:T(8,128)(2,1)S(1)}, bf16[1040,128]{1,0:T(8,128)(2,1)S(1)}, u32[]{:S(2)}, u32[]{:S(2)}) collective-permute-start(bf16[1040,128]{1,0:T(8,128)(2,1)S(1)} %get-tuple-element.13.a.zp), channel_id=1, source_target_pairs={{0,32},{1,225},{2,34},{3,226},{4,36},{5,228},{6,38},{7,230},{8,40}... | collective-permute-start | bytes 798728 | tf_op jit(solution)/shard_map/ppermute | solution.py:48
  13.3 3.7 %collective-permute-start = (bf16[1040,128]{1,0:T(8,128)(2,1)S(1)}, bf16[1040,128]{1,0:T(8,128)(2,1)S(1)}, u32[]{:S(2)}, u32[]{:S(2)}) collective-permute-start(bf16[1040,128]{1,0:T(8,128)(2,1)S(1)} %get-tuple-element.12.a.hp), channel_id=1, source_target_pairs={{0,2},{1,3},{2,0},{3,1},{4,6},{5,7},{6,4},{7,5},{8,10},{9,11},{10,... | collective-permute-start | bytes 798728 | tf_op jit(solution)/shard_map/ppermute | solution.py:56
  16.9 0.1 collective-permute-done.3.b.z1
  17.1 1.9 %collective-permute-start.4 = (bf16[2080,128]{1,0:T(8,128)(2,1)S(1)}, bf16[2080,128]{1,0:T(8,128)(2,1)S(1)}, u32[]{:S(2)}, u32[]{:S(2)}) collective-permute-start(bf16[2080,128]{1,0:T(8,128)(2,1)S(1)} %join.3), channel_id=1, source_target_pairs={{0,224},{1,33},{2,227},{3,35},{4,229},{5,37},{6,231},{7,39},{8,233... | collective-permute-start | bytes 1597448 | tf_op jit(solution)/shard_map/ppermute | solution.py:48
  19.0 2.0 %collective-permute-done.b.h1 = bf16[1040,128]{1,0:T(8,128)(2,1)S(1)} collective-permute-done((bf16[1040,128]{1,0:T(8,128)(2,1)S(1)}, bf16[1040,128]{1,0:T(8,128)(2,1)S(1)}, u32[]{:S(2)}, u32[]{:S(2)}) %collective-permute-start) | collective-permute-done | bytes 266272 | tf_op jit(solution)/shard_map/ppermute | solution.py:56
  21.1 5.9 %collective-permute-start.1 = (bf16[2080,128]{1,0:T(8,128)(2,1)S(1)}, bf16[2080,128]{1,0:T(8,128)(2,1)S(1)}, u32[]{:S(2)}, u32[]{:S(2)}) collective-permute-start(bf16[2080,128]{1,0:T(8,128)(2,1)S(1)} %join.2), channel_id=1, source_target_pairs={{0,4},{1,28},{2,6},{3,30},{4,0},{5,9},{6,2},{7,11},{8,12},{9,5},{1... | collective-permute-start | bytes 1597448 | tf_op jit(solution)/shard_map/ppermute | solution.py:52
  27.0 0.4 collective-permute-done.4.z2
  27.4 4.6 %collective-permute-start.5 = (bf16[2080,128]{1,0:T(8,128)(2,1)S(1)}, bf16[2080,128]{1,0:T(8,128)(2,1)S(1)}, u32[]{:S(2)}, u32[]{:S(2)}) collective-permute-start(bf16[2080,128]{1,0:T(8,128)(2,1)S(1)} %collective-permute-done.4.z2), channel_id=1, source_target_pairs={{0,32},{1,225},{2,34},{3,226},{4,36},{5,228},{6,38},{7,230},{8,40}... | collective-permute-start | bytes 1597448 | tf_op jit(solution)/shard_map/ppermute | solution.py:48
  32.0 5.2 %collective-permute-start.2 = (bf16[2080,128]{1,0:T(8,128)(2,1)S(1)}, bf16[2080,128]{1,0:T(8,128)(2,1)}, u32[]{:S(2)}, u32[]{:S(2)}) collective-permute-start(bf16[2080,128]{1,0:T(8,128)(2,1)S(1)} %join.2), channel_id=1, source_target_pairs={{0,29},{1,5},{2,31},{3,7},{4,8},{5,1},{6,10},{7,3},{8,4},{9,13},{1... | collective-permute-start | bytes 1597448 | tf_op jit(solution)/shard_map/ppermute | solution.py:52
  37.2 0.0 collective-permute-done.1.h2
  37.2 1.9 %collective-permute-start.6 = (bf16[2080,128]{1,0:T(8,128)(2,1)S(1)}, bf16[2080,128]{1,0:T(8,128)(2,1)}, u32[]{:S(2)}, u32[]{:S(2)}) collective-permute-start(bf16[2080,128]{1,0:T(8,128)(2,1)S(1)} %collective-permute-done.1.h2), channel_id=1, source_target_pairs={{0,29},{1,5},{2,31},{3,7},{4,8},{5,1},{6,10},{7,3},{8,4},{9,13},{1... | collective-permute-start | bytes 1597448 | tf_op jit(solution)/shard_map/ppermute | solution.py:52
  39.1 0.0 collective-permute-done.5.z3
  39.1 1.9 %collective-permute-start.7 = (bf16[2080,128]{1,0:T(8,128)(2,1)S(1)}, bf16[2080,128]{1,0:T(8,128)(2,1)S(1)}, u32[]{:S(2)}, u32[]{:S(2)}) collective-permute-start(bf16[2080,128]{1,0:T(8,128)(2,1)S(1)} %collective-permute-done.5.z3), channel_id=1, source_target_pairs={{0,224},{1,33},{2,227},{3,35},{4,229},{5,37},{6,231},{7,39},{8,233... | collective-permute-start | bytes 1597448 | tf_op jit(solution)/shard_map/ppermute | solution.py:48
  41.1 3.2 %collective-permute-done.2.h3 = bf16[2080,128]{1,0:T(8,128)(2,1)} collective-permute-done((bf16[2080,128]{1,0:T(8,128)(2,1)S(1)}, bf16[2080,128]{1,0:T(8,128)(2,1)}, u32[]{:S(2)}, u32[]{:S(2)}) %collective-permute-start.2) | collective-permute-done | bytes 532512 | tf_op jit(solution)/shard_map/ppermute | solution.py:52
  44.2 4.1 %early.1 = (f32[512,512]{1,0:T(8,128)S(1)}, bf16[512,1536]{1,0:T(8,128)(2,1)S(1)}, bf16[1536,512]{1,0:T(8,128)(2,1)S(1)}) custom-call(bf16[1040,128]{1,0:T(8,128)(2,1)S(1)} %get-tuple-element.12.a.hp, bf16[1040,128]{1,0:T(8,128)(2,1)S(1)} %collective-permute-done.b.h1, bf16[2080,128]{1,0:T(8,128)(2,1)S(1)} %collective-permute-done.1.h2, ...), custom_call_target="tpu_custom_call" | custom-call | flops 1342177280 | bytes 5242880 | tf_op jit(solution)/shard_map/early/pallas_call | solution.py:251
  48.3 1.5 %collective-permute-done.6.h4 = bf16[2080,128]{1,0:T(8,128)(2,1)} collective-permute-done((bf16[2080,128]{1,0:T(8,128)(2,1)S(1)}, bf16[2080,128]{1,0:T(8,128)(2,1)}, u32[]{:S(2)}, u32[]{:S(2)}) %collective-permute-start.6) | collective-permute-done | bytes 532512 | tf_op jit(solution)/shard_map/ppermute | solution.py:52
  49.8 0.0 copy-start
  49.8 1.3 %middle.1.hd = bf16[512,1536]{1,0:T(8,128)(2,1)S(1)} custom-call(bf16[2080,128]{1,0:T(8,128)(2,1)} %collective-permute-done.6.h4, bf16[512,1536]{1,0:T(8,128)(2,1)S(1)} %get-tuple-element.15.late_h), custom_call_target="tpu_custom_call", output_to_operand_aliasing={{}: (1, {})} | custom-call | flops 8589934592 | bytes 1048576 | tf_op jit(solution)/shard_map/middle/pallas_call | solution.py:269
  51.1 0.0 collective-permute-done.7.z4
  51.1 0.0 copy-done
  51.1 1.8 %late.1 = (f32[4,128,128]{2,1,0:T(8,128)S(1)}, f32[4,128,128]{2,1,0:T(8,128)S(1)}, bf16[1536,512]{1,0:T(8,128)(2,1)S(1)}) custom-call(s32[2,8]{1,0:T(2,128)S(1)} %bitcast.12, f32[512,512]{1,0:T(8,128)S(1)} %get-tuple-element.14.acc, bf16[512,1536]{1,0:T(8,128)(2,1)S(1)} %middle.1.hd, ...), custom_call_target="tpu_custom_call", output_to_operand_aliasing={{2}: (3, {})} | custom-call | flops 805306368 | bytes 2097152 | tf_op jit(solution)/shard_map/late/pallas_call | solution.py:283
  52.9 4.0 %all-gather = f32[8,128,128]{2,1,0:T(8,128)S(1)} all-gather(f32[4,128,128]{2,1,0:T(8,128)S(1)} %get-tuple-element.18), channel_id=2, replica_groups={{0,1},{2,3},{4,5},{6,7},{8,9},{10,11},{12,13},{14,15},{16,17},{18,19},{..., dimensions={0}, use_global_device_ids=true | all-gather | bytes 786432 | tf_op jit(solution)/shard_map/all_gather | solution.py:313
  56.9 0.7 %fusion = f32[1,1,4,128,128]{4,3,2,1,0:T(8,128)} fusion(f32[4,128,128]{2,1,0:T(8,128)S(1)} %get-tuple-element.17, f32[2,4,128,128]{3,2,1,0:T(8,128)S(1)} %bitcast.13, s32[]{:T(128)S(6)} %select_n.4), kind=kLoop, calls=%fused_computation.1 | loop fusion | flops 65536 | bytes 786436 | tf_op jit(solution)/shard_map/broadcast_in_dim | solution.py:317
  (2 shorter events, 0.1 us)
Async XLA Ops:
  1.8 15.3 %collective-permute-start.3 = (bf16[1040,128]{1,0:T(8,128)(2,1)S(1)}, bf16[1040,128]{1,0:T(8,128)(2,1)S(1)}, u32[]{:S(2)}, u32[]{:S(2)}) collective-permute-start(bf16[1040,128]{1,0:T(8,128)(2,1)S(1)} %get-tuple-element.13.a.zp), channel_id=1, source_target_pairs={{0,32},{1,225},{2,34},{3,226},{4,36},{5,228},{6,38},{7,230},{8,40}... | collective-permute-start | bytes 798728 | tf_op jit(solution)/shard_map/ppermute | solution.py:48
  13.3 7.8 %collective-permute-start = (bf16[1040,128]{1,0:T(8,128)(2,1)S(1)}, bf16[1040,128]{1,0:T(8,128)(2,1)S(1)}, u32[]{:S(2)}, u32[]{:S(2)}) collective-permute-start(bf16[1040,128]{1,0:T(8,128)(2,1)S(1)} %get-tuple-element.12.a.hp), channel_id=1, source_target_pairs={{0,2},{1,3},{2,0},{3,1},{4,6},{5,7},{6,4},{7,5},{8,10},{9,11},{10,... | collective-permute-start | bytes 798728 | tf_op jit(solution)/shard_map/ppermute | solution.py:56
  17.1 10.3 %collective-permute-start.4 = (bf16[2080,128]{1,0:T(8,128)(2,1)S(1)}, bf16[2080,128]{1,0:T(8,128)(2,1)S(1)}, u32[]{:S(2)}, u32[]{:S(2)}) collective-permute-start(bf16[2080,128]{1,0:T(8,128)(2,1)S(1)} %join.3), channel_id=1, source_target_pairs={{0,224},{1,33},{2,227},{3,35},{4,229},{5,37},{6,231},{7,39},{8,233... | collective-permute-start | bytes 1597448 | tf_op jit(solution)/shard_map/ppermute | solution.py:48
  21.1 16.1 %collective-permute-start.1 = (bf16[2080,128]{1,0:T(8,128)(2,1)S(1)}, bf16[2080,128]{1,0:T(8,128)(2,1)S(1)}, u32[]{:S(2)}, u32[]{:S(2)}) collective-permute-start(bf16[2080,128]{1,0:T(8,128)(2,1)S(1)} %join.2), channel_id=1, source_target_pairs={{0,4},{1,28},{2,6},{3,30},{4,0},{5,9},{6,2},{7,11},{8,12},{9,5},{1... | collective-permute-start | bytes 1597448 | tf_op jit(solution)/shard_map/ppermute | solution.py:52
  27.4 11.7 %collective-permute-start.5 = (bf16[2080,128]{1,0:T(8,128)(2,1)S(1)}, bf16[2080,128]{1,0:T(8,128)(2,1)S(1)}, u32[]{:S(2)}, u32[]{:S(2)}) collective-permute-start(bf16[2080,128]{1,0:T(8,128)(2,1)S(1)} %collective-permute-done.4.z2), channel_id=1, source_target_pairs={{0,32},{1,225},{2,34},{3,226},{4,36},{5,228},{6,38},{7,230},{8,40}... | collective-permute-start | bytes 1597448 | tf_op jit(solution)/shard_map/ppermute | solution.py:48
  32.0 12.2 %collective-permute-start.2 = (bf16[2080,128]{1,0:T(8,128)(2,1)S(1)}, bf16[2080,128]{1,0:T(8,128)(2,1)}, u32[]{:S(2)}, u32[]{:S(2)}) collective-permute-start(bf16[2080,128]{1,0:T(8,128)(2,1)S(1)} %join.2), channel_id=1, source_target_pairs={{0,29},{1,5},{2,31},{3,7},{4,8},{5,1},{6,10},{7,3},{8,4},{9,13},{1... | collective-permute-start | bytes 1597448 | tf_op jit(solution)/shard_map/ppermute | solution.py:52
  37.2 12.6 %collective-permute-start.6 = (bf16[2080,128]{1,0:T(8,128)(2,1)S(1)}, bf16[2080,128]{1,0:T(8,128)(2,1)}, u32[]{:S(2)}, u32[]{:S(2)}) collective-permute-start(bf16[2080,128]{1,0:T(8,128)(2,1)S(1)} %collective-permute-done.1.h2), channel_id=1, source_target_pairs={{0,29},{1,5},{2,31},{3,7},{4,8},{5,1},{6,10},{7,3},{8,4},{9,13},{1... | collective-permute-start | bytes 1597448 | tf_op jit(solution)/shard_map/ppermute | solution.py:52
  39.1 12.0 %collective-permute-start.7 = (bf16[2080,128]{1,0:T(8,128)(2,1)S(1)}, bf16[2080,128]{1,0:T(8,128)(2,1)S(1)}, u32[]{:S(2)}, u32[]{:S(2)}) collective-permute-start(bf16[2080,128]{1,0:T(8,128)(2,1)S(1)} %collective-permute-done.5.z3), channel_id=1, source_target_pairs={{0,224},{1,33},{2,227},{3,35},{4,229},{5,37},{6,231},{7,39},{8,233... | collective-permute-start | bytes 1597448 | tf_op jit(solution)/shard_map/ppermute | solution.py:48
  49.8 1.3 %copy-start = (s32[1,1,2,8]{3,2,1,0:T(2,128)S(1)}, s32[1,1,2,8]{3,2,1,0:T(2,128)}, u32[]{:S(2)}) copy-start(s32[1,1,2,8]{3,2,1,0:T(2,128)} %param.9) | copy-start | bytes 196

commit v5 on v4

v5 whole, which is shorter than its diff:
```python
import functools

import jax
import jax.numpy as jnp
from jax import lax
from jax.experimental import pallas as pl
from jax.experimental.pallas import tpu as pltpu
from jax.sharding import PartitionSpec as P

TILE = 4
NNZ = 8
WIDTH = 128
GRID = 16
HALF = 8
SPAN = TILE * WIDTH
ROWS = NNZ * WIDTH + 16
BOTH = ("row", "col")


def even_pair(n):
    return n ^ 1


def odd_pair(n):
    return ((n - 1) ^ 1) + 1


def flat_id(i, c, role):
    layer = role ^ int((i + c) % GRID >= HALF)
    return i * 2 * GRID + c * 2 + layer


def route(step):
    pairs = []
    for i in range(GRID):
        for c in range(GRID):
            for role in range(2):
                z, y, x = step(i % HALF, c // 2, c % 2, role)
                pairs.append((flat_id(i, c, role), flat_id(i // HALF * HALF + z % HALF, (y % HALF) * 2 + x, role)))
    return pairs


def pair_of(kind, n, role):
    return even_pair(n) if kind == role else odd_pair(n)


def exchange_z(x, kind):
    return lax.ppermute(x, BOTH, route(lambda z, y, xl, r: (pair_of(kind, z, r), y, xl)))


def exchange_h(x, hop):
    def step(z, y, xl, r):
        if hop == 2:
            return z, pair_of(1, y, r), xl
        if hop == 0:
            return z, y, xl ^ 1
        return z, pair_of(0, y, r), xl

    return lax.ppermute(x, BOTH, route(step))


def pack_kernel(places_z, places_h, blocks_z, blocks_h, out_z, out_h, sem):
    lane = lax.broadcasted_iota(jnp.int32, (ROWS - NNZ * WIDTH, WIDTH), 1)
    copies = []
    for n, (blocks, out) in enumerate(((blocks_z, out_z), (blocks_h, out_h))):
        copies.append(pltpu.make_async_copy(blocks, out.at[pl.ds(0, NNZ * WIDTH)], sem.at[n]))
        copies[-1].start()
    for places, out in ((places_z, out_z), (places_h, out_h)):
        slots = jnp.zeros(lane.shape, jnp.int32)
        for k in range(NNZ):
            slots = jnp.where(lane == k, places[0, k] * TILE + places[1, k], slots)
        out[pl.ds(NNZ * WIDTH, ROWS - NNZ * WIDTH), :] = slots.astype(jnp.float32).astype(out.dtype)
    for copy in copies:
        copy.wait()


PACK_LIMIT = 56 * 1024 * 1024


def pack(places_z, places_h, blocks_z, blocks_h):
    smem = pl.BlockSpec(memory_space=pltpu.SMEM)
    hbm = pl.BlockSpec(memory_space=pl.ANY)
    vmem = pl.BlockSpec(memory_space=pltpu.VMEM)
    return pl.pallas_call(
        pack_kernel,
        out_shape=(pltpu.VMEM((ROWS, WIDTH), blocks_z.dtype),) * 2,
        in_specs=[smem, smem, hbm, hbm],
        out_specs=(vmem, vmem),
        scratch_shapes=[pltpu.SemaphoreType.DMA((2,))],
        compiler_params=pltpu.CompilerParams(vmem_limit_bytes=PACK_LIMIT),
        cost_estimate=pl.CostEstimate(flops=0, bytes_accessed=ROWS * WIDTH * 8, transcendentals=0),
        name="pack",
    )(places_z, places_h, blocks_z.reshape(NNZ * WIDTH, WIDTH), blocks_h.reshape(NNZ * WIDTH, WIDTH))


def join_kernel(a, b, out):
    out[: a.shape[0], :] = a[...]
    out[a.shape[0] :, :] = b[...]


def join(a, b, tiles=0):
    vmem = pl.BlockSpec(memory_space=pltpu.VMEM)
    rows = a.shape[0] + b.shape[0]
    return pl.pallas_call(
        join_kernel,
        out_shape=jax.ShapeDtypeStruct((rows, WIDTH), a.dtype),
        in_specs=[vmem, vmem],
        out_specs=vmem,
        compiler_params=pltpu.CompilerParams(vmem_limit_bytes=4 * 1024 * 1024),
        cost_estimate=cost(tiles, rows * WIDTH * 4),
        name="join",
    )(a, b)


def near(n, kind, role):
    even = n ^ 1
    odd = ((n - 1) ^ 1) + 1
    return jnp.where(role == kind, even, odd) & 7


def position():
    i = lax.axis_index("row")
    j = lax.axis_index("col")
    c = j >> 1
    layer = j & 1
    role = layer ^ (((i + c) & 15) >> 3)
    return i & 7, c >> 1, c & 1, layer, role


def offsets():
    z, y, xl, _, role = position()
    ya = near(y, 0, role)
    yb = near(y, 1, role)
    yab = near(yb, 0, role)
    xo = xl ^ 1
    first = ((y, xl), (y, xo), (ya, xl), (ya, xo), (yb, xl), (yb, xo), (yab, xl), (yab, xo))
    def ahead(yy, xx):
        return (2 * (yy - y) + xx - xl) & 7

    of_h = [ahead(*p) for p in first]
    up = near(z, 0, role) - z
    of_z = [(up * n) & 7 for n in (0, 1, -1, -2, 2, 3, -3, 4)]
    return of_h, of_z


def turn_of(of_h, ahead):
    turn = jnp.int32(0)
    for n in range(1, HALF):
        turn = jnp.where(of_h[n] == ahead, n, turn)
    return turn


class Slots:
    def __init__(self, parts):
        self.rows = []
        for buf, part in parts:
            base = part * ROWS + NNZ * WIDTH
            self.rows.append(buf[base : base + 16, :].astype(jnp.float32).astype(jnp.int32))

    def __getitem__(self, at):
        n, k = at
        return self.rows[n][0, k]


def place(buf, part, slots, n, put):
    for k in range(NNZ):
        row = pl.multiple_of((slots[n, k] >> 2) * WIDTH, WIDTH)
        col = pl.multiple_of((slots[n, k] & 3) * WIDTH, WIDTH)
        at = part * ROWS + k * WIDTH
        put(row, col, buf[at : at + WIDTH, :])


def into_h(dense, turn):
    def put(row, col, block):
        dense[pl.ds(row, WIDTH), pl.ds(pl.multiple_of(turn * SPAN + col, WIDTH), WIDTH)] = block

    return put


def into_z(dense, turn):
    def put(row, col, block):
        dense[pl.ds(pl.multiple_of(turn * SPAN + row, WIDTH), WIDTH), pl.ds(col, WIDTH)] = block

    return put


FIRST = 4
LAST = 2


def clear(ref):
    ref[...] = jnp.zeros_like(ref)


def keep_for_last(of_h, of_z, first_turn, parts, slots, last_h):
    for n, (buf, part) in enumerate(parts):
        for m in range(LAST):

            @pl.when(of_h[first_turn + n] == of_z[HALF - LAST + m])
            def _():
                place(buf, part, slots, n, into_h(last_h, m))


def early_kernel(hp, h1, h2, zp, z1, z2, z3, acc, mid_z, last_h, hd, zd):
    h_parts = [(hp, 0), (h1, 0), (h2, 0), (h2, 1)]
    z_parts = [(zp, 0), (z1, 0), (z2, 0), (z2, 1), (z3, 0), (z3, 1)]
    slots = Slots(h_parts + z_parts)
    for ref in (hd, zd, mid_z, last_h):
        clear(ref)
    of_h, of_z = offsets()
    for n, (buf, part) in enumerate(h_parts):
        place(buf, part, slots, n, into_h(hd, n))
    keep_for_last(of_h, of_z, 0, h_parts, slots, last_h)
    for n, (buf, part) in enumerate(z_parts):
        turn = turn_of(of_h, of_z[n])

        @pl.when(turn < FIRST)
        def _():
            place(buf, part, slots, FIRST + n, into_z(zd, turn))

        @pl.when(turn >= FIRST)
        def _():
            place(buf, part, slots, FIRST + n, into_z(mid_z, turn - FIRST))

    for m in range(0, SPAN, 256):
        acc[m : m + 256, :] = jnp.dot(hd[m : m + 256, :], zd[...], preferred_element_type=jnp.float32)


def middle_kernel(h3, h4, mid_z, acc, in_h, out_acc, last_h, hd):
    parts = [(h3, 0), (h3, 1), (h4, 0), (h4, 1)]
    slots = Slots(parts)
    clear(hd)
    of_h, of_z = offsets()
    for n, (buf, part) in enumerate(parts):
        place(buf, part, slots, n, into_h(hd, n))
    keep_for_last(of_h, of_z, FIRST, parts, slots, last_h)
    for m in range(0, SPAN, 256):
        out_acc[m : m + 256, :] = acc[m : m + 256, :] + jnp.dot(
            hd[m : m + 256, :], mid_z[...], preferred_element_type=jnp.float32
        )


def late_kernel(keep, acc, last_h, z4, own, other, zd, total):
    parts = [(z4, 0), (z4, 1)]
    slots = Slots(parts)
    clear(zd)
    layer = lax.axis_index("col") & 1
    for n, (buf, part) in enumerate(parts):
        place(buf, part, slots, n, into_z(zd, n))
    for m in range(0, SPAN, 256):
        total[m : m + 256, :] = acc[m : m + 256, :] + jnp.dot(
            last_h[m : m + 256, :], zd[...], preferred_element_type=jnp.float32
        )
    for q in range(TILE):
        for dst, first in ((own, layer * TILE), (other, (1 - layer) * TILE)):
            r = pl.multiple_of(keep[0, first + q] * WIDTH, WIDTH)
            s = pl.multiple_of(keep[1, first + q] * WIDTH, WIDTH)
            dst[q] = total[pl.ds(r, WIDTH), pl.ds(s, WIDTH)]


def finish_kernel(own, both, out):
    layer = lax.axis_index("col") & 1
    out[...] = own[...] + both[pl.ds((1 - layer) * TILE, TILE)]


VMEM = pl.BlockSpec(memory_space=pltpu.VMEM)
ACC = jax.ShapeDtypeStruct((SPAN, SPAN), jnp.float32)
LAST_H = jax.ShapeDtypeStruct((SPAN, LAST * SPAN), jnp.bfloat16)
HALF_OUT = jax.ShapeDtypeStruct((TILE, WIDTH, WIDTH), jnp.float32)


def cost(tiles, moved):
    return pl.CostEstimate(flops=2 * SPAN * SPAN * SPAN * tiles, bytes_accessed=moved, transcendentals=0)


def limit(mib):
    return pltpu.CompilerParams(vmem_limit_bytes=mib * 1024 * 1024)


def wide(tiles):
    return pltpu.VMEM((SPAN, tiles * SPAN), jnp.bfloat16)


def tall(tiles):
    return pltpu.VMEM((tiles * SPAN, SPAN), jnp.bfloat16)


def early_product(*tiles):
    return pl.pallas_call(
        early_kernel,
        out_shape=(ACC, jax.ShapeDtypeStruct((FIRST * SPAN, SPAN), jnp.bfloat16), LAST_H),
        in_specs=[VMEM] * len(tiles),
        out_specs=(VMEM,) * 3,
        scratch_shapes=[wide(FIRST), tall(FIRST)],
        compiler_params=limit(14),
        cost_estimate=cost(FIRST, 4 * 1024 * 1024),
        name="early",
    )(*tiles)


def middle_product(h3, h4, mid_z, acc, last_h):
    return pl.pallas_call(
        middle_kernel,
        out_shape=(ACC, LAST_H),
        in_specs=[VMEM] * 5,
        out_specs=(VMEM,) * 2,
        input_output_aliases={3: 0, 4: 1},
        scratch_shapes=[wide(FIRST)],
        compiler_params=limit(12),
        cost_estimate=cost(MIDDLE_TILES, 1024 * 1024),
        name="middle",
    )(h3, h4, mid_z, acc, last_h)


def late_product(keep, acc, last_h, z4):
    return pl.pallas_call(
        late_kernel,
        out_shape=(HALF_OUT, HALF_OUT),
        in_specs=[pl.BlockSpec(memory_space=pltpu.SMEM)] + [VMEM] * 3,
        out_specs=(VMEM,) * 2,
        scratch_shapes=[tall(LAST), pltpu.VMEM((SPAN, SPAN), jnp.float32)],
        compiler_params=limit(10),
        cost_estimate=cost(LAST, 2 * 1024 * 1024),
        name="late",
    )(keep, acc, last_h, z4)


def finish(own, both):
    return pl.pallas_call(
        finish_kernel,
        out_shape=HALF_OUT,
        in_specs=[VMEM] * 2,
        out_specs=VMEM,
        compiler_params=limit(4),
        cost_estimate=cost(0, 1024 * 1024),
        name="finish",
    )(own, both)


MIDDLE_TILES = 8


def per_device(h_blocks, h_index, z_blocks, z_index, keep_index):
    zp, hp = pack(z_index[0, 0], h_index[0, 0], z_blocks[0, 0], h_blocks[0, 0])
    z1 = exchange_z(zp, 0)
    h1 = exchange_h(hp, 0)
    z2 = join(exchange_z(zp, 1), exchange_z(z1, 1))
    h01 = join(hp, h1)
    h2 = exchange_h(h01, 1)
    h3 = exchange_h(h01, 2)
    z3 = exchange_z(z2, 0)
    h4 = exchange_h(h2, 2)
    z4 = exchange_z(z3, 1)
    acc, mid_z, last_h = early_product(hp, h1, h2, zp, z1, z2, z3)
    acc, last_h = middle_product(h3, h4, mid_z, acc, last_h)
    own, other = late_product(keep_index[0, 0], acc, last_h, z4)
    both = lax.all_gather(
        other, "col", axis_index_groups=[[2 * c, 2 * c + 1] for c in range(GRID)], tiled=True
    )
    return finish(own, both)[None, None]


def solution(mesh):
    return jax.shard_map(
        per_device,
        mesh=mesh,
        in_specs=(
            P("row", "col", None, None, None),
            P("row", "col", None, None),
            P("row", "col", None, None, None),
            P("row", "col", None, None),
            P("row", "col", None, None),
        ),
        out_specs=P("row", "col", None, None, None),
        check_vma=False,
    )
```

time: 58.1 us -> 57.4 us (0.988)
  blocking collectives: 4.02 us -> 4.86 us
  other arithmetic: 0.73 us -> 0 us
    ppermute x4, waiting for transfers between devices: 6.66 us -> 3.06 us  [exchange_h(): return lax.ppermute(x, BOTH, route(step))]
    ppermute x4 -> x5, waiting for transfers between devices: 0.51 us -> 3.71 us  [exchange_z(): lax.ppermute(x, BOTH, route(lambda z, y, xl, r: (pair_of(kind, z, r), y,...]
    ppermute x4, starting transfers between devices: 16.7 us -> 15.6 us  [exchange_h(): return lax.ppermute(x, BOTH, route(step))]
    all_gather x1, blocking collectives: 4.02 us -> 4.86 us  [per_device(): lax.all_gather(other, 'col', axis_index_groups=[[2 * c, 2 * c + 1] for c...]
    broadcast_in_dim x1 -> x0, other arithmetic: 0.73 us -> none  [per_device(): return (own + partner)[None, None]]
    ppermute x4 -> x5, starting transfers between devices: 19.9 us -> 20.6 us  [exchange_z(): lax.ppermute(x, BOTH, route(lambda z, y, xl, r: (pair_of(kind, z, r), y,...]
    pallas_call x3 -> x4, Pallas kernels: 7.16 us -> 7.18 us  [the longest x1 3 us: early_product(): pl.pallas_call(early_kernel, out_shape=(ACC, jax.ShapeDtypeStruct((FIRST...]
  transfers between devices with their start and end apart: 8 -> 9, of which waited for: 5 -> 4; matrix products, arithmetic and copies ran while one was open for 0% -> 0% of each run, Pallas kernels for 9% -> 9%
where the time goes in v5:
time: 57.4 us; the launch traced here: 57 us
  starting transfers between devices  36.2 us (63%)
  Pallas kernels  9 us (16%)
  waiting for transfers between devices  6.77 us (12%)
  blocking collectives  4.86 us (8%)
    ppermute x5, starting transfers between devices, exchange_z(): lax.ppermute(x, BOTH, route(lambda z, y, xl, r: (pair_of(kind, z, r), y,...  20.6 us
    ppermute x4, starting transfers between devices, exchange_h(): return lax.ppermute(x, BOTH, route(step))  15.6 us
    all_gather x1, blocking collectives, per_device(): lax.all_gather(other, 'col', axis_index_groups=[[2 * c, 2 * c + 1] for c...  4.86 us
    ppermute x5, waiting for transfers between devices, exchange_z(): lax.ppermute(x, BOTH, route(lambda z, y, xl, r: (pair_of(kind, z, r), y,...  3.71 us
    ppermute x4, waiting for transfers between devices, exchange_h(): return lax.ppermute(x, BOTH, route(step))  3.06 us
    pallas_call x1, Pallas kernels, early_product(): pl.pallas_call(early_kernel, out_shape=(ACC, jax.ShapeDtypeStruct((FIRST...  3 us
    pallas_call x1, Pallas kernels, middle_product(): pl.pallas_call(middle_kernel, out_shape=(ACC, LAST_H), in_specs=[VMEM] *...  1.92 us
    pallas_call x1, Pallas kernels, pack(): pl.pallas_call(pack_kernel, out_shape=(pltpu.VMEM((ROWS, WIDTH), blocks_z...  1.75 us
  transfers between devices with their start and end apart: 9, of which 4 were waited for; matrix products, arithmetic and copies ran while one was open for 0% of the time, Pallas kernels for 9%

profile of v5, /device:TPU:1, one launch (start us, length us, event | category | flops | bytes accessed | tf_op | source)
XLA Modules:
  0.0 57.0 jit_solution(16682268135209484013)
XLA Ops:
  0.0 1.7 %pack.1 = (bf16[1040,128]{1,0:T(8,128)(2,1)S(1)}, bf16[1040,128]{1,0:T(8,128)(2,1)S(1)}) custom-call(s32[2,8]{1,0:T(2,128)} %bitcast.9, s32[2,8]{1,0:T(2,128)} %bitcast.10, bf16[1024,128]{1,0:T(8,128)(2,1)} %bitcast.7, bf16[1024,128]{1,0:T(8,128)(2,1)} %bitcast.8), custom_call_target="tpu_custom_call" | custom-call | bytes 1064960 | tf_op jit(solution)/shard_map/pack/pallas_call | solution.py:84
  1.8 11.5 %collective-permute-start.4 = (bf16[1040,128]{1,0:T(8,128)(2,1)S(1)}, bf16[1040,128]{1,0:T(8,128)(2,1)S(1)}, u32[]{:S(2)}, u32[]{:S(2)}) collective-permute-start(bf16[1040,128]{1,0:T(8,128)(2,1)S(1)} %get-tuple-element.15.zp), channel_id=1, source_target_pairs={{0,32},{1,225},{2,34},{3,226},{4,36},{5,228},{6,38},{7,230},{8,40}... | collective-permute-start | bytes 798728 | tf_op jit(solution)/shard_map/ppermute | solution.py:48
  13.3 3.7 %collective-permute-start = (bf16[1040,128]{1,0:T(8,128)(2,1)S(1)}, bf16[1040,128]{1,0:T(8,128)(2,1)S(1)}, u32[]{:S(2)}, u32[]{:S(2)}) collective-permute-start(bf16[1040,128]{1,0:T(8,128)(2,1)S(1)} %get-tuple-element.14.a.hp), channel_id=1, source_target_pairs={{0,2},{1,3},{2,0},{3,1},{4,6},{5,7},{6,4},{7,5},{8,10},{9,11},{10,... | collective-permute-start | bytes 798728 | tf_op jit(solution)/shard_map/ppermute | solution.py:59
  16.9 1.9 %collective-permute-start.5 = (bf16[1040,128]{1,0:T(8,128)(2,1)S(1)}, bf16[1040,128]{1,0:T(8,128)(2,1)S(1)}, u32[]{:S(2)}, u32[]{:S(2)}) collective-permute-start(bf16[1040,128]{1,0:T(8,128)(2,1)S(1)} %get-tuple-element.15.zp), channel_id=1, source_target_pairs={{0,224},{1,33},{2,227},{3,35},{4,229},{5,37},{6,231},{7,39},{8,233... | collective-permute-start | bytes 798728 | tf_op jit(solution)/shard_map/ppermute | solution.py:48
  18.9 0.0 collective-permute-done.4.z1
  18.9 3.4 %collective-permute-start.6 = (bf16[1040,128]{1,0:T(8,128)(2,1)S(1)}, bf16[1040,128]{1,0:T(8,128)(2,1)S(1)}, u32[]{:S(2)}, u32[]{:S(2)}) collective-permute-start(bf16[1040,128]{1,0:T(8,128)(2,1)S(1)} %collective-permute-done.4.z1), channel_id=1, source_target_pairs={{0,224},{1,33},{2,227},{3,35},{4,229},{5,37},{6,231},{7,39},{8,233... | collective-permute-start | bytes 798728 | tf_op jit(solution)/shard_map/ppermute | solution.py:48
  22.3 0.0 collective-permute-done.b.h1
  22.3 5.7 %collective-permute-start.2 = (bf16[2080,128]{1,0:T(8,128)(2,1)S(1)}, bf16[2080,128]{1,0:T(8,128)(2,1)S(1)}, u32[]{:S(2)}, u32[]{:S(2)}) collective-permute-start(bf16[2080,128]{1,0:T(8,128)(2,1)S(1)} %join.2), channel_id=1, source_target_pairs={{0,4},{1,28},{2,6},{3,30},{4,0},{5,9},{6,2},{7,11},{8,12},{9,5},{1... | collective-permute-start | bytes 1597448 | tf_op jit(solution)/shard_map/ppermute | solution.py:59
  28.0 0.0 collective-permute-done.5.a
  28.0 0.0 collective-permute-done.6.b
  28.0 1.9 %collective-permute-start.7 = (bf16[2080,128]{1,0:T(8,128)(2,1)S(1)}, bf16[2080,128]{1,0:T(8,128)(2,1)S(1)}, u32[]{:S(2)}, u32[]{:S(2)}) collective-permute-start(bf16[2080,128]{1,0:T(8,128)(2,1)S(1)} %join.3.z2), channel_id=1, source_target_pairs={{0,32},{1,225},{2,34},{3,226},{4,36},{5,228},{6,38},{7,230},{8,40}... | collective-permute-start | bytes 1597448 | tf_op jit(solution)/shard_map/ppermute | solution.py:48
  30.0 4.3 %collective-permute-start.1 = (bf16[2080,128]{1,0:T(8,128)(2,1)S(1)}, bf16[2080,128]{1,0:T(8,128)(2,1)S(1)}, u32[]{:S(2)}, u32[]{:S(2)}) collective-permute-start(bf16[2080,128]{1,0:T(8,128)(2,1)S(1)} %join.2), channel_id=1, source_target_pairs={{0,29},{1,5},{2,31},{3,7},{4,8},{5,1},{6,10},{7,3},{8,4},{9,13},{1... | collective-permute-start | bytes 1597448 | tf_op jit(solution)/shard_map/ppermute | solution.py:59
  34.3 0.6 %collective-permute-done.2.h2 = bf16[2080,128]{1,0:T(8,128)(2,1)S(1)} collective-permute-done((bf16[2080,128]{1,0:T(8,128)(2,1)S(1)}, bf16[2080,128]{1,0:T(8,128)(2,1)S(1)}, u32[]{:S(2)}, u32[]{:S(2)}) %collective-permute-start.2) | collective-permute-done | bytes 532512 | tf_op jit(solution)/shard_map/ppermute | solution.py:59
  34.9 1.9 %collective-permute-start.3 = (bf16[2080,128]{1,0:T(8,128)(2,1)S(1)}, bf16[2080,128]{1,0:T(8,128)(2,1)S(1)}, u32[]{:S(2)}, u32[]{:S(2)}) collective-permute-start(bf16[2080,128]{1,0:T(8,128)(2,1)S(1)} %collective-permute-done.2.h2), channel_id=1, source_target_pairs={{0,29},{1,5},{2,31},{3,7},{4,8},{5,1},{6,10},{7,3},{8,4},{9,13},{1... | collective-permute-start | bytes 1597448 | tf_op jit(solution)/shard_map/ppermute | solution.py:59
  36.8 2.7 %collective-permute-done.7.z3 = bf16[2080,128]{1,0:T(8,128)(2,1)S(1)} collective-permute-done((bf16[2080,128]{1,0:T(8,128)(2,1)S(1)}, bf16[2080,128]{1,0:T(8,128)(2,1)S(1)}, u32[]{:S(2)}, u32[]{:S(2)}) %collective-permute-start.7) | collective-permute-done | bytes 532512 | tf_op jit(solution)/shard_map/ppermute | solution.py:48
  39.6 1.9 %collective-permute-start.8 = (bf16[2080,128]{1,0:T(8,128)(2,1)S(1)}, bf16[2080,128]{1,0:T(8,128)(2,1)S(1)}, u32[]{:S(2)}, u32[]{:S(2)}) collective-permute-start(bf16[2080,128]{1,0:T(8,128)(2,1)S(1)} %collective-permute-done.7.z3), channel_id=1, source_target_pairs={{0,224},{1,33},{2,227},{3,35},{4,229},{5,37},{6,231},{7,39},{8,233... | collective-permute-start | bytes 1597448 | tf_op jit(solution)/shard_map/ppermute | solution.py:48
  41.5 3.0 %early.1 = (f32[512,512]{1,0:T(8,128)S(1)}, bf16[2048,512]{1,0:T(8,128)(2,1)S(1)}, bf16[512,1024]{1,0:T(8,128)(2,1)S(1)}) custom-call(bf16[1040,128]{1,0:T(8,128)(2,1)S(1)} %get-tuple-element.14.a.hp, bf16[1040,128]{1,0:T(8,128)(2,1)S(1)} %collective-permute-done.b.h1, bf16[2080,128]{1,0:T(8,128)(2,1)S(1)} %collective-permute-done.2.h2, ...), custom_call_target="tpu_custom_call" | custom-call | flops 1073741824 | bytes 4194304 | tf_op jit(solution)/shard_map/early/pallas_call | solution.py:289
  44.5 0.0 collective-permute-done.1.h3
  44.5 2.5 %collective-permute-done.3.h4 = bf16[2080,128]{1,0:T(8,128)(2,1)S(1)} collective-permute-done((bf16[2080,128]{1,0:T(8,128)(2,1)S(1)}, bf16[2080,128]{1,0:T(8,128)(2,1)S(1)}, u32[]{:S(2)}, u32[]{:S(2)}) %collective-permute-start.3) | collective-permute-done | bytes 532512 | tf_op jit(solution)/shard_map/ppermute | solution.py:59
  47.0 1.9 %middle.1 = (f32[512,512]{1,0:T(8,128)S(1)}, bf16[512,1024]{1,0:T(8,128)(2,1)S(1)}) custom-call(bf16[2080,128]{1,0:T(8,128)(2,1)S(1)} %collective-permute-done.1.h3, bf16[2080,128]{1,0:T(8,128)(2,1)S(1)} %collective-permute-done.3.h4, bf16[2048,512]{1,0:T(8,128)(2,1)S(1)} %get-tuple-element.16.mid_z, ...), custom_call_target="tpu_custom_call", output_to_operand_aliasing={{0}: (3, {}), {1}: (4, {})} | custom-call | flops 2147483648 | bytes 1048576 | tf_op jit(solution)/shard_map/middle/pallas_call | solution.py:302
  48.9 1.0 %collective-permute-done.8.z4 = bf16[2080,128]{1,0:T(8,128)(2,1)S(1)} collective-permute-done((bf16[2080,128]{1,0:T(8,128)(2,1)S(1)}, bf16[2080,128]{1,0:T(8,128)(2,1)S(1)}, u32[]{:S(2)}, u32[]{:S(2)}) %collective-permute-start.8) | collective-permute-done | bytes 532512 | tf_op jit(solution)/shard_map/ppermute | solution.py:48
  49.9 1.5 %late.1 = (f32[4,128,128]{2,1,0:T(8,128)S(1)}, f32[4,128,128]{2,1,0:T(8,128)S(1)}) custom-call(s32[2,8]{1,0:T(2,128)S(1)} %bitcast.6, f32[512,512]{1,0:T(8,128)S(1)} %get-tuple-element.19.acc, bf16[512,1024]{1,0:T(8,128)(2,1)S(1)} %get-tuple-element.20.last_h, bf16[2080,128]{1,0:T(8,128)(2,1)S(1)} %collective-permute-done.8.z4), custom_call_target="tpu_custom_call" | custom-call | flops 536870912 | bytes 2097152 | tf_op jit(solution)/shard_map/late/pallas_call | solution.py:316
  51.4 4.9 %all_gather.3.both = f32[8,128,128]{2,1,0:T(8,128)S(1)} all-gather(f32[4,128,128]{2,1,0:T(8,128)S(1)} %get-tuple-element.22), channel_id=1, replica_groups={{0,1},{2,3},{4,5},{6,7},{8,9},{10,11},{12,13},{14,15},{16,17},{18,19},{..., dimensions={0}, use_global_device_ids=true | all-gather | bytes 786432 | tf_op jit(solution)/shard_map/all_gather | solution.py:357
  56.3 0.7 %finish.1 = f32[4,128,128]{2,1,0:T(8,128)} custom-call(f32[4,128,128]{2,1,0:T(8,128)S(1)} %get-tuple-element.21.own, f32[8,128,128]{2,1,0:T(8,128)S(1)} %all_gather.3.both), custom_call_target="tpu_custom_call" | custom-call | bytes 1048576 | tf_op jit(solution)/shard_map/finish/pallas_call | solution.py:329
  (4 shorter events, 0.1 us)
Async XLA Ops:
  1.8 17.1 %collective-permute-start.4 = (bf16[1040,128]{1,0:T(8,128)(2,1)S(1)}, bf16[1040,128]{1,0:T(8,128)(2,1)S(1)}, u32[]{:S(2)}, u32[]{:S(2)}) collective-permute-start(bf16[1040,128]{1,0:T(8,128)(2,1)S(1)} %get-tuple-element.15.zp), channel_id=1, source_target_pairs={{0,32},{1,225},{2,34},{3,226},{4,36},{5,228},{6,38},{7,230},{8,40}... | collective-permute-start | bytes 798728 | tf_op jit(solution)/shard_map/ppermute | solution.py:48
  13.3 9.0 %collective-permute-start = (bf16[1040,128]{1,0:T(8,128)(2,1)S(1)}, bf16[1040,128]{1,0:T(8,128)(2,1)S(1)}, u32[]{:S(2)}, u32[]{:S(2)}) collective-permute-start(bf16[1040,128]{1,0:T(8,128)(2,1)S(1)} %get-tuple-element.14.a.hp), channel_id=1, source_target_pairs={{0,2},{1,3},{2,0},{3,1},{4,6},{5,7},{6,4},{7,5},{8,10},{9,11},{10,... | collective-permute-start | bytes 798728 | tf_op jit(solution)/shard_map/ppermute | solution.py:59
  16.9 11.0 %collective-permute-start.5 = (bf16[1040,128]{1,0:T(8,128)(2,1)S(1)}, bf16[1040,128]{1,0:T(8,128)(2,1)S(1)}, u32[]{:S(2)}, u32[]{:S(2)}) collective-permute-start(bf16[1040,128]{1,0:T(8,128)(2,1)S(1)} %get-tuple-element.15.zp), channel_id=1, source_target_pairs={{0,224},{1,33},{2,227},{3,35},{4,229},{5,37},{6,231},{7,39},{8,233... | collective-permute-start | bytes 798728 | tf_op jit(solution)/shard_map/ppermute | solution.py:48
  18.9 9.1 %collective-permute-start.6 = (bf16[1040,128]{1,0:T(8,128)(2,1)S(1)}, bf16[1040,128]{1,0:T(8,128)(2,1)S(1)}, u32[]{:S(2)}, u32[]{:S(2)}) collective-permute-start(bf16[1040,128]{1,0:T(8,128)(2,1)S(1)} %collective-permute-done.4.z1), channel_id=1, source_target_pairs={{0,224},{1,33},{2,227},{3,35},{4,229},{5,37},{6,231},{7,39},{8,233... | collective-permute-start | bytes 798728 | tf_op jit(solution)/shard_map/ppermute | solution.py:48
  22.3 12.6 %collective-permute-start.2 = (bf16[2080,128]{1,0:T(8,128)(2,1)S(1)}, bf16[2080,128]{1,0:T(8,128)(2,1)S(1)}, u32[]{:S(2)}, u32[]{:S(2)}) collective-permute-start(bf16[2080,128]{1,0:T(8,128)(2,1)S(1)} %join.2), channel_id=1, source_target_pairs={{0,4},{1,28},{2,6},{3,30},{4,0},{5,9},{6,2},{7,11},{8,12},{9,5},{1... | collective-permute-start | bytes 1597448 | tf_op jit(solution)/shard_map/ppermute | solution.py:59
  28.0 11.5 %collective-permute-start.7 = (bf16[2080,128]{1,0:T(8,128)(2,1)S(1)}, bf16[2080,128]{1,0:T(8,128)(2,1)S(1)}, u32[]{:S(2)}, u32[]{:S(2)}) collective-permute-start(bf16[2080,128]{1,0:T(8,128)(2,1)S(1)} %join.3.z2), channel_id=1, source_target_pairs={{0,32},{1,225},{2,34},{3,226},{4,36},{5,228},{6,38},{7,230},{8,40}... | collective-permute-start | bytes 1597448 | tf_op jit(solution)/shard_map/ppermute | solution.py:48
  30.0 14.5 %collective-permute-start.1 = (bf16[2080,128]{1,0:T(8,128)(2,1)S(1)}, bf16[2080,128]{1,0:T(8,128)(2,1)S(1)}, u32[]{:S(2)}, u32[]{:S(2)}) collective-permute-start(bf16[2080,128]{1,0:T(8,128)(2,1)S(1)} %join.2), channel_id=1, source_target_pairs={{0,29},{1,5},{2,31},{3,7},{4,8},{5,1},{6,10},{7,3},{8,4},{9,13},{1... | collective-permute-start | bytes 1597448 | tf_op jit(solution)/shard_map/ppermute | solution.py:59
  34.9 12.0 %collective-permute-start.3 = (bf16[2080,128]{1,0:T(8,128)(2,1)S(1)}, bf16[2080,128]{1,0:T(8,128)(2,1)S(1)}, u32[]{:S(2)}, u32[]{:S(2)}) collective-permute-start(bf16[2080,128]{1,0:T(8,128)(2,1)S(1)} %collective-permute-done.2.h2), channel_id=1, source_target_pairs={{0,29},{1,5},{2,31},{3,7},{4,8},{5,1},{6,10},{7,3},{8,4},{9,13},{1... | collective-permute-start | bytes 1597448 | tf_op jit(solution)/shard_map/ppermute | solution.py:59
  39.6 10.3 %collective-permute-start.8 = (bf16[2080,128]{1,0:T(8,128)(2,1)S(1)}, bf16[2080,128]{1,0:T(8,128)(2,1)S(1)}, u32[]{:S(2)}, u32[]{:S(2)}) collective-permute-start(bf16[2080,128]{1,0:T(8,128)(2,1)S(1)} %collective-permute-done.7.z3), channel_id=1, source_target_pairs={{0,224},{1,33},{2,227},{3,35},{4,229},{5,37},{6,231},{7,39},{8,233... | collective-permute-start | bytes 1597448 | tf_op jit(solution)/shard_map/ppermute | solution.py:48
  47.0 2.9 %copy-start = (s32[1,1,2,8]{3,2,1,0:T(2,128)S(1)}, s32[1,1,2,8]{3,2,1,0:T(2,128)}, u32[]{:S(2)}) copy-start(s32[1,1,2,8]{3,2,1,0:T(2,128)} %param.9) | copy-start | bytes 196

commit v6 on v5

--- a/solution.py
+++ b/solution.py
@@ -59,16 +59,20 @@
     return lax.ppermute(x, BOTH, route(step))
 
 
-def pack_kernel(places_z, places_h, blocks_z, blocks_h, out_z, out_h, sem):
+def pack_kernel(places_z, places_h, blocks_z, blocks_h, out_z, out_h, seen, sem):
     lane = lax.broadcasted_iota(jnp.int32, (ROWS - NNZ * WIDTH, WIDTH), 1)
     copies = []
     for n, (blocks, out) in enumerate(((blocks_z, out_z), (blocks_h, out_h))):
         copies.append(pltpu.make_async_copy(blocks, out.at[pl.ds(0, NNZ * WIDTH)], sem.at[n]))
         copies[-1].start()
-    for places, out in ((places_z, out_z), (places_h, out_h)):
+    lists = [pltpu.make_async_copy(p, seen.at[n], sem.at[2 + n]) for n, p in enumerate((places_z, places_h))]
+    for copy in lists:
+        copy.start()
+    for n, out in enumerate((out_z, out_h)):
+        lists[n].wait()
         slots = jnp.zeros(lane.shape, jnp.int32)
         for k in range(NNZ):
-            slots = jnp.where(lane == k, places[0, k] * TILE + places[1, k], slots)
+            slots = jnp.where(lane == k, seen[n, 0, k] * TILE + seen[n, 1, k], slots)
         out[pl.ds(NNZ * WIDTH, ROWS - NNZ * WIDTH), :] = slots.astype(jnp.float32).astype(out.dtype)
     for copy in copies:
         copy.wait()
@@ -78,15 +82,14 @@
 
 
 def pack(places_z, places_h, blocks_z, blocks_h):
-    smem = pl.BlockSpec(memory_space=pltpu.SMEM)
     hbm = pl.BlockSpec(memory_space=pl.ANY)
     vmem = pl.BlockSpec(memory_space=pltpu.VMEM)
     return pl.pallas_call(
         pack_kernel,
         out_shape=(pltpu.VMEM((ROWS, WIDTH), blocks_z.dtype),) * 2,
-        in_specs=[smem, smem, hbm, hbm],
+        in_specs=[hbm] * 4,
         out_specs=(vmem, vmem),
-        scratch_shapes=[pltpu.SemaphoreType.DMA((2,))],
+        scratch_shapes=[pltpu.SMEM((2, 2, NNZ), jnp.int32), pltpu.SemaphoreType.DMA((4,))],
         compiler_params=pltpu.CompilerParams(vmem_limit_bytes=PACK_LIMIT),
         cost_estimate=pl.CostEstimate(flops=0, bytes_accessed=ROWS * WIDTH * 8, transcendentals=0),
         name="pack",
@@ -240,7 +243,9 @@
         )
 
 
-def late_kernel(keep, acc, last_h, z4, own, other, zd, total):
+def late_kernel(keep_list, acc, last_h, z4, own, other, zd, total, keep, sem):
+    copy = pltpu.make_async_copy(keep_list, keep, sem)
+    copy.start()
     parts = [(z4, 0), (z4, 1)]
     slots = Slots(parts)
     clear(zd)
@@ -251,6 +256,7 @@
         total[m : m + 256, :] = acc[m : m + 256, :] + jnp.dot(
             last_h[m : m + 256, :], zd[...], preferred_element_type=jnp.float32
         )
+    copy.wait()
     for q in range(TILE):
         for dst, first in ((own, layer * TILE), (other, (1 - layer) * TILE)):
             r = pl.multiple_of(keep[0, first + q] * WIDTH, WIDTH)
@@ -316,9 +322,14 @@
     return pl.pallas_call(
         late_kernel,
         out_shape=(HALF_OUT, HALF_OUT),
-        in_specs=[pl.BlockSpec(memory_space=pltpu.SMEM)] + [VMEM] * 3,
+        in_specs=[pl.BlockSpec(memory_space=pl.ANY)] + [VMEM] * 3,
         out_specs=(VMEM,) * 2,
-        scratch_shapes=[tall(LAST), pltpu.VMEM((SPAN, SPAN), jnp.float32)],
+        scratch_shapes=[
+            tall(LAST),
+            pltpu.VMEM((SPAN, SPAN), jnp.float32),
+            pltpu.SMEM((2, NNZ), jnp.int32),
+            pltpu.SemaphoreType.DMA,
+        ],
         compiler_params=limit(10),
         cost_estimate=cost(LAST, 2 * 1024 * 1024),
         name="late",

time: 57.4 us -> 56.1 us (0.977)
  Pallas kernels: 9 us -> 7.8 us
    pallas_call x1, Pallas kernels: 1.75 us -> 1.06 us  [pack(): pl.pallas_call(pack_kernel, out_shape=(pltpu.VMEM((ROWS, WIDTH), blocks_z...]
where the time goes in v6:
time: 56.1 us; the launch traced here: 55.8 us
  starting transfers between devices  36.2 us (65%)
  Pallas kernels  7.8 us (14%)
  waiting for transfers between devices  6.76 us (12%)
  blocking collectives  4.86 us (9%)
    ppermute x5, starting transfers between devices, exchange_z(): lax.ppermute(x, BOTH, route(lambda z, y, xl, r: (pair_of(kind, z, r), y,...  20.6 us
    ppermute x4, starting transfers between devices, exchange_h(): return lax.ppermute(x, BOTH, route(step))  15.6 us
    all_gather x1, blocking collectives, per_device(): lax.all_gather(other, 'col', axis_index_groups=[[2 * c, 2 * c + 1] for c...  4.86 us
    ppermute x5, waiting for transfers between devices, exchange_z(): lax.ppermute(x, BOTH, route(lambda z, y, xl, r: (pair_of(kind, z, r), y,...  3.7 us
    ppermute x4, waiting for transfers between devices, exchange_h(): return lax.ppermute(x, BOTH, route(step))  3.06 us
    pallas_call x1, Pallas kernels, early_product(): pl.pallas_call(early_kernel, out_shape=(ACC, jax.ShapeDtypeStruct((FIRST...  3.01 us
    pallas_call x1, Pallas kernels, middle_product(): pl.pallas_call(middle_kernel, out_shape=(ACC, LAST_H), in_specs=[VMEM] *...  1.92 us
  transfers between devices with their start and end apart: 9, of which 4 were waited for; matrix products, arithmetic and copies ran while one was open for 0% of the time, Pallas kernels for 9%

profile of v6, /device:TPU:1, one launch (start us, length us, event | category | flops | bytes accessed | tf_op | source)
XLA Modules:
  0.0 55.8 jit_solution(14237427825534176743)
XLA Ops:
  0.0 1.1 %pack.1 = (bf16[1040,128]{1,0:T(8,128)(2,1)S(1)}, bf16[1040,128]{1,0:T(8,128)(2,1)S(1)}) custom-call(s32[2,8]{1,0:T(2,128)} %bitcast.9, s32[2,8]{1,0:T(2,128)} %bitcast.10, bf16[1024,128]{1,0:T(8,128)(2,1)} %bitcast.7, bf16[1024,128]{1,0:T(8,128)(2,1)} %bitcast.8), custom_call_target="tpu_custom_call" | custom-call | bytes 1064960 | tf_op jit(solution)/shard_map/pack/pallas_call | solution.py:87
  1.1 11.5 %collective-permute-start.4 = (bf16[1040,128]{1,0:T(8,128)(2,1)S(1)}, bf16[1040,128]{1,0:T(8,128)(2,1)S(1)}, u32[]{:S(2)}, u32[]{:S(2)}) collective-permute-start(bf16[1040,128]{1,0:T(8,128)(2,1)S(1)} %get-tuple-element.15.zp), channel_id=1, source_target_pairs={{0,32},{1,225},{2,34},{3,226},{4,36},{5,228},{6,38},{7,230},{8,40}... | collective-permute-start | bytes 798728 | tf_op jit(solution)/shard_map/ppermute | solution.py:48
  12.6 3.7 %collective-permute-start = (bf16[1040,128]{1,0:T(8,128)(2,1)S(1)}, bf16[1040,128]{1,0:T(8,128)(2,1)S(1)}, u32[]{:S(2)}, u32[]{:S(2)}) collective-permute-start(bf16[1040,128]{1,0:T(8,128)(2,1)S(1)} %get-tuple-element.14.a.hp), channel_id=1, source_target_pairs={{0,2},{1,3},{2,0},{3,1},{4,6},{5,7},{6,4},{7,5},{8,10},{9,11},{10,... | collective-permute-start | bytes 798728 | tf_op jit(solution)/shard_map/ppermute | solution.py:59
  16.3 1.9 %collective-permute-start.5 = (bf16[1040,128]{1,0:T(8,128)(2,1)S(1)}, bf16[1040,128]{1,0:T(8,128)(2,1)S(1)}, u32[]{:S(2)}, u32[]{:S(2)}) collective-permute-start(bf16[1040,128]{1,0:T(8,128)(2,1)S(1)} %get-tuple-element.15.zp), channel_id=1, source_target_pairs={{0,224},{1,33},{2,227},{3,35},{4,229},{5,37},{6,231},{7,39},{8,233... | collective-permute-start | bytes 798728 | tf_op jit(solution)/shard_map/ppermute | solution.py:48
  18.2 0.0 collective-permute-done.4.z1
  18.2 3.4 %collective-permute-start.6 = (bf16[1040,128]{1,0:T(8,128)(2,1)S(1)}, bf16[1040,128]{1,0:T(8,128)(2,1)S(1)}, u32[]{:S(2)}, u32[]{:S(2)}) collective-permute-start(bf16[1040,128]{1,0:T(8,128)(2,1)S(1)} %collective-permute-done.4.z1), channel_id=1, source_target_pairs={{0,224},{1,33},{2,227},{3,35},{4,229},{5,37},{6,231},{7,39},{8,233... | collective-permute-start | bytes 798728 | tf_op jit(solution)/shard_map/ppermute | solution.py:48
  21.6 0.0 collective-permute-done.b.h1
  21.6 5.7 %collective-permute-start.2 = (bf16[2080,128]{1,0:T(8,128)(2,1)S(1)}, bf16[2080,128]{1,0:T(8,128)(2,1)S(1)}, u32[]{:S(2)}, u32[]{:S(2)}) collective-permute-start(bf16[2080,128]{1,0:T(8,128)(2,1)S(1)} %join.2), channel_id=1, source_target_pairs={{0,4},{1,28},{2,6},{3,30},{4,0},{5,9},{6,2},{7,11},{8,12},{9,5},{1... | collective-permute-start | bytes 1597448 | tf_op jit(solution)/shard_map/ppermute | solution.py:59
  27.3 0.0 collective-permute-done.5.a
  27.3 0.0 collective-permute-done.6.b
  27.4 1.9 %collective-permute-start.7 = (bf16[2080,128]{1,0:T(8,128)(2,1)S(1)}, bf16[2080,128]{1,0:T(8,128)(2,1)S(1)}, u32[]{:S(2)}, u32[]{:S(2)}) collective-permute-start(bf16[2080,128]{1,0:T(8,128)(2,1)S(1)} %join.3.z2), channel_id=1, source_target_pairs={{0,32},{1,225},{2,34},{3,226},{4,36},{5,228},{6,38},{7,230},{8,40}... | collective-permute-start | bytes 1597448 | tf_op jit(solution)/shard_map/ppermute | solution.py:48
  29.3 4.3 %collective-permute-start.1 = (bf16[2080,128]{1,0:T(8,128)(2,1)S(1)}, bf16[2080,128]{1,0:T(8,128)(2,1)S(1)}, u32[]{:S(2)}, u32[]{:S(2)}) collective-permute-start(bf16[2080,128]{1,0:T(8,128)(2,1)S(1)} %join.2), channel_id=1, source_target_pairs={{0,29},{1,5},{2,31},{3,7},{4,8},{5,1},{6,10},{7,3},{8,4},{9,13},{1... | collective-permute-start | bytes 1597448 | tf_op jit(solution)/shard_map/ppermute | solution.py:59
  33.6 0.6 %collective-permute-done.2.h2 = bf16[2080,128]{1,0:T(8,128)(2,1)S(1)} collective-permute-done((bf16[2080,128]{1,0:T(8,128)(2,1)S(1)}, bf16[2080,128]{1,0:T(8,128)(2,1)S(1)}, u32[]{:S(2)}, u32[]{:S(2)}) %collective-permute-start.2) | collective-permute-done | bytes 532512 | tf_op jit(solution)/shard_map/ppermute | solution.py:59
  34.2 1.9 %collective-permute-start.3 = (bf16[2080,128]{1,0:T(8,128)(2,1)S(1)}, bf16[2080,128]{1,0:T(8,128)(2,1)S(1)}, u32[]{:S(2)}, u32[]{:S(2)}) collective-permute-start(bf16[2080,128]{1,0:T(8,128)(2,1)S(1)} %collective-permute-done.2.h2), channel_id=1, source_target_pairs={{0,29},{1,5},{2,31},{3,7},{4,8},{5,1},{6,10},{7,3},{8,4},{9,13},{1... | collective-permute-start | bytes 1597448 | tf_op jit(solution)/shard_map/ppermute | solution.py:59
  36.1 2.7 %collective-permute-done.7.z3 = bf16[2080,128]{1,0:T(8,128)(2,1)S(1)} collective-permute-done((bf16[2080,128]{1,0:T(8,128)(2,1)S(1)}, bf16[2080,128]{1,0:T(8,128)(2,1)S(1)}, u32[]{:S(2)}, u32[]{:S(2)}) %collective-permute-start.7) | collective-permute-done | bytes 532512 | tf_op jit(solution)/shard_map/ppermute | solution.py:48
  38.9 1.9 %collective-permute-start.8 = (bf16[2080,128]{1,0:T(8,128)(2,1)S(1)}, bf16[2080,128]{1,0:T(8,128)(2,1)S(1)}, u32[]{:S(2)}, u32[]{:S(2)}) collective-permute-start(bf16[2080,128]{1,0:T(8,128)(2,1)S(1)} %collective-permute-done.7.z3), channel_id=1, source_target_pairs={{0,224},{1,33},{2,227},{3,35},{4,229},{5,37},{6,231},{7,39},{8,233... | collective-permute-start | bytes 1597448 | tf_op jit(solution)/shard_map/ppermute | solution.py:48
  40.8 3.0 %early.1 = (f32[512,512]{1,0:T(8,128)S(1)}, bf16[2048,512]{1,0:T(8,128)(2,1)S(1)}, bf16[512,1024]{1,0:T(8,128)(2,1)S(1)}) custom-call(bf16[1040,128]{1,0:T(8,128)(2,1)S(1)} %get-tuple-element.14.a.hp, bf16[1040,128]{1,0:T(8,128)(2,1)S(1)} %collective-permute-done.b.h1, bf16[2080,128]{1,0:T(8,128)(2,1)S(1)} %collective-permute-done.2.h2, ...), custom_call_target="tpu_custom_call" | custom-call | flops 1073741824 | bytes 4194304 | tf_op jit(solution)/shard_map/early/pallas_call | solution.py:295
  43.8 0.0 collective-permute-done.1.h3
  43.8 2.5 %collective-permute-done.3.h4 = bf16[2080,128]{1,0:T(8,128)(2,1)S(1)} collective-permute-done((bf16[2080,128]{1,0:T(8,128)(2,1)S(1)}, bf16[2080,128]{1,0:T(8,128)(2,1)S(1)}, u32[]{:S(2)}, u32[]{:S(2)}) %collective-permute-start.3) | collective-permute-done | bytes 532512 | tf_op jit(solution)/shard_map/ppermute | solution.py:59
  46.3 1.9 %middle.1 = (f32[512,512]{1,0:T(8,128)S(1)}, bf16[512,1024]{1,0:T(8,128)(2,1)S(1)}) custom-call(bf16[2080,128]{1,0:T(8,128)(2,1)S(1)} %collective-permute-done.1.h3, bf16[2080,128]{1,0:T(8,128)(2,1)S(1)} %collective-permute-done.3.h4, bf16[2048,512]{1,0:T(8,128)(2,1)S(1)} %get-tuple-element.16.mid_z, ...), custom_call_target="tpu_custom_call", output_to_operand_aliasing={{0}: (3, {}), {1}: (4, {})} | custom-call | flops 2147483648 | bytes 1048576 | tf_op jit(solution)/shard_map/middle/pallas_call | solution.py:308
  48.2 1.0 %collective-permute-done.8.z4 = bf16[2080,128]{1,0:T(8,128)(2,1)S(1)} collective-permute-done((bf16[2080,128]{1,0:T(8,128)(2,1)S(1)}, bf16[2080,128]{1,0:T(8,128)(2,1)S(1)}, u32[]{:S(2)}, u32[]{:S(2)}) %collective-permute-start.8) | collective-permute-done | bytes 532512 | tf_op jit(solution)/shard_map/ppermute | solution.py:48
  49.2 1.0 %late.1 = (f32[4,128,128]{2,1,0:T(8,128)S(1)}, f32[4,128,128]{2,1,0:T(8,128)S(1)}) custom-call(s32[2,8]{1,0:T(2,128)S(1)} %bitcast.6, f32[512,512]{1,0:T(8,128)S(1)} %get-tuple-element.19.acc, bf16[512,1024]{1,0:T(8,128)(2,1)S(1)} %get-tuple-element.20.last_h, bf16[2080,128]{1,0:T(8,128)(2,1)S(1)} %collective-permute-done.8.z4), custom_call_target="tpu_custom_call" | custom-call | flops 536870912 | bytes 2097152 | tf_op jit(solution)/shard_map/late/pallas_call | solution.py:322
  50.2 4.9 %all_gather.3.both = f32[8,128,128]{2,1,0:T(8,128)S(1)} all-gather(f32[4,128,128]{2,1,0:T(8,128)S(1)} %get-tuple-element.22), channel_id=1, replica_groups={{0,1},{2,3},{4,5},{6,7},{8,9},{10,11},{12,13},{14,15},{16,17},{18,19},{..., dimensions={0}, use_global_device_ids=true | all-gather | bytes 786432 | tf_op jit(solution)/shard_map/all_gather | solution.py:368
  55.1 0.7 %finish.1 = f32[4,128,128]{2,1,0:T(8,128)} custom-call(f32[4,128,128]{2,1,0:T(8,128)S(1)} %get-tuple-element.21.own, f32[8,128,128]{2,1,0:T(8,128)S(1)} %all_gather.3.both), custom_call_target="tpu_custom_call" | custom-call | bytes 1048576 | tf_op jit(solution)/shard_map/finish/pallas_call | solution.py:340
  (4 shorter events, 0.1 us)
Async XLA Ops:
  1.1 17.1 %collective-permute-start.4 = (bf16[1040,128]{1,0:T(8,128)(2,1)S(1)}, bf16[1040,128]{1,0:T(8,128)(2,1)S(1)}, u32[]{:S(2)}, u32[]{:S(2)}) collective-permute-start(bf16[1040,128]{1,0:T(8,128)(2,1)S(1)} %get-tuple-element.15.zp), channel_id=1, source_target_pairs={{0,32},{1,225},{2,34},{3,226},{4,36},{5,228},{6,38},{7,230},{8,40}... | collective-permute-start | bytes 798728 | tf_op jit(solution)/shard_map/ppermute | solution.py:48
  12.6 9.0 %collective-permute-start = (bf16[1040,128]{1,0:T(8,128)(2,1)S(1)}, bf16[1040,128]{1,0:T(8,128)(2,1)S(1)}, u32[]{:S(2)}, u32[]{:S(2)}) collective-permute-start(bf16[1040,128]{1,0:T(8,128)(2,1)S(1)} %get-tuple-element.14.a.hp), channel_id=1, source_target_pairs={{0,2},{1,3},{2,0},{3,1},{4,6},{5,7},{6,4},{7,5},{8,10},{9,11},{10,... | collective-permute-start | bytes 798728 | tf_op jit(solution)/shard_map/ppermute | solution.py:59
  16.3 11.0 %collective-permute-start.5 = (bf16[1040,128]{1,0:T(8,128)(2,1)S(1)}, bf16[1040,128]{1,0:T(8,128)(2,1)S(1)}, u32[]{:S(2)}, u32[]{:S(2)}) collective-permute-start(bf16[1040,128]{1,0:T(8,128)(2,1)S(1)} %get-tuple-element.15.zp), channel_id=1, source_target_pairs={{0,224},{1,33},{2,227},{3,35},{4,229},{5,37},{6,231},{7,39},{8,233... | collective-permute-start | bytes 798728 | tf_op jit(solution)/shard_map/ppermute | solution.py:48
  18.2 9.1 %collective-permute-start.6 = (bf16[1040,128]{1,0:T(8,128)(2,1)S(1)}, bf16[1040,128]{1,0:T(8,128)(2,1)S(1)}, u32[]{:S(2)}, u32[]{:S(2)}) collective-permute-start(bf16[1040,128]{1,0:T(8,128)(2,1)S(1)} %collective-permute-done.4.z1), channel_id=1, source_target_pairs={{0,224},{1,33},{2,227},{3,35},{4,229},{5,37},{6,231},{7,39},{8,233... | collective-permute-start | bytes 798728 | tf_op jit(solution)/shard_map/ppermute | solution.py:48
  21.6 12.6 %collective-permute-start.2 = (bf16[2080,128]{1,0:T(8,128)(2,1)S(1)}, bf16[2080,128]{1,0:T(8,128)(2,1)S(1)}, u32[]{:S(2)}, u32[]{:S(2)}) collective-permute-start(bf16[2080,128]{1,0:T(8,128)(2,1)S(1)} %join.2), channel_id=1, source_target_pairs={{0,4},{1,28},{2,6},{3,30},{4,0},{5,9},{6,2},{7,11},{8,12},{9,5},{1... | collective-permute-start | bytes 1597448 | tf_op jit(solution)/shard_map/ppermute | solution.py:59
  27.4 11.5 %collective-permute-start.7 = (bf16[2080,128]{1,0:T(8,128)(2,1)S(1)}, bf16[2080,128]{1,0:T(8,128)(2,1)S(1)}, u32[]{:S(2)}, u32[]{:S(2)}) collective-permute-start(bf16[2080,128]{1,0:T(8,128)(2,1)S(1)} %join.3.z2), channel_id=1, source_target_pairs={{0,32},{1,225},{2,34},{3,226},{4,36},{5,228},{6,38},{7,230},{8,40}... | collective-permute-start | bytes 1597448 | tf_op jit(solution)/shard_map/ppermute | solution.py:48
  29.3 14.5 %collective-permute-start.1 = (bf16[2080,128]{1,0:T(8,128)(2,1)S(1)}, bf16[2080,128]{1,0:T(8,128)(2,1)S(1)}, u32[]{:S(2)}, u32[]{:S(2)}) collective-permute-start(bf16[2080,128]{1,0:T(8,128)(2,1)S(1)} %join.2), channel_id=1, source_target_pairs={{0,29},{1,5},{2,31},{3,7},{4,8},{5,1},{6,10},{7,3},{8,4},{9,13},{1... | collective-permute-start | bytes 1597448 | tf_op jit(solution)/shard_map/ppermute | solution.py:59
  34.2 12.0 %collective-permute-start.3 = (bf16[2080,128]{1,0:T(8,128)(2,1)S(1)}, bf16[2080,128]{1,0:T(8,128)(2,1)S(1)}, u32[]{:S(2)}, u32[]{:S(2)}) collective-permute-start(bf16[2080,128]{1,0:T(8,128)(2,1)S(1)} %collective-permute-done.2.h2), channel_id=1, source_target_pairs={{0,29},{1,5},{2,31},{3,7},{4,8},{5,1},{6,10},{7,3},{8,4},{9,13},{1... | collective-permute-start | bytes 1597448 | tf_op jit(solution)/shard_map/ppermute | solution.py:59
  38.9 10.3 %collective-permute-start.8 = (bf16[2080,128]{1,0:T(8,128)(2,1)S(1)}, bf16[2080,128]{1,0:T(8,128)(2,1)S(1)}, u32[]{:S(2)}, u32[]{:S(2)}) collective-permute-start(bf16[2080,128]{1,0:T(8,128)(2,1)S(1)} %collective-permute-done.7.z3), channel_id=1, source_target_pairs={{0,224},{1,33},{2,227},{3,35},{4,229},{5,37},{6,231},{7,39},{8,233... | collective-permute-start | bytes 1597448 | tf_op jit(solution)/shard_map/ppermute | solution.py:48
  46.3 2.9 %copy-start = (s32[1,1,2,8]{3,2,1,0:T(2,128)S(1)}, s32[1,1,2,8]{3,2,1,0:T(2,128)}, u32[]{:S(2)}) copy-start(s32[1,1,2,8]{3,2,1,0:T(2,128)} %param.9) | copy-start | bytes 196

commit v7 on v6

--- a/solution.py
+++ b/solution.py
@@ -45,7 +45,7 @@
 
 
 def exchange_z(x, kind):
-    return lax.ppermute(x, BOTH, route(lambda z, y, xl, r: (pair_of(kind, z, r), y, xl)))
+    return lax.ppermute(x, BOTH, route(lambda z, y, xl, r: (pair_of(1 - kind, z, r), y, xl)))
 
 
 def exchange_h(x, hop):
@@ -141,7 +141,7 @@
         return (2 * (yy - y) + xx - xl) & 7
 
     of_h = [ahead(*p) for p in first]
-    up = near(z, 0, role) - z
+    up = near(z, 1, role) - z
     of_z = [(up * n) & 7 for n in (0, 1, -1, -2, 2, 3, -3, 4)]
     return of_h, of_z
 

time: 56.1 us -> 55.3 us (0.986)
  waiting for transfers between devices: 6.76 us -> 6.17 us
    ppermute x4, starting transfers between devices: 15.6 us -> 14.9 us  [exchange_h(): return lax.ppermute(x, BOTH, route(step))]
where the time goes in v7:
time: 55.3 us; the launch traced here: 54.7 us
  starting transfers between devices  36 us (65%)
  Pallas kernels  7.81 us (14%)
  waiting for transfers between devices  6.17 us (11%)
  blocking collectives  4.48 us (8%)
    ppermute x5, starting transfers between devices, exchange_z(): lax.ppermute(x, BOTH, route(lambda z, y, xl, r: (pair_of(1 - kind, z, r),...  21.1 us
    ppermute x4, starting transfers between devices, exchange_h(): return lax.ppermute(x, BOTH, route(step))  14.9 us
    all_gather x1, blocking collectives, per_device(): lax.all_gather(other, 'col', axis_index_groups=[[2 * c, 2 * c + 1] for c...  4.48 us
    ppermute x5, waiting for transfers between devices, exchange_z(): lax.ppermute(x, BOTH, route(lambda z, y, xl, r: (pair_of(1 - kind, z, r),...  3.63 us
    pallas_call x1, Pallas kernels, early_product(): pl.pallas_call(early_kernel, out_shape=(ACC, jax.ShapeDtypeStruct((FIRST...  3.01 us
    ppermute x4, waiting for transfers between devices, exchange_h(): return lax.ppermute(x, BOTH, route(step))  2.53 us
    pallas_call x1, Pallas kernels, middle_product(): pl.pallas_call(middle_kernel, out_shape=(ACC, LAST_H), in_specs=[VMEM] *...  1.93 us
  transfers between devices with their start and end apart: 9, of which 4 were waited for; matrix products, arithmetic and copies ran while one was open for 0% of the time, Pallas kernels for 9%

profile of v7, /device:TPU:1, one launch (start us, length us, event | category | flops | bytes accessed | tf_op | source)
XLA Modules:
  0.0 54.7 jit_solution(4516700637383626513)
XLA Ops:
  0.0 1.1 %pack.1 = (bf16[1040,128]{1,0:T(8,128)(2,1)S(1)}, bf16[1040,128]{1,0:T(8,128)(2,1)S(1)}) custom-call(s32[2,8]{1,0:T(2,128)} %bitcast.9, s32[2,8]{1,0:T(2,128)} %bitcast.10, bf16[1024,128]{1,0:T(8,128)(2,1)} %bitcast.7, bf16[1024,128]{1,0:T(8,128)(2,1)} %bitcast.8), custom_call_target="tpu_custom_call" | custom-call | bytes 1064960 | tf_op jit(solution)/shard_map/pack/pallas_call | solution.py:87
  1.1 4.8 %collective-permute-start.4 = (bf16[1040,128]{1,0:T(8,128)(2,1)S(1)}, bf16[1040,128]{1,0:T(8,128)(2,1)S(1)}, u32[]{:S(2)}, u32[]{:S(2)}) collective-permute-start(bf16[1040,128]{1,0:T(8,128)(2,1)S(1)} %get-tuple-element.15.zp), channel_id=1, source_target_pairs={{0,224},{1,33},{2,227},{3,35},{4,229},{5,37},{6,231},{7,39},{8,233... | collective-permute-start | bytes 798728 | tf_op jit(solution)/shard_map/ppermute | solution.py:48
  5.9 3.1 %collective-permute-start = (bf16[1040,128]{1,0:T(8,128)(2,1)S(1)}, bf16[1040,128]{1,0:T(8,128)(2,1)S(1)}, u32[]{:S(2)}, u32[]{:S(2)}) collective-permute-start(bf16[1040,128]{1,0:T(8,128)(2,1)S(1)} %get-tuple-element.14.a.hp), channel_id=1, source_target_pairs={{0,2},{1,3},{2,0},{3,1},{4,6},{5,7},{6,4},{7,5},{8,10},{9,11},{10,... | collective-permute-start | bytes 798728 | tf_op jit(solution)/shard_map/ppermute | solution.py:59
  9.0 9.1 %collective-permute-start.5 = (bf16[1040,128]{1,0:T(8,128)(2,1)S(1)}, bf16[1040,128]{1,0:T(8,128)(2,1)S(1)}, u32[]{:S(2)}, u32[]{:S(2)}) collective-permute-start(bf16[1040,128]{1,0:T(8,128)(2,1)S(1)} %get-tuple-element.15.zp), channel_id=1, source_target_pairs={{0,32},{1,225},{2,34},{3,226},{4,36},{5,228},{6,38},{7,230},{8,40}... | collective-permute-start | bytes 798728 | tf_op jit(solution)/shard_map/ppermute | solution.py:48
  18.2 0.0 collective-permute-done.4.z1
  18.2 1.9 %collective-permute-start.6 = (bf16[1040,128]{1,0:T(8,128)(2,1)S(1)}, bf16[1040,128]{1,0:T(8,128)(2,1)S(1)}, u32[]{:S(2)}, u32[]{:S(2)}) collective-permute-start(bf16[1040,128]{1,0:T(8,128)(2,1)S(1)} %collective-permute-done.4.z1), channel_id=1, source_target_pairs={{0,32},{1,225},{2,34},{3,226},{4,36},{5,228},{6,38},{7,230},{8,40}... | collective-permute-start | bytes 798728 | tf_op jit(solution)/shard_map/ppermute | solution.py:48
  20.1 0.0 collective-permute-done.b.h1
  20.2 5.3 %collective-permute-start.2 = (bf16[2080,128]{1,0:T(8,128)(2,1)S(1)}, bf16[2080,128]{1,0:T(8,128)(2,1)S(1)}, u32[]{:S(2)}, u32[]{:S(2)}) collective-permute-start(bf16[2080,128]{1,0:T(8,128)(2,1)S(1)} %join.2), channel_id=1, source_target_pairs={{0,4},{1,28},{2,6},{3,30},{4,0},{5,9},{6,2},{7,11},{8,12},{9,5},{1... | collective-permute-start | bytes 1597448 | tf_op jit(solution)/shard_map/ppermute | solution.py:59
  25.5 0.0 collective-permute-done.5.a
  25.5 1.1 %collective-permute-done.6.b = bf16[1040,128]{1,0:T(8,128)(2,1)S(1)} collective-permute-done((bf16[1040,128]{1,0:T(8,128)(2,1)S(1)}, bf16[1040,128]{1,0:T(8,128)(2,1)S(1)}, u32[]{:S(2)}, u32[]{:S(2)}) %collective-permute-start.6) | collective-permute-done | bytes 266272 | tf_op jit(solution)/shard_map/ppermute | solution.py:48
  26.6 1.9 %collective-permute-start.7 = (bf16[2080,128]{1,0:T(8,128)(2,1)S(1)}, bf16[2080,128]{1,0:T(8,128)(2,1)S(1)}, u32[]{:S(2)}, u32[]{:S(2)}) collective-permute-start(bf16[2080,128]{1,0:T(8,128)(2,1)S(1)} %join.3.z2), channel_id=1, source_target_pairs={{0,224},{1,33},{2,227},{3,35},{4,229},{5,37},{6,231},{7,39},{8,233... | collective-permute-start | bytes 1597448 | tf_op jit(solution)/shard_map/ppermute | solution.py:48
  28.5 4.6 %collective-permute-start.1 = (bf16[2080,128]{1,0:T(8,128)(2,1)S(1)}, bf16[2080,128]{1,0:T(8,128)(2,1)S(1)}, u32[]{:S(2)}, u32[]{:S(2)}) collective-permute-start(bf16[2080,128]{1,0:T(8,128)(2,1)S(1)} %join.2), channel_id=1, source_target_pairs={{0,29},{1,5},{2,31},{3,7},{4,8},{5,1},{6,10},{7,3},{8,4},{9,13},{1... | collective-permute-start | bytes 1597448 | tf_op jit(solution)/shard_map/ppermute | solution.py:59
  33.2 0.0 collective-permute-done.2.h2
  33.2 1.9 %collective-permute-start.3 = (bf16[2080,128]{1,0:T(8,128)(2,1)S(1)}, bf16[2080,128]{1,0:T(8,128)(2,1)S(1)}, u32[]{:S(2)}, u32[]{:S(2)}) collective-permute-start(bf16[2080,128]{1,0:T(8,128)(2,1)S(1)} %collective-permute-done.2.h2), channel_id=1, source_target_pairs={{0,29},{1,5},{2,31},{3,7},{4,8},{5,1},{6,10},{7,3},{8,4},{9,13},{1... | collective-permute-start | bytes 1597448 | tf_op jit(solution)/shard_map/ppermute | solution.py:59
  35.1 1.8 %collective-permute-done.7.z3 = bf16[2080,128]{1,0:T(8,128)(2,1)S(1)} collective-permute-done((bf16[2080,128]{1,0:T(8,128)(2,1)S(1)}, bf16[2080,128]{1,0:T(8,128)(2,1)S(1)}, u32[]{:S(2)}, u32[]{:S(2)}) %collective-permute-start.7) | collective-permute-done | bytes 532512 | tf_op jit(solution)/shard_map/ppermute | solution.py:48
  36.9 3.3 %collective-permute-start.8 = (bf16[2080,128]{1,0:T(8,128)(2,1)S(1)}, bf16[2080,128]{1,0:T(8,128)(2,1)S(1)}, u32[]{:S(2)}, u32[]{:S(2)}) collective-permute-start(bf16[2080,128]{1,0:T(8,128)(2,1)S(1)} %collective-permute-done.7.z3), channel_id=1, source_target_pairs={{0,32},{1,225},{2,34},{3,226},{4,36},{5,228},{6,38},{7,230},{8,40}... | collective-permute-start | bytes 1597448 | tf_op jit(solution)/shard_map/ppermute | solution.py:48
  40.2 3.0 %early.1 = (f32[512,512]{1,0:T(8,128)S(1)}, bf16[2048,512]{1,0:T(8,128)(2,1)S(1)}, bf16[512,1024]{1,0:T(8,128)(2,1)S(1)}) custom-call(bf16[1040,128]{1,0:T(8,128)(2,1)S(1)} %get-tuple-element.14.a.hp, bf16[1040,128]{1,0:T(8,128)(2,1)S(1)} %collective-permute-done.b.h1, bf16[2080,128]{1,0:T(8,128)(2,1)S(1)} %collective-permute-done.2.h2, ...), custom_call_target="tpu_custom_call" | custom-call | flops 1073741824 | bytes 4194304 | tf_op jit(solution)/shard_map/early/pallas_call | solution.py:295
  43.3 0.0 collective-permute-done.1.h3
  43.3 2.5 %collective-permute-done.3.h4 = bf16[2080,128]{1,0:T(8,128)(2,1)S(1)} collective-permute-done((bf16[2080,128]{1,0:T(8,128)(2,1)S(1)}, bf16[2080,128]{1,0:T(8,128)(2,1)S(1)}, u32[]{:S(2)}, u32[]{:S(2)}) %collective-permute-start.3) | collective-permute-done | bytes 532512 | tf_op jit(solution)/shard_map/ppermute | solution.py:59
  45.8 1.9 %middle.1 = (f32[512,512]{1,0:T(8,128)S(1)}, bf16[512,1024]{1,0:T(8,128)(2,1)S(1)}) custom-call(bf16[2080,128]{1,0:T(8,128)(2,1)S(1)} %collective-permute-done.1.h3, bf16[2080,128]{1,0:T(8,128)(2,1)S(1)} %collective-permute-done.3.h4, bf16[2048,512]{1,0:T(8,128)(2,1)S(1)} %get-tuple-element.16.mid_z, ...), custom_call_target="tpu_custom_call", output_to_operand_aliasing={{0}: (3, {}), {1}: (4, {})} | custom-call | flops 2147483648 | bytes 1048576 | tf_op jit(solution)/shard_map/middle/pallas_call | solution.py:308
  47.7 0.7 %collective-permute-done.8.z4 = bf16[2080,128]{1,0:T(8,128)(2,1)S(1)} collective-permute-done((bf16[2080,128]{1,0:T(8,128)(2,1)S(1)}, bf16[2080,128]{1,0:T(8,128)(2,1)S(1)}, u32[]{:S(2)}, u32[]{:S(2)}) %collective-permute-start.8) | collective-permute-done | bytes 532512 | tf_op jit(solution)/shard_map/ppermute | solution.py:48
  48.4 1.0 %late.1 = (f32[4,128,128]{2,1,0:T(8,128)S(1)}, f32[4,128,128]{2,1,0:T(8,128)S(1)}) custom-call(s32[2,8]{1,0:T(2,128)S(1)} %bitcast.6, f32[512,512]{1,0:T(8,128)S(1)} %get-tuple-element.19.acc, bf16[512,1024]{1,0:T(8,128)(2,1)S(1)} %get-tuple-element.20.last_h, bf16[2080,128]{1,0:T(8,128)(2,1)S(1)} %collective-permute-done.8.z4), custom_call_target="tpu_custom_call" | custom-call | flops 536870912 | bytes 2097152 | tf_op jit(solution)/shard_map/late/pallas_call | solution.py:322
  49.4 4.5 %all_gather.3.both = f32[8,128,128]{2,1,0:T(8,128)S(1)} all-gather(f32[4,128,128]{2,1,0:T(8,128)S(1)} %get-tuple-element.22), channel_id=1, replica_groups={{0,1},{2,3},{4,5},{6,7},{8,9},{10,11},{12,13},{14,15},{16,17},{18,19},{..., dimensions={0}, use_global_device_ids=true | all-gather | bytes 786432 | tf_op jit(solution)/shard_map/all_gather | solution.py:368
  53.9 0.7 %finish.1 = f32[4,128,128]{2,1,0:T(8,128)} custom-call(f32[4,128,128]{2,1,0:T(8,128)S(1)} %get-tuple-element.21.own, f32[8,128,128]{2,1,0:T(8,128)S(1)} %all_gather.3.both), custom_call_target="tpu_custom_call" | custom-call | bytes 1048576 | tf_op jit(solution)/shard_map/finish/pallas_call | solution.py:340
  (4 shorter events, 0.1 us)
Async XLA Ops:
  1.1 17.1 %collective-permute-start.4 = (bf16[1040,128]{1,0:T(8,128)(2,1)S(1)}, bf16[1040,128]{1,0:T(8,128)(2,1)S(1)}, u32[]{:S(2)}, u32[]{:S(2)}) collective-permute-start(bf16[1040,128]{1,0:T(8,128)(2,1)S(1)} %get-tuple-element.15.zp), channel_id=1, source_target_pairs={{0,224},{1,33},{2,227},{3,35},{4,229},{5,37},{6,231},{7,39},{8,233... | collective-permute-start | bytes 798728 | tf_op jit(solution)/shard_map/ppermute | solution.py:48
  5.9 14.2 %collective-permute-start = (bf16[1040,128]{1,0:T(8,128)(2,1)S(1)}, bf16[1040,128]{1,0:T(8,128)(2,1)S(1)}, u32[]{:S(2)}, u32[]{:S(2)}) collective-permute-start(bf16[1040,128]{1,0:T(8,128)(2,1)S(1)} %get-tuple-element.14.a.hp), channel_id=1, source_target_pairs={{0,2},{1,3},{2,0},{3,1},{4,6},{5,7},{6,4},{7,5},{8,10},{9,11},{10,... | collective-permute-start | bytes 798728 | tf_op jit(solution)/shard_map/ppermute | solution.py:59
  9.0 16.4 %collective-permute-start.5 = (bf16[1040,128]{1,0:T(8,128)(2,1)S(1)}, bf16[1040,128]{1,0:T(8,128)(2,1)S(1)}, u32[]{:S(2)}, u32[]{:S(2)}) collective-permute-start(bf16[1040,128]{1,0:T(8,128)(2,1)S(1)} %get-tuple-element.15.zp), channel_id=1, source_target_pairs={{0,32},{1,225},{2,34},{3,226},{4,36},{5,228},{6,38},{7,230},{8,40}... | collective-permute-start | bytes 798728 | tf_op jit(solution)/shard_map/ppermute | solution.py:48
  18.2 8.4 %collective-permute-start.6 = (bf16[1040,128]{1,0:T(8,128)(2,1)S(1)}, bf16[1040,128]{1,0:T(8,128)(2,1)S(1)}, u32[]{:S(2)}, u32[]{:S(2)}) collective-permute-start(bf16[1040,128]{1,0:T(8,128)(2,1)S(1)} %collective-permute-done.4.z1), channel_id=1, source_target_pairs={{0,32},{1,225},{2,34},{3,226},{4,36},{5,228},{6,38},{7,230},{8,40}... | collective-permute-start | bytes 798728 | tf_op jit(solution)/shard_map/ppermute | solution.py:48
  20.2 13.0 %collective-permute-start.2 = (bf16[2080,128]{1,0:T(8,128)(2,1)S(1)}, bf16[2080,128]{1,0:T(8,128)(2,1)S(1)}, u32[]{:S(2)}, u32[]{:S(2)}) collective-permute-start(bf16[2080,128]{1,0:T(8,128)(2,1)S(1)} %join.2), channel_id=1, source_target_pairs={{0,4},{1,28},{2,6},{3,30},{4,0},{5,9},{6,2},{7,11},{8,12},{9,5},{1... | collective-permute-start | bytes 1597448 | tf_op jit(solution)/shard_map/ppermute | solution.py:59
  26.6 10.3 %collective-permute-start.7 = (bf16[2080,128]{1,0:T(8,128)(2,1)S(1)}, bf16[2080,128]{1,0:T(8,128)(2,1)S(1)}, u32[]{:S(2)}, u32[]{:S(2)}) collective-permute-start(bf16[2080,128]{1,0:T(8,128)(2,1)S(1)} %join.3.z2), channel_id=1, source_target_pairs={{0,224},{1,33},{2,227},{3,35},{4,229},{5,37},{6,231},{7,39},{8,233... | collective-permute-start | bytes 1597448 | tf_op jit(solution)/shard_map/ppermute | solution.py:48
  28.5 14.7 %collective-permute-start.1 = (bf16[2080,128]{1,0:T(8,128)(2,1)S(1)}, bf16[2080,128]{1,0:T(8,128)(2,1)S(1)}, u32[]{:S(2)}, u32[]{:S(2)}) collective-permute-start(bf16[2080,128]{1,0:T(8,128)(2,1)S(1)} %join.2), channel_id=1, source_target_pairs={{0,29},{1,5},{2,31},{3,7},{4,8},{5,1},{6,10},{7,3},{8,4},{9,13},{1... | collective-permute-start | bytes 1597448 | tf_op jit(solution)/shard_map/ppermute | solution.py:59
  33.2 12.6 %collective-permute-start.3 = (bf16[2080,128]{1,0:T(8,128)(2,1)S(1)}, bf16[2080,128]{1,0:T(8,128)(2,1)S(1)}, u32[]{:S(2)}, u32[]{:S(2)}) collective-permute-start(bf16[2080,128]{1,0:T(8,128)(2,1)S(1)} %collective-permute-done.2.h2), channel_id=1, source_target_pairs={{0,29},{1,5},{2,31},{3,7},{4,8},{5,1},{6,10},{7,3},{8,4},{9,13},{1... | collective-permute-start | bytes 1597448 | tf_op jit(solution)/shard_map/ppermute | solution.py:59
  36.9 11.5 %collective-permute-start.8 = (bf16[2080,128]{1,0:T(8,128)(2,1)S(1)}, bf16[2080,128]{1,0:T(8,128)(2,1)S(1)}, u32[]{:S(2)}, u32[]{:S(2)}) collective-permute-start(bf16[2080,128]{1,0:T(8,128)(2,1)S(1)} %collective-permute-done.7.z3), channel_id=1, source_target_pairs={{0,32},{1,225},{2,34},{3,226},{4,36},{5,228},{6,38},{7,230},{8,40}... | collective-permute-start | bytes 1597448 | tf_op jit(solution)/shard_map/ppermute | solution.py:48
  45.8 2.6 %copy-start = (s32[1,1,2,8]{3,2,1,0:T(2,128)S(1)}, s32[1,1,2,8]{3,2,1,0:T(2,128)}, u32[]{:S(2)}) copy-start(s32[1,1,2,8]{3,2,1,0:T(2,128)} %param.9) | copy-start | bytes 196

commit v8 on v7

--- a/solution.py
+++ b/solution.py
@@ -51,10 +51,10 @@
 def exchange_h(x, hop):
     def step(z, y, xl, r):
         if hop == 2:
-            return z, pair_of(1, y, r), xl
+            return z, pair_of(0, y, r), xl
         if hop == 0:
             return z, y, xl ^ 1
-        return z, pair_of(0, y, r), xl
+        return z, pair_of(1, y, r), xl
 
     return lax.ppermute(x, BOTH, route(step))
 
@@ -132,9 +132,9 @@
 
 def offsets():
     z, y, xl, _, role = position()
-    ya = near(y, 0, role)
-    yb = near(y, 1, role)
-    yab = near(yb, 0, role)
+    ya = near(y, 1, role)
+    yb = near(y, 0, role)
+    yab = near(yb, 1, role)
     xo = xl ^ 1
     first = ((y, xl), (y, xo), (ya, xl), (ya, xo), (yb, xl), (yb, xo), (yab, xl), (yab, xo))
     def ahead(yy, xx):

time: 55.3 us -> 55.3 us (level)
  starting transfers between devices: 36 us -> 36.7 us
    ppermute x5, waiting for transfers between devices: 3.63 us -> 2.18 us  [exchange_z(): lax.ppermute(x, BOTH, route(lambda z, y, xl, r: (pair_of(1 - kind, z, r),...]
    ppermute x4, waiting for transfers between devices: 2.53 us -> 3.68 us  [exchange_h(): return lax.ppermute(x, BOTH, route(step))]
    ppermute x4, starting transfers between devices: 14.9 us -> 15.7 us  [exchange_h(): return lax.ppermute(x, BOTH, route(step))]
  transfers between devices with their start and end apart: 9 -> 9, of which waited for: 4 -> 3; matrix products, arithmetic and copies ran while one was open for 0% -> 0% of each run, Pallas kernels for 9% -> 9%
where the time goes in v8:
time: 55.3 us; the launch traced here: 54.7 us
  starting transfers between devices  36.7 us (66%)
  Pallas kernels  7.79 us (14%)
  waiting for transfers between devices  5.85 us (11%)
  blocking collectives  4.12 us (7%)
    ppermute x5, starting transfers between devices, exchange_z(): lax.ppermute(x, BOTH, route(lambda z, y, xl, r: (pair_of(1 - kind, z, r),...  21 us
    ppermute x4, starting transfers between devices, exchange_h(): return lax.ppermute(x, BOTH, route(step))  15.7 us
    all_gather x1, blocking collectives, per_device(): lax.all_gather(other, 'col', axis_index_groups=[[2 * c, 2 * c + 1] for c...  4.12 us
    ppermute x4, waiting for transfers between devices, exchange_h(): return lax.ppermute(x, BOTH, route(step))  3.68 us
    pallas_call x1, Pallas kernels, early_product(): pl.pallas_call(early_kernel, out_shape=(ACC, jax.ShapeDtypeStruct((FIRST...  3 us
    ppermute x5, waiting for transfers between devices, exchange_z(): lax.ppermute(x, BOTH, route(lambda z, y, xl, r: (pair_of(1 - kind, z, r),...  2.18 us
    pallas_call x1, Pallas kernels, middle_product(): pl.pallas_call(middle_kernel, out_shape=(ACC, LAST_H), in_specs=[VMEM] *...  1.92 us
  transfers between devices with their start and end apart: 9, of which 3 were waited for; matrix products, arithmetic and copies ran while one was open for 0% of the time, Pallas kernels for 9%

profile of v8, /device:TPU:1, one launch (start us, length us, event | category | flops | bytes accessed | tf_op | source)
XLA Modules:
  0.0 54.7 jit_solution(6435148186228612649)
XLA Ops:
  0.0 1.1 %pack.1 = (bf16[1040,128]{1,0:T(8,128)(2,1)S(1)}, bf16[1040,128]{1,0:T(8,128)(2,1)S(1)}) custom-call(s32[2,8]{1,0:T(2,128)} %bitcast.9, s32[2,8]{1,0:T(2,128)} %bitcast.10, bf16[1024,128]{1,0:T(8,128)(2,1)} %bitcast.7, bf16[1024,128]{1,0:T(8,128)(2,1)} %bitcast.8), custom_call_target="tpu_custom_call" | custom-call | bytes 1064960 | tf_op jit(solution)/shard_map/pack/pallas_call | solution.py:87
  1.1 4.8 %collective-permute-start.4 = (bf16[1040,128]{1,0:T(8,128)(2,1)S(1)}, bf16[1040,128]{1,0:T(8,128)(2,1)S(1)}, u32[]{:S(2)}, u32[]{:S(2)}) collective-permute-start(bf16[1040,128]{1,0:T(8,128)(2,1)S(1)} %get-tuple-element.15.zp), channel_id=1, source_target_pairs={{0,224},{1,33},{2,227},{3,35},{4,229},{5,37},{6,231},{7,39},{8,233... | collective-permute-start | bytes 798728 | tf_op jit(solution)/shard_map/ppermute | solution.py:48
  5.9 3.1 %collective-permute-start = (bf16[1040,128]{1,0:T(8,128)(2,1)S(1)}, bf16[1040,128]{1,0:T(8,128)(2,1)S(1)}, u32[]{:S(2)}, u32[]{:S(2)}) collective-permute-start(bf16[1040,128]{1,0:T(8,128)(2,1)S(1)} %get-tuple-element.14.a.hp), channel_id=1, source_target_pairs={{0,2},{1,3},{2,0},{3,1},{4,6},{5,7},{6,4},{7,5},{8,10},{9,11},{10,... | collective-permute-start | bytes 798728 | tf_op jit(solution)/shard_map/ppermute | solution.py:59
  9.0 9.1 %collective-permute-start.5 = (bf16[1040,128]{1,0:T(8,128)(2,1)S(1)}, bf16[1040,128]{1,0:T(8,128)(2,1)S(1)}, u32[]{:S(2)}, u32[]{:S(2)}) collective-permute-start(bf16[1040,128]{1,0:T(8,128)(2,1)S(1)} %get-tuple-element.15.zp), channel_id=1, source_target_pairs={{0,32},{1,225},{2,34},{3,226},{4,36},{5,228},{6,38},{7,230},{8,40}... | collective-permute-start | bytes 798728 | tf_op jit(solution)/shard_map/ppermute | solution.py:48
  18.2 0.0 collective-permute-done.4.z1
  18.2 1.9 %collective-permute-start.6 = (bf16[1040,128]{1,0:T(8,128)(2,1)S(1)}, bf16[1040,128]{1,0:T(8,128)(2,1)S(1)}, u32[]{:S(2)}, u32[]{:S(2)}) collective-permute-start(bf16[1040,128]{1,0:T(8,128)(2,1)S(1)} %collective-permute-done.4.z1), channel_id=1, source_target_pairs={{0,32},{1,225},{2,34},{3,226},{4,36},{5,228},{6,38},{7,230},{8,40}... | collective-permute-start | bytes 798728 | tf_op jit(solution)/shard_map/ppermute | solution.py:48
  20.1 0.0 collective-permute-done.b.h1
  20.2 4.5 %collective-permute-start.2 = (bf16[2080,128]{1,0:T(8,128)(2,1)S(1)}, bf16[2080,128]{1,0:T(8,128)(2,1)S(1)}, u32[]{:S(2)}, u32[]{:S(2)}) collective-permute-start(bf16[2080,128]{1,0:T(8,128)(2,1)S(1)} %join.2), channel_id=1, source_target_pairs={{0,29},{1,5},{2,31},{3,7},{4,8},{5,1},{6,10},{7,3},{8,4},{9,13},{1... | collective-permute-start | bytes 1597448 | tf_op jit(solution)/shard_map/ppermute | solution.py:59
  24.7 0.0 collective-permute-done.5.a
  24.7 1.9 %collective-permute-done.6.b = bf16[1040,128]{1,0:T(8,128)(2,1)S(1)} collective-permute-done((bf16[1040,128]{1,0:T(8,128)(2,1)S(1)}, bf16[1040,128]{1,0:T(8,128)(2,1)S(1)}, u32[]{:S(2)}, u32[]{:S(2)}) %collective-permute-start.6) | collective-permute-done | bytes 266272 | tf_op jit(solution)/shard_map/ppermute | solution.py:48
  26.6 1.9 %collective-permute-start.7 = (bf16[2080,128]{1,0:T(8,128)(2,1)S(1)}, bf16[2080,128]{1,0:T(8,128)(2,1)S(1)}, u32[]{:S(2)}, u32[]{:S(2)}) collective-permute-start(bf16[2080,128]{1,0:T(8,128)(2,1)S(1)} %join.3.z2), channel_id=1, source_target_pairs={{0,224},{1,33},{2,227},{3,35},{4,229},{5,37},{6,231},{7,39},{8,233... | collective-permute-start | bytes 1597448 | tf_op jit(solution)/shard_map/ppermute | solution.py:48
  28.5 5.7 %collective-permute-start.1 = (bf16[2080,128]{1,0:T(8,128)(2,1)S(1)}, bf16[2080,128]{1,0:T(8,128)(2,1)S(1)}, u32[]{:S(2)}, u32[]{:S(2)}) collective-permute-start(bf16[2080,128]{1,0:T(8,128)(2,1)S(1)} %join.2), channel_id=1, source_target_pairs={{0,4},{1,28},{2,6},{3,30},{4,0},{5,9},{6,2},{7,11},{8,12},{9,5},{1... | collective-permute-start | bytes 1597448 | tf_op jit(solution)/shard_map/ppermute | solution.py:59
  34.2 0.0 collective-permute-done.2.h2
  34.2 2.4 %collective-permute-start.3 = (bf16[2080,128]{1,0:T(8,128)(2,1)S(1)}, bf16[2080,128]{1,0:T(8,128)(2,1)S(1)}, u32[]{:S(2)}, u32[]{:S(2)}) collective-permute-start(bf16[2080,128]{1,0:T(8,128)(2,1)S(1)} %collective-permute-done.2.h2), channel_id=1, source_target_pairs={{0,4},{1,28},{2,6},{3,30},{4,0},{5,9},{6,2},{7,11},{8,12},{9,5},{1... | collective-permute-start | bytes 1597448 | tf_op jit(solution)/shard_map/ppermute | solution.py:59
  36.6 0.3 collective-permute-done.7.z3
  36.9 3.2 %collective-permute-start.8 = (bf16[2080,128]{1,0:T(8,128)(2,1)S(1)}, bf16[2080,128]{1,0:T(8,128)(2,1)S(1)}, u32[]{:S(2)}, u32[]{:S(2)}) collective-permute-start(bf16[2080,128]{1,0:T(8,128)(2,1)S(1)} %collective-permute-done.7.z3), channel_id=1, source_target_pairs={{0,32},{1,225},{2,34},{3,226},{4,36},{5,228},{6,38},{7,230},{8,40}... | collective-permute-start | bytes 1597448 | tf_op jit(solution)/shard_map/ppermute | solution.py:48
  40.2 3.0 %early.1 = (f32[512,512]{1,0:T(8,128)S(1)}, bf16[2048,512]{1,0:T(8,128)(2,1)S(1)}, bf16[512,1024]{1,0:T(8,128)(2,1)S(1)}) custom-call(bf16[1040,128]{1,0:T(8,128)(2,1)S(1)} %get-tuple-element.14.a.hp, bf16[1040,128]{1,0:T(8,128)(2,1)S(1)} %collective-permute-done.b.h1, bf16[2080,128]{1,0:T(8,128)(2,1)S(1)} %collective-permute-done.2.h2, ...), custom_call_target="tpu_custom_call" | custom-call | flops 1073741824 | bytes 4194304 | tf_op jit(solution)/shard_map/early/pallas_call | solution.py:295
  43.2 0.0 collective-permute-done.1.h3
  43.2 3.7 %collective-permute-done.3.h4 = bf16[2080,128]{1,0:T(8,128)(2,1)S(1)} collective-permute-done((bf16[2080,128]{1,0:T(8,128)(2,1)S(1)}, bf16[2080,128]{1,0:T(8,128)(2,1)S(1)}, u32[]{:S(2)}, u32[]{:S(2)}) %collective-permute-start.3) | collective-permute-done | bytes 532512 | tf_op jit(solution)/shard_map/ppermute | solution.py:59
  46.8 1.9 %middle.1 = (f32[512,512]{1,0:T(8,128)S(1)}, bf16[512,1024]{1,0:T(8,128)(2,1)S(1)}) custom-call(bf16[2080,128]{1,0:T(8,128)(2,1)S(1)} %collective-permute-done.1.h3, bf16[2080,128]{1,0:T(8,128)(2,1)S(1)} %collective-permute-done.3.h4, bf16[2048,512]{1,0:T(8,128)(2,1)S(1)} %get-tuple-element.16.mid_z, ...), custom_call_target="tpu_custom_call", output_to_operand_aliasing={{0}: (3, {}), {1}: (4, {})} | custom-call | flops 2147483648 | bytes 1048576 | tf_op jit(solution)/shard_map/middle/pallas_call | solution.py:308
  48.8 0.0 collective-permute-done.8.z4
  48.8 1.0 %late.1 = (f32[4,128,128]{2,1,0:T(8,128)S(1)}, f32[4,128,128]{2,1,0:T(8,128)S(1)}) custom-call(s32[2,8]{1,0:T(2,128)S(1)} %bitcast.6, f32[512,512]{1,0:T(8,128)S(1)} %get-tuple-element.19.acc, bf16[512,1024]{1,0:T(8,128)(2,1)S(1)} %get-tuple-element.20.last_h, bf16[2080,128]{1,0:T(8,128)(2,1)S(1)} %collective-permute-done.8.z4), custom_call_target="tpu_custom_call" | custom-call | flops 536870912 | bytes 2097152 | tf_op jit(solution)/shard_map/late/pallas_call | solution.py:322
  49.8 4.1 %all_gather.3.both = f32[8,128,128]{2,1,0:T(8,128)S(1)} all-gather(f32[4,128,128]{2,1,0:T(8,128)S(1)} %get-tuple-element.22), channel_id=1, replica_groups={{0,1},{2,3},{4,5},{6,7},{8,9},{10,11},{12,13},{14,15},{16,17},{18,19},{..., dimensions={0}, use_global_device_ids=true | all-gather | bytes 786432 | tf_op jit(solution)/shard_map/all_gather | solution.py:368
  53.9 0.7 %finish.1 = f32[4,128,128]{2,1,0:T(8,128)} custom-call(f32[4,128,128]{2,1,0:T(8,128)S(1)} %get-tuple-element.21.own, f32[8,128,128]{2,1,0:T(8,128)S(1)} %all_gather.3.both), custom_call_target="tpu_custom_call" | custom-call | bytes 1048576 | tf_op jit(solution)/shard_map/finish/pallas_call | solution.py:340
  (4 shorter events, 0.1 us)
Async XLA Ops:
  1.1 17.1 %collective-permute-start.4 = (bf16[1040,128]{1,0:T(8,128)(2,1)S(1)}, bf16[1040,128]{1,0:T(8,128)(2,1)S(1)}, u32[]{:S(2)}, u32[]{:S(2)}) collective-permute-start(bf16[1040,128]{1,0:T(8,128)(2,1)S(1)} %get-tuple-element.15.zp), channel_id=1, source_target_pairs={{0,224},{1,33},{2,227},{3,35},{4,229},{5,37},{6,231},{7,39},{8,233... | collective-permute-start | bytes 798728 | tf_op jit(solution)/shard_map/ppermute | solution.py:48
  5.9 14.2 %collective-permute-start = (bf16[1040,128]{1,0:T(8,128)(2,1)S(1)}, bf16[1040,128]{1,0:T(8,128)(2,1)S(1)}, u32[]{:S(2)}, u32[]{:S(2)}) collective-permute-start(bf16[1040,128]{1,0:T(8,128)(2,1)S(1)} %get-tuple-element.14.a.hp), channel_id=1, source_target_pairs={{0,2},{1,3},{2,0},{3,1},{4,6},{5,7},{6,4},{7,5},{8,10},{9,11},{10,... | collective-permute-start | bytes 798728 | tf_op jit(solution)/shard_map/ppermute | solution.py:59
  9.0 15.7 %collective-permute-start.5 = (bf16[1040,128]{1,0:T(8,128)(2,1)S(1)}, bf16[1040,128]{1,0:T(8,128)(2,1)S(1)}, u32[]{:S(2)}, u32[]{:S(2)}) collective-permute-start(bf16[1040,128]{1,0:T(8,128)(2,1)S(1)} %get-tuple-element.15.zp), channel_id=1, source_target_pairs={{0,32},{1,225},{2,34},{3,226},{4,36},{5,228},{6,38},{7,230},{8,40}... | collective-permute-start | bytes 798728 | tf_op jit(solution)/shard_map/ppermute | solution.py:48
  18.2 8.4 %collective-permute-start.6 = (bf16[1040,128]{1,0:T(8,128)(2,1)S(1)}, bf16[1040,128]{1,0:T(8,128)(2,1)S(1)}, u32[]{:S(2)}, u32[]{:S(2)}) collective-permute-start(bf16[1040,128]{1,0:T(8,128)(2,1)S(1)} %collective-permute-done.4.z1), channel_id=1, source_target_pairs={{0,32},{1,225},{2,34},{3,226},{4,36},{5,228},{6,38},{7,230},{8,40}... | collective-permute-start | bytes 798728 | tf_op jit(solution)/shard_map/ppermute | solution.py:48
  20.2 14.0 %collective-permute-start.2 = (bf16[2080,128]{1,0:T(8,128)(2,1)S(1)}, bf16[2080,128]{1,0:T(8,128)(2,1)S(1)}, u32[]{:S(2)}, u32[]{:S(2)}) collective-permute-start(bf16[2080,128]{1,0:T(8,128)(2,1)S(1)} %join.2), channel_id=1, source_target_pairs={{0,29},{1,5},{2,31},{3,7},{4,8},{5,1},{6,10},{7,3},{8,4},{9,13},{1... | collective-permute-start | bytes 1597448 | tf_op jit(solution)/shard_map/ppermute | solution.py:59
  26.6 10.3 %collective-permute-start.7 = (bf16[2080,128]{1,0:T(8,128)(2,1)S(1)}, bf16[2080,128]{1,0:T(8,128)(2,1)S(1)}, u32[]{:S(2)}, u32[]{:S(2)}) collective-permute-start(bf16[2080,128]{1,0:T(8,128)(2,1)S(1)} %join.3.z2), channel_id=1, source_target_pairs={{0,224},{1,33},{2,227},{3,35},{4,229},{5,37},{6,231},{7,39},{8,233... | collective-permute-start | bytes 1597448 | tf_op jit(solution)/shard_map/ppermute | solution.py:48
  28.5 14.6 %collective-permute-start.1 = (bf16[2080,128]{1,0:T(8,128)(2,1)S(1)}, bf16[2080,128]{1,0:T(8,128)(2,1)S(1)}, u32[]{:S(2)}, u32[]{:S(2)}) collective-permute-start(bf16[2080,128]{1,0:T(8,128)(2,1)S(1)} %join.2), channel_id=1, source_target_pairs={{0,4},{1,28},{2,6},{3,30},{4,0},{5,9},{6,2},{7,11},{8,12},{9,5},{1... | collective-permute-start | bytes 1597448 | tf_op jit(solution)/shard_map/ppermute | solution.py:59
  34.2 12.6 %collective-permute-start.3 = (bf16[2080,128]{1,0:T(8,128)(2,1)S(1)}, bf16[2080,128]{1,0:T(8,128)(2,1)S(1)}, u32[]{:S(2)}, u32[]{:S(2)}) collective-permute-start(bf16[2080,128]{1,0:T(8,128)(2,1)S(1)} %collective-permute-done.2.h2), channel_id=1, source_target_pairs={{0,4},{1,28},{2,6},{3,30},{4,0},{5,9},{6,2},{7,11},{8,12},{9,5},{1... | collective-permute-start | bytes 1597448 | tf_op jit(solution)/shard_map/ppermute | solution.py:59
  36.9 11.9 %collective-permute-start.8 = (bf16[2080,128]{1,0:T(8,128)(2,1)S(1)}, bf16[2080,128]{1,0:T(8,128)(2,1)S(1)}, u32[]{:S(2)}, u32[]{:S(2)}) collective-permute-start(bf16[2080,128]{1,0:T(8,128)(2,1)S(1)} %collective-permute-done.7.z3), channel_id=1, source_target_pairs={{0,32},{1,225},{2,34},{3,226},{4,36},{5,228},{6,38},{7,230},{8,40}... | collective-permute-start | bytes 1597448 | tf_op jit(solution)/shard_map/ppermute | solution.py:48
  46.8 1.9 %copy-start = (s32[1,1,2,8]{3,2,1,0:T(2,128)S(1)}, s32[1,1,2,8]{3,2,1,0:T(2,128)}, u32[]{:S(2)}) copy-start(s32[1,1,2,8]{3,2,1,0:T(2,128)} %param.9) | copy-start | bytes 196
